TPU v7x, 512 devices: a whole 4x4x16 slice. The times are simulated.
512 devices in a mesh: grp: 8 (over x, core), own: 64 (over z, y).
Axes of the slice: x: 4, y: 4, z: 16, core: 2. Of those that a mesh axis runs over, the one named last changes fastest.
Arguments:
- left: bfloat16 [32768, 128, 64], P(('grp', 'own')), may hold values from -0.75 to 0.75
- right: bfloat16 [32768, 128, 64], P(('grp', 'own')), may hold values from -0.75 to 0.75
- values: bfloat16 [32768, 128], P(('grp', 'own')), may hold values from -6 to 6
- core: bfloat16 [10240, 64, 64], P(('grp', 'own')), may hold values from -6 to 6
- tile_slice: int32 [32768], P(('grp', 'own')), may hold values from 0 to 10239, as said below
- tile_fill: int32 [32768], P(('grp', 'own')), may hold values from 64 to 128
Outputs:
- new_core: bfloat16 [10240, 64, 64], P(('grp', 'own'))
- new_left: bfloat16 [32768, 128, 64], P(('grp', 'own'))
Inputs may be any that keep to these rules, and one draw needn't show every extreme that they name: `tile_slice`: call j // 20 the block of slice j and its remainder mod 64 its class. Among the tiles of one device at most 2 have slices of one class; in every group of 64 consecutive devices some class gets exactly 2 tiles from every device of the group.
All inputs are finite; a program needn't handle non-finite values.
Results may differ from a plain program's by a relative error of at most 0.0052.
Values may be sent and summed in bfloat16 or wider, within the bound.
No kernel may reach another device: no remote copies, remote signals or barrier semaphores. Data moves between devices by JAX's collectives and lax.ppermute only.
A program may use at most 64 MiB of HBM per device.

v0:
```python
import jax
import jax.numpy as jnp
from jax import lax
from jax.sharding import PartitionSpec as P


def tile_terms(left_tiles, right_tiles, value_tiles, fill_counts, slice_tables):
    tile_rows = left_tiles.shape[1]
    projected = jnp.einsum(
        "sea,sab->seb", left_tiles, slice_tables, preferred_element_type=jnp.float32
    )
    predicted = jnp.sum(projected * right_tiles.astype(jnp.float32), axis=-1)
    live_rows = jnp.arange(tile_rows)[None, :] < fill_counts[:, None]
    residual = jnp.where(live_rows, predicted - value_tiles.astype(jnp.float32), 0.0)
    weighted = (residual[:, :, None] * left_tiles.astype(jnp.float32)).astype(jnp.bfloat16)
    return jnp.einsum("sea,seb->sab", weighted, right_tiles, preferred_element_type=jnp.float32)


def body(left, right, values, core, tile_slice, tile_fill):
    owners = lax.axis_size("own")
    groups = lax.axis_size("grp")
    tile_count, tile_rows, rank_width = left.shape
    per_device = core.shape[0]
    local_count = groups * per_device
    slot_cap = 2 * tile_count // owners
    slot_total = owners * slot_cap
    dev_block = tile_slice // per_device
    target_owner = dev_block % owners
    local_slice = dev_block // owners * per_device + tile_slice % per_device
    positions = jnp.arange(tile_count)
    same_owner = target_owner[:, None] == target_owner[None, :]
    earlier = positions[None, :] < positions[:, None]
    rank_among = jnp.sum((same_owner & earlier).astype(jnp.int32), axis=1)
    slot_of_tile = target_owner * slot_cap + rank_among
    slot_match = slot_of_tile[None, :] == jnp.arange(slot_total)[:, None]
    slot_live = jnp.any(slot_match, axis=1)
    tile_of_slot = jnp.sum(jnp.where(slot_match, positions[None, :], 0), axis=1)
    send_slice = jnp.where(slot_live, local_slice[tile_of_slot], 0)
    old_tables = lax.all_gather(core, "grp", axis=0, tiled=True)
    send_left = left[tile_of_slot]
    send_right = right[tile_of_slot]
    send_values = values[tile_of_slot]
    send_fill = jnp.where(slot_live, tile_fill[tile_of_slot], 0)
    got_left, got_right, got_values, got_slice, got_fill = (
        lax.all_to_all(send_left, "own", split_axis=0, concat_axis=0, tiled=True),
        lax.all_to_all(send_right, "own", split_axis=0, concat_axis=0, tiled=True),
        lax.all_to_all(send_values, "own", split_axis=0, concat_axis=0, tiled=True),
        lax.all_to_all(send_slice, "own", split_axis=0, concat_axis=0, tiled=True),
        lax.all_to_all(send_fill, "own", split_axis=0, concat_axis=0, tiled=True),
    )
    tile_grad = tile_terms(got_left, got_right, got_values, got_fill, old_tables[got_slice])
    selector = (got_slice[:, None] == jnp.arange(local_count)[None, :]).astype(jnp.float32)
    grad_part = jnp.dot(
        selector.T,
        tile_grad.reshape(slot_total, rank_width * rank_width),
        precision=lax.Precision.HIGHEST,
        preferred_element_type=jnp.float32,
    ).reshape(local_count, rank_width, rank_width)
    grad_whole = lax.psum(grad_part, "grp")
    new_tables = (old_tables.astype(jnp.float32) - grad_whole).astype(jnp.bfloat16)
    new_mine = lax.dynamic_slice_in_dim(
        new_tables, lax.axis_index("grp") * per_device, per_device, 0
    )
    refreshed = jnp.einsum(
        "sea,sab->seb", got_left, new_tables[got_slice], preferred_element_type=jnp.float32
    ).astype(jnp.bfloat16)
    returned = lax.all_to_all(refreshed, "own", split_axis=0, concat_axis=0, tiled=True)
    new_left = returned[slot_of_tile]
    return (new_mine, new_left)


def solution(mesh):
    return jax.shard_map(
        body,
        mesh=mesh,
        in_specs=(
            P(("grp", "own"), None, None),
            P(("grp", "own"), None, None),
            P(("grp", "own"), None),
            P(("grp", "own"), None, None),
            P(("grp", "own")),
            P(("grp", "own")),
        ),
        out_specs=(P(("grp", "own"), None, None), P(("grp", "own"), None, None)),
        check_vma=False,
    )
```

profile of v0, /device:TPU:7, one launch (start us, length us, event | category | flops | bytes accessed | tf_op | source)
XLA Modules:
  0.0 528.3 jit_solution(8652673713095691326)
XLA Ops:
  9.6 1.6 gather_fusion.1
  12.0 18.5 %all-to-all-start.1 = ((s32[64,2,1]{1,2,0:T(1,128)}), s32[64,2,1]{1,2,0:T(1,128)S(1)}, u32[]{:S(2)}, u32[]{:S(2)}) async-start(s32[64,2,1]{1,2,0:T(1,128)} %bitcast.4), calls=%async_computation.1 | async-start | bytes 65536 | tf_op jit(solution)/shard_map/all_to_all | solution.py:49
  31.2 12.7 %all-to-all-done.1 = s32[64,2,1]{1,2,0:T(1,128)S(1)} async-done(((s32[64,2,1]{1,2,0:T(1,128)}), s32[64,2,1]{1,2,0:T(1,128)S(1)}, u32[]{:S(2)}, u32[]{:S(2)}) %all-to-all-start.1) | async-done | bytes 544 | tf_op jit(solution)/shard_map/all_to_all | solution.py:49
  43.8 4.6 all-to-all-start
  48.4 2.1 gather_fusion.4
  50.6 11.4 %all-to-all-done = s32[64,2,1]{1,2,0:T(1,128)S(1)} async-done(((s32[64,2,1]{1,2,0:T(1,128)}), s32[64,2,1]{1,2,0:T(1,128)S(1)}, u32[]{:S(2)}, u32[]{:S(2)}) %all-to-all-start) | async-done | bytes 544 | tf_op jit(solution)/shard_map/all_to_all | solution.py:48
  61.9 4.7 all-to-all-start.3
  66.6 3.4 gather_fusion.2
  70.0 90.1 %all-to-all-done.3 = bf16[128,128,64]{1,2,0:T(8,128)(2,1)S(1)} async-done(((bf16[128,128,64]{1,2,0:T(8,128)(2,1)}), bf16[128,128,64]{1,2,0:T(8,128)(2,1)S(1)}, u32[]{:S(2)}, u32[]{:S(2)}) %all-to-all-start.3) | async-done | bytes 2097184 | tf_op jit(solution)/shard_map/all_to_all | solution.py:46
  160.2 1.3 copy-done.1
  161.5 10.7 %all-to-all-start.2 = ((bf16[128,128,64]{1,2,0:T(8,128)(2,1)}), bf16[128,128,64]{1,2,0:T(8,128)(2,1)S(1)}, u32[]{:S(2)}, u32[]{:S(2)}) async-start(bf16[128,128,64]{1,2,0:T(8,128)(2,1)} %gather_fusion.2), calls=%async_computation.2 | async-start | bytes 4194304 | tf_op jit(solution)/shard_map/all_to_all | solution.py:45
  172.9 1.3 gather_fusion.5
  176.7 34.6 %all-gather.2.cloned.1.call-done = bf16[160,64,64]{2,1,0:T(8,128)(2,1)} async-done(((bf16[20,64,64]{2,1,0:T(8,128)(2,1)}), bf16[160,64,64]{2,1,0:T(8,128)(2,1)}) %all-gather.2.cloned.1.call-update) | async-done | bytes 1310736 | tf_op jit(solution)/shard_map/all_gather | solution.py:39
  211.3 3.9 gather_fusion.3
  215.2 50.7 %all-to-all-done.2 = bf16[128,128,64]{1,2,0:T(8,128)(2,1)S(1)} async-done(((bf16[128,128,64]{1,2,0:T(8,128)(2,1)}), bf16[128,128,64]{1,2,0:T(8,128)(2,1)S(1)}, u32[]{:S(2)}, u32[]{:S(2)}) %all-to-all-start.2) | async-done | bytes 2097184 | tf_op jit(solution)/shard_map/all_to_all | solution.py:45
  265.9 11.0 %all-to-all-start.4 = ((bf16[64,2,128]{2,1,0:T(2,128)(2,1)}), bf16[64,2,128]{2,1,0:T(2,128)(2,1)S(1)}, u32[]{:S(2)}, u32[]{:S(2)}) async-start(bf16[64,2,128]{2,1,0:T(2,128)(2,1)} %bitcast.6), calls=%async_computation.4 | async-start | bytes 65536 | tf_op jit(solution)/shard_map/all_to_all | solution.py:47
  277.1 3.2 multiply_reduce_fusion
  280.4 9.9 %all-to-all-done.4 = bf16[64,2,128]{2,1,0:T(2,128)(2,1)S(1)} async-done(((bf16[64,2,128]{2,1,0:T(2,128)(2,1)}), bf16[64,2,128]{2,1,0:T(2,128)(2,1)S(1)}, u32[]{:S(2)}, u32[]{:S(2)}) %all-to-all-start.4) | async-done | bytes 32800 | tf_op jit(solution)/shard_map/all_to_all | solution.py:47
  290.4 4.8 fusion
  295.2 4.8 copy.30
  299.9 5.4 %fusion.1 = f32[160,64,64]{0,2,1:T(8,128)} fusion(f32[128,64,64]{0,2,1:T(8,128)} %copy.30, s32[128]{0:T(128)S(1)} %eq.50), kind=kOutput, calls=%fused_computation.12 | convolution fusion | flops 1006653440 | bytes 4719104 | tf_op jit(solution)/shard_map/dot_general | solution.py:53
  305.3 4.9 copy.26
  310.3 75.1 %all-reduce.2.cloned.1.call-done = f32[160,64,64]{0,2,1:T(8,128)} async-done(((f32[160,64,64]{0,2,1:T(8,128)}), f32[160,64,64]{0,2,1:T(8,128)}) %all-reduce.2.cloned.1.call-update) | async-done | bytes 2621456 | tf_op jit(solution)/shard_map/psum | solution.py:59
  385.4 5.0 subtract_convert_fusion
  390.4 5.0 copy.31
  395.4 3.9 gather_fusion.6
  399.3 3.8 convolution_convert_fusion
  403.0 15.8 %all-to-all-start.5 = ((bf16[128,128,64]{1,2,0:T(8,128)(2,1)}), bf16[128,128,64]{1,2,0:T(8,128)(2,1)}, u32[]{:S(2)}, u32[]{:S(2)}) async-start(bf16[128,128,64]{1,2,0:T(8,128)(2,1)} %convolution_convert_fusion), calls=%async_computation.5 | async-start | bytes 4194304 | tf_op jit(solution)/shard_map/all_to_all | solution.py:67
  418.8 1.5 constant_dynamic-slice_fusion
  420.3 2.6 copy.33
  422.8 95.4 %all-to-all-done.5 = bf16[128,128,64]{1,2,0:T(8,128)(2,1)} async-done(((bf16[128,128,64]{1,2,0:T(8,128)(2,1)}), bf16[128,128,64]{1,2,0:T(8,128)(2,1)}, u32[]{:S(2)}, u32[]{:S(2)}) %all-to-all-start.5) | async-done | bytes 2097184 | tf_op jit(solution)/shard_map/all_to_all | solution.py:67
  518.3 3.2 gather_fusion.7
  (33 shorter events, 7.4 us)
Async XLA Ops:
  7.2 41.3 %copy-start = (bf16[64,128,64]{1,2,0:T(8,128)(2,1)S(1)}, bf16[64,128,64]{1,2,0:T(8,128)(2,1)}, u32[]{:S(2)}) copy-start(bf16[64,128,64]{1,2,0:T(8,128)(2,1)} %param.7) | copy-start | bytes 3145732
  12.0 31.9 %all-to-all-start.1 = ((s32[64,2,1]{1,2,0:T(1,128)}), s32[64,2,1]{1,2,0:T(1,128)S(1)}, u32[]{:S(2)}, u32[]{:S(2)}) async-start(s32[64,2,1]{1,2,0:T(1,128)} %bitcast.4), calls=%async_computation.1 | async-start | bytes 65536 | tf_op jit(solution)/shard_map/all_to_all | solution.py:49
  43.8 18.1 %all-to-all-start = ((s32[64,2,1]{1,2,0:T(1,128)}), s32[64,2,1]{1,2,0:T(1,128)S(1)}, u32[]{:S(2)}, u32[]{:S(2)}) async-start(s32[64,2,1]{1,2,0:T(1,128)} %bitcast.2), calls=%async_computation | async-start | bytes 65536 | tf_op jit(solution)/shard_map/all_to_all | solution.py:48
  61.9 98.2 %all-to-all-start.3 = ((bf16[128,128,64]{1,2,0:T(8,128)(2,1)}), bf16[128,128,64]{1,2,0:T(8,128)(2,1)S(1)}, u32[]{:S(2)}, u32[]{:S(2)}) async-start(bf16[128,128,64]{1,2,0:T(8,128)(2,1)} %gather_fusion.4), calls=%async_computation.3 | async-start | bytes 4194304 | tf_op jit(solution)/shard_map/all_to_all | solution.py:46
  70.0 102.9 %copy-start.3 = (bf16[64,128]{1,0:T(8,128)(2,1)S(1)}, bf16[64,128]{1,0:T(8,128)(2,1)}, u32[]{:S(2)}) copy-start(bf16[64,128]{1,0:T(8,128)(2,1)} %param.8) | copy-start | bytes 49156
  160.2 1.3 copy-start.1
  161.5 104.4 %all-to-all-start.2 = ((bf16[128,128,64]{1,2,0:T(8,128)(2,1)}), bf16[128,128,64]{1,2,0:T(8,128)(2,1)S(1)}, u32[]{:S(2)}, u32[]{:S(2)}) async-start(bf16[128,128,64]{1,2,0:T(8,128)(2,1)} %gather_fusion.2), calls=%async_computation.2 | async-start | bytes 4194304 | tf_op jit(solution)/shard_map/all_to_all | solution.py:45
  172.2 39.1 %all-gather.2.cloned.1.call-start = ((), (), s32[]{:S(2)}) async-start(), calls=%async_computation.6 | async-start | bytes 2949120 | tf_op jit(solution)/shard_map/all_gather | solution.py:39
  265.9 24.4 %all-to-all-start.4 = ((bf16[64,2,128]{2,1,0:T(2,128)(2,1)}), bf16[64,2,128]{2,1,0:T(2,128)(2,1)S(1)}, u32[]{:S(2)}, u32[]{:S(2)}) async-start(bf16[64,2,128]{2,1,0:T(2,128)(2,1)} %bitcast.6), calls=%async_computation.4 | async-start | bytes 65536 | tf_op jit(solution)/shard_map/all_to_all | solution.py:47
  276.9 108.5 %all-reduce.2.cloned.1.call-start = ((), (), s32[]{:S(2)}) async-start(), calls=%async_computation.7 | async-start | bytes 8388608 | tf_op jit(solution)/shard_map/psum | solution.py:59
  403.0 15.8 %copy-start.2 = (bf16[160,64,64]{0,2,1:T(8,128)(2,1)S(1)}, bf16[160,64,64]{0,2,1:T(8,128)(2,1)}, u32[]{:S(2)}) copy-start(bf16[160,64,64]{0,2,1:T(8,128)(2,1)} %subtract_convert_fusion) | copy-start | bytes 3932164
  403.0 115.2 %all-to-all-start.5 = ((bf16[128,128,64]{1,2,0:T(8,128)(2,1)}), bf16[128,128,64]{1,2,0:T(8,128)(2,1)}, u32[]{:S(2)}, u32[]{:S(2)}) async-start(bf16[128,128,64]{1,2,0:T(8,128)(2,1)} %convolution_convert_fusion), calls=%async_computation.5 | async-start | bytes 4194304 | tf_op jit(solution)/shard_map/all_to_all | solution.py:67
Sparse Core Ops, SparseCore 0:
  175.1 36.1 all-gather.1
  305.5 79.8 all-reduce.1
where the time goes:
time: 529 us; the launch traced here: 528 us
  waiting for transfers between devices  381 us (72%)
  starting transfers between devices  65.5 us (12%)
  local copies, waits for them, and re-layouts  43.1 us (8%)
  matrix products  17.1 us (3%)
  between operations  14.2 us (3%)
  other arithmetic  7.74 us (1%)
    all_to_all x1, waiting for transfers between devices, body(): lax.all_to_all(refreshed, 'own', split_axis=0, concat_axis=0, tiled=True)  95.4 us
    all_to_all x1, waiting for transfers between devices, body(): lax.all_to_all(send_right, 'own', split_axis=0, concat_axis=0, tiled=True)  90.1 us
    psum x1, waiting for transfers between devices, body(): grad_whole = lax.psum(grad_part, 'grp')  75.1 us
    all_to_all x1, waiting for transfers between devices, body(): lax.all_to_all(send_left, 'own', split_axis=0, concat_axis=0, tiled=True)  50.7 us
    all_gather x1, waiting for transfers between devices, body(): old_tables = lax.all_gather(core, 'grp', axis=0, tiled=True)  34.6 us
    all_to_all x1, starting transfers between devices, body(): lax.all_to_all(send_fill, 'own', split_axis=0, concat_axis=0, tiled=True)  18.5 us
    all_to_all x1, starting transfers between devices, body(): lax.all_to_all(refreshed, 'own', split_axis=0, concat_axis=0, tiled=True)  15.8 us
    all_to_all x1, waiting for transfers between devices, body(): lax.all_to_all(send_fill, 'own', split_axis=0, concat_axis=0, tiled=True)  12.7 us
  transfers between devices with their start and end apart: 8, of which 8 were waited for; matrix products, arithmetic and copies ran while one was open for 5% of the time, Pallas kernels for 0%

commit v1 on v0

v1 whole, which is shorter than its diff:
```python
import functools

import jax
import jax.numpy as jnp
from jax import lax
from jax.experimental import pallas as pl
from jax.experimental.pallas import tpu as pltpu
from jax.sharding import PartitionSpec as P

VMEM = pl.BlockSpec(memory_space=pltpu.VMEM)
SMEM = pl.BlockSpec(memory_space=pltpu.SMEM)
BF16 = jnp.bfloat16
F32 = jnp.float32


def pack(square):
    half = square.shape[0] // 2
    return jnp.concatenate([square[:half], square[half:]], axis=1)


def unpack(packed):
    width = packed.shape[1] // 2
    return jnp.concatenate([packed[:, :width], packed[:, width:]], axis=0)


def pack_kernel(core_ref, out_ref):
    for i in range(core_ref.shape[0]):
        out_ref[i] = pack(core_ref[i].astype(F32).T).astype(BF16)


def pick_kernel(ids_ref, table_ref, out_ref):
    def step(k, carry):
        out_ref[k] = table_ref[jnp.maximum(ids_ref[k], 0)]
        return carry

    lax.fori_loop(0, out_ref.shape[0], step, 0, unroll=8)


def grad_kernel(slot_ref, fill_ref, left_ref, right_ref, value_ref, slice_ref, out_ref, value_scr):
    value_scr[...] = value_ref[...].astype(F32)
    lanes = lax.broadcasted_iota(jnp.int32, (1, left_ref.shape[2]), 1)

    def step(t, carry):
        slot = slot_ref[t]
        left = left_ref[t]
        right = right_ref[t]
        table = unpack(slice_ref[slot])
        projected = jnp.dot(table, left, preferred_element_type=F32)
        predicted = jnp.sum(projected * right.astype(F32), axis=0, keepdims=True)
        residual = jnp.where(lanes < fill_ref[t], predicted - value_scr[pl.ds(t, 1), :], 0.0)
        weighted = (residual * left.astype(F32)).astype(BF16)
        grad = lax.dot_general(
            right, weighted, (((1,), (1,)), ((), ())), preferred_element_type=F32
        )
        out_ref[slot] = pack(grad).astype(BF16)
        return carry

    lax.fori_loop(0, left_ref.shape[0], step, 0, unroll=8)


def sum_kernel(ids_ref, grad_ref, out_ref, acc_ref):
    acc_ref[...] = jnp.zeros_like(acc_ref)

    def step(k, carry):
        @pl.when(ids_ref[k] >= 0)
        def _():
            acc_ref[ids_ref[k]] += grad_ref[k].astype(F32)

        return carry

    lax.fori_loop(0, grad_ref.shape[0], step, 0, unroll=4)
    out_ref[...] = acc_ref[...].astype(BF16)


def update_kernel(table_ref, part_ref, packed_ref, out_ref):
    total = jnp.sum(part_ref[...].astype(F32), axis=0)
    packed_ref[...] = (table_ref[...].astype(F32) - total).astype(BF16)
    for i in range(out_ref.shape[0]):
        out_ref[i] = unpack(packed_ref[i].astype(F32)).T.astype(BF16)


def refresh_kernel(slot_ref, left_ref, slice_ref, out_ref):
    def step(t, carry):
        table = unpack(slice_ref[slot_ref[t]])
        out_ref[t] = jnp.dot(table, left_ref[t], preferred_element_type=F32).astype(BF16)
        return carry

    lax.fori_loop(0, left_ref.shape[0], step, 0, unroll=8)


def call(kernel, in_specs, outs, scratch=(), flops=10**6, moved=4 * 10**6):
    many = isinstance(outs, tuple)
    return pl.pallas_call(
        kernel,
        out_shape=outs,
        in_specs=in_specs,
        out_specs=(VMEM,) * len(outs) if many else VMEM,
        scratch_shapes=list(scratch),
        cost_estimate=pl.CostEstimate(flops=flops, bytes_accessed=moved, transcendentals=0),
    )


def exchange(x, axis):
    return lax.all_to_all(x, axis, split_axis=0, concat_axis=0, tiled=True)


def body(left, right, values, core, tile_slice, tile_fill):
    owners = lax.axis_size("own")
    groups = lax.axis_size("grp")
    tiles, rows, rank = left.shape
    per_device = core.shape[0]
    local_count = groups * per_device
    slots = 2 * owners
    packed_shape = (rank // 2, 2 * rank)

    block = tile_slice // per_device
    owner = block % owners
    local = block // owners * per_device + tile_slice % per_device
    position = jnp.arange(tiles)
    same = (owner[:, None] == owner[None, :]) & (position[None, :] < position[:, None])
    slot = 2 * owner + jnp.sum(same.astype(jnp.int32), axis=1)
    hit = slot[None, :] == jnp.arange(slots)[:, None]
    wanted = jnp.max(jnp.where(hit, local[None, :], -1), axis=1)

    left_t = jnp.swapaxes(left, 1, 2)
    right_t = jnp.swapaxes(right, 1, 2)
    sds = jax.ShapeDtypeStruct
    slot_sds = sds((slots,) + packed_shape, BF16)

    mine = call(pack_kernel, [VMEM], sds((per_device,) + packed_shape, BF16))(core)
    ids = exchange(wanted.reshape(owners, 2), "own").reshape(slots)
    spread = jnp.broadcast_to(mine[None], (groups,) + mine.shape).reshape((local_count,) + packed_shape)
    tables = exchange(spread, "grp")
    outgoing = call(pick_kernel, [SMEM, VMEM], slot_sds)(ids, tables)
    got = exchange(outgoing, "own")
    grads = call(
        grad_kernel,
        [SMEM, SMEM, VMEM, VMEM, VMEM, VMEM],
        slot_sds,
        [pltpu.VMEM((tiles, rows), F32)],
    )(slot, tile_fill, left_t, right_t, values, got)
    got_grads = exchange(grads, "own")
    partial = call(
        sum_kernel,
        [SMEM, VMEM],
        sds((local_count,) + packed_shape, BF16),
        [pltpu.VMEM((local_count,) + packed_shape, F32)],
    )(ids, got_grads)
    parts = exchange(partial, "grp").reshape((groups, per_device) + packed_shape)
    new_mine, new_core = call(
        update_kernel,
        [VMEM, VMEM],
        (sds((per_device,) + packed_shape, BF16), sds(core.shape, BF16)),
    )(mine, parts)
    new_spread = jnp.broadcast_to(new_mine[None], (groups,) + mine.shape).reshape(spread.shape)
    new_tables = exchange(new_spread, "grp")
    new_outgoing = call(pick_kernel, [SMEM, VMEM], slot_sds)(ids, new_tables)
    new_got = exchange(new_outgoing, "own")
    new_left_t = call(refresh_kernel, [SMEM, VMEM, VMEM], sds(left_t.shape, BF16))(
        slot, left_t, new_got
    )
    return (new_core, jnp.swapaxes(new_left_t, 1, 2))


def solution(mesh):
    spec3 = P(("grp", "own"), None, None)
    spec2 = P(("grp", "own"), None)
    spec1 = P(("grp", "own"))
    return jax.shard_map(
        body,
        mesh=mesh,
        in_specs=(spec3, spec3, spec2, spec3, spec1, spec1),
        out_specs=(spec3, spec3),
        check_vma=False,
    )
```

time: 529 us -> 318 us (0.60)
  the two profiles are of different devices: /device:TPU:7 before, /device:TPU:8 now
where the time goes in v1:
time: 318 us; the launch traced here: 317 us
  blocking collectives  227 us (71%)
  waiting for transfers between devices  28.7 us (9%)
  Pallas kernels  28.3 us (9%)
  starting transfers between devices  23 us (7%)
  local copies, waits for them, and re-layouts  6.32 us (2%)
    all_to_all x5, blocking collectives, exchange(): return lax.all_to_all(x, axis, split_axis=0, concat_axis=0, tiled=True)  227 us
    all_to_all x2, waiting for transfers between devices, exchange(): return lax.all_to_all(x, axis, split_axis=0, concat_axis=0, tiled=True)  28.7 us
    all_to_all x2, starting transfers between devices, exchange(): return lax.all_to_all(x, axis, split_axis=0, concat_axis=0, tiled=True)  23 us
    pallas_call x1, Pallas kernels, body(): call(grad_kernel, [SMEM, SMEM, VMEM, VMEM, VMEM, VMEM], slot_sds, [pltpu....  10.3 us
  transfers between devices with their start and end apart: 2, of which 2 were waited for; matrix products, arithmetic and copies ran while one was open for 1% of the time, Pallas kernels for 1%

profile of v1, /device:TPU:8, one launch (start us, length us, event | category | flops | bytes accessed | tf_op | source)
XLA Modules:
  0.0 316.9 jit_solution(17393610980712999822)
XLA Ops:
  0.6 0.7 and_select_fusion.2
  1.3 0.7 fusion.1
  2.0 0.2 convert_reduce_fusion
  2.2 0.0 copy-start.1
  2.2 0.1 select_reduce_fusion
  2.3 0.8 all_to_all.24
  3.0 18.7 %all-to-all-start = ((s32[64,1,2]{2,1,0:T(1,128)}), s32[64,1,2]{2,1,0:T(1,128)S(1)}, u32[]{:S(2)}, u32[]{:S(2)}) async-start(s32[64,1,2]{2,1,0:T(1,128)} %bitcast), calls=%async_computation | async-start | bytes 65536 | tf_op jit(solution)/shard_map/all_to_all | solution.py:104
  21.8 1.9 shard_map.77.table_ref
  23.6 11.9 %all-to-all-done = s32[64,1,2]{2,1,0:T(1,128)S(1)} async-done(((s32[64,1,2]{2,1,0:T(1,128)}), s32[64,1,2]{2,1,0:T(1,128)S(1)}, u32[]{:S(2)}, u32[]{:S(2)}) %all-to-all-start) | async-done | bytes 544 | tf_op jit(solution)/shard_map/all_to_all | solution.py:104
  35.5 2.2 broadcast_in_dim.18
  37.7 0.0 copy-done.1
  37.7 4.3 %all-to-all-start.1 = ((bf16[160,32,128]{2,1,0:T(8,128)(2,1)}), bf16[160,32,128]{2,1,0:T(8,128)(2,1)S(1)}, u32[]{:S(2)}, u32[]{:S(2)}) async-start(bf16[160,32,128]{2,1,0:T(8,128)(2,1)} %bitcast.3), calls=%async_computation.1 | async-start | bytes 2621440 | tf_op jit(solution)/shard_map/all_to_all | solution.py:104
  42.0 0.5 broadcast.20
  42.5 0.7 reduce.3
  43.3 0.7 reshape.27.ids_ref
  43.9 16.8 %all-to-all-done.1.table_ref = bf16[160,32,128]{2,1,0:T(8,128)(2,1)S(1)} async-done(((bf16[160,32,128]{2,1,0:T(8,128)(2,1)}), bf16[160,32,128]{2,1,0:T(8,128)(2,1)S(1)}, u32[]{:S(2)}, u32[]{:S(2)}) %all-to-all-start.1) | async-done | bytes 1310752 | tf_op jit(solution)/shard_map/all_to_all | solution.py:104
  60.8 0.0 copy-start
  60.8 1.1 copy-done
  61.8 2.6 shard_map.78
  64.4 61.4 %all_to_all.39.slice_ref = bf16[128,32,128]{2,1,0:T(8,128)(2,1)} all-to-all(bf16[128,32,128]{2,1,0:T(8,128)(2,1)} %shard_map.78), channel_id=1, replica_groups=mesh['grp'=8,'own'=64] {'own'}, dimensions={0} | all-to-all | bytes 2097152 | tf_op jit(solution)/shard_map/all_to_all | solution.py:104
  125.8 10.3 %shard_map.79 = bf16[128,32,128]{2,1,0:T(8,128)(2,1)} custom-call(s32[64]{0:T(128)} %copy-done.1, s32[64]{0:T(128)} %fill_ref.1, bf16[64,64,128]{2,1,0:T(8,128)(2,1)} %bitcast.9, bf16[64,64,128]{2,1,0:T(8,128)(2,1)} %bitcast.11, bf16[64,128]{1,0:T(8,128)(2,1)} %value_ref.1, bf16[128,32,128]{2,1,0:T(8,128)(2,1)} %all_to_all.39.slice_ref), custom_call_target="tpu_custom_call" | custom-call | flops 1000000 | bytes 4000000 | tf_op jit(solution)/shard_map/pallas_call | solution.py:136
  136.0 60.3 %all_to_all.40.grad_ref = bf16[128,32,128]{2,1,0:T(8,128)(2,1)} all-to-all(bf16[128,32,128]{2,1,0:T(8,128)(2,1)} %shard_map.79), channel_id=1, replica_groups=mesh['grp'=8,'own'=64] {'own'}, dimensions={0} | all-to-all | bytes 2097152 | tf_op jit(solution)/shard_map/all_to_all | solution.py:104
  196.4 4.1 %shard_map.80 = bf16[160,32,128]{2,1,0:T(8,128)(2,1)} custom-call(s32[128]{0:T(128)} %reshape.27.ids_ref, bf16[128,32,128]{2,1,0:T(8,128)(2,1)} %all_to_all.40.grad_ref), custom_call_target="tpu_custom_call" | custom-call | flops 1000000 | bytes 4000000 | tf_op jit(solution)/shard_map/pallas_call | solution.py:143
  200.5 23.0 %all_to_all.41 = bf16[160,32,128]{2,1,0:T(8,128)(2,1)} all-to-all(bf16[160,32,128]{2,1,0:T(8,128)(2,1)} %shard_map.80), channel_id=1, replica_groups=mesh['grp'=8,'own'=64] {'grp'}, dimensions={0} | all-to-all | bytes 2621440 | tf_op jit(solution)/shard_map/all_to_all | solution.py:104
  223.5 2.6 shard_map.81
  226.2 1.1 broadcast_in_dim.19
  227.3 21.9 %all_to_all.42.table_ref = bf16[160,32,128]{2,1,0:T(8,128)(2,1)} all-to-all(bf16[160,32,128]{2,1,0:T(8,128)(2,1)S(1)} %bitcast.8), channel_id=1, replica_groups=mesh['grp'=8,'own'=64] {'grp'}, dimensions={0} | all-to-all | bytes 2621440 | tf_op jit(solution)/shard_map/all_to_all | solution.py:104
  249.2 2.6 shard_map.82
  251.8 60.8 %all_to_all.43.slice_ref = bf16[128,32,128]{2,1,0:T(8,128)(2,1)} all-to-all(bf16[128,32,128]{2,1,0:T(8,128)(2,1)} %shard_map.82), channel_id=1, replica_groups=mesh['grp'=8,'own'=64] {'own'}, dimensions={0} | all-to-all | bytes 2097152 | tf_op jit(solution)/shard_map/all_to_all | solution.py:104
  312.6 4.3 %shard_map.83 = bf16[64,64,128]{2,1,0:T(8,128)(2,1)} custom-call(s32[64]{0:T(128)} %copy-done.1, bf16[64,64,128]{2,1,0:T(8,128)(2,1)} %bitcast.10, bf16[128,32,128]{2,1,0:T(8,128)(2,1)} %all_to_all.43.slice_ref), custom_call_target="tpu_custom_call" | custom-call | flops 1000000 | bytes 4000000 | tf_op jit(solution)/shard_map/pallas_call | solution.py:159
  (1 shorter events, 0.0 us)
Async XLA Ops:
  2.2 35.6 %copy-start.1 = (s32[64]{0:T(128)}, s32[64]{0:T(128)S(1)}, u32[]{:S(2)}) copy-start(s32[64]{0:T(128)S(1)} %multiply_add_fusion.slot_ref) | copy-start | bytes 772
  3.0 32.5 %all-to-all-start = ((s32[64,1,2]{2,1,0:T(1,128)}), s32[64,1,2]{2,1,0:T(1,128)S(1)}, u32[]{:S(2)}, u32[]{:S(2)}) async-start(s32[64,1,2]{2,1,0:T(1,128)} %bitcast), calls=%async_computation | async-start | bytes 65536 | tf_op jit(solution)/shard_map/all_to_all | solution.py:104
  37.7 23.0 %all-to-all-start.1 = ((bf16[160,32,128]{2,1,0:T(8,128)(2,1)}), bf16[160,32,128]{2,1,0:T(8,128)(2,1)S(1)}, u32[]{:S(2)}, u32[]{:S(2)}) async-start(bf16[160,32,128]{2,1,0:T(8,128)(2,1)} %bitcast.3), calls=%async_computation.1 | async-start | bytes 2621440 | tf_op jit(solution)/shard_map/all_to_all | solution.py:104
  60.8 1.1 copy-start

commit v2 on v1

--- a/solution.py
+++ b/solution.py
@@ -28,7 +28,12 @@
         out_ref[i] = pack(core_ref[i].astype(F32).T).astype(BF16)
 
 
-def pick_kernel(ids_ref, table_ref, out_ref):
+def pick_kernel(ids_ref, *refs):
+    pieces, out_ref, table_ref = refs[:-2], refs[-2], refs[-1]
+    size = pieces[0].shape[0]
+    for i, piece in enumerate(pieces):
+        table_ref[pl.ds(i * size, size)] = piece[...]
+
     def step(k, carry):
         out_ref[k] = table_ref[jnp.maximum(ids_ref[k], 0)]
         return carry
@@ -58,7 +63,7 @@
     lax.fori_loop(0, left_ref.shape[0], step, 0, unroll=8)
 
 
-def sum_kernel(ids_ref, grad_ref, out_ref, acc_ref):
+def sum_kernel(ids_ref, grad_ref, near_ref, far_ref, acc_ref):
     acc_ref[...] = jnp.zeros_like(acc_ref)
 
     def step(k, carry):
@@ -69,11 +74,24 @@
         return carry
 
     lax.fori_loop(0, grad_ref.shape[0], step, 0, unroll=4)
-    out_ref[...] = acc_ref[...].astype(BF16)
-
-
-def update_kernel(table_ref, part_ref, packed_ref, out_ref):
-    total = jnp.sum(part_ref[...].astype(F32), axis=0)
+    half = near_ref.shape[0]
+    near_ref[...] = acc_ref[:half]
+    far_ref[...] = acc_ref[half:].astype(BF16)
+
+
+def join_kernel(near_ref, other_ref, keep_ref, *send_refs):
+    size = keep_ref.shape[0]
+    keep_ref[...] = near_ref[:size] + other_ref[:size].astype(F32)
+    for i, send_ref in enumerate(send_refs):
+        rows = pl.ds((i + 1) * size, size)
+        send_ref[...] = (near_ref[rows] + other_ref[rows].astype(F32)).astype(BF16)
+
+
+def update_kernel(table_ref, keep_ref, *refs):
+    parts, packed_ref, out_ref = refs[:-2], refs[-2], refs[-1]
+    total = keep_ref[...]
+    for part in parts:
+        total += part[...].astype(F32)
     packed_ref[...] = (table_ref[...].astype(F32) - total).astype(BF16)
     for i in range(out_ref.shape[0]):
         out_ref[i] = unpack(packed_ref[i].astype(F32)).T.astype(BF16)
@@ -104,9 +122,24 @@
     return lax.all_to_all(x, axis, split_axis=0, concat_axis=0, tiled=True)
 
 
+def shift(x, groups, step):
+    return lax.ppermute(x, "grp", [(g, (g + 2 * step) % groups) for g in range(groups)])
+
+
+def swap(x, groups):
+    return lax.ppermute(x, "grp", [(g, g ^ 1) for g in range(groups)])
+
+
+def spread(mine, groups):
+    near = [mine] + [shift(mine, groups, -k) for k in range(1, groups // 2)]
+    return near + [swap(piece, groups) for piece in near]
+
+
 def body(left, right, values, core, tile_slice, tile_fill):
     owners = lax.axis_size("own")
     groups = lax.axis_size("grp")
+    chips = groups // 2
+    me = lax.axis_index("grp")
     tiles, rows, rank = left.shape
     per_device = core.shape[0]
     local_count = groups * per_device
@@ -115,7 +148,10 @@
 
     block = tile_slice // per_device
     owner = block % owners
-    local = block // owners * per_device + tile_slice % per_device
+    group = block // owners
+    side = (group % 2) ^ (me % 2)
+    away = (group // 2 - me // 2) % chips
+    local = (side * chips + away) * per_device + tile_slice % per_device
     position = jnp.arange(tiles)
     same = (owner[:, None] == owner[None, :]) & (position[None, :] < position[:, None])
     slot = 2 * owner + jnp.sum(same.astype(jnp.int32), axis=1)
@@ -126,13 +162,14 @@
     right_t = jnp.swapaxes(right, 1, 2)
     sds = jax.ShapeDtypeStruct
     slot_sds = sds((slots,) + packed_shape, BF16)
-
-    mine = call(pack_kernel, [VMEM], sds((per_device,) + packed_shape, BF16))(core)
+    mine_sds = sds((per_device,) + packed_shape, BF16)
+    keep_sds = sds((per_device,) + packed_shape, F32)
+    table_scr = pltpu.VMEM((local_count,) + packed_shape, BF16)
+    pick = call(pick_kernel, [SMEM] + [VMEM] * groups, slot_sds, [table_scr])
+
+    mine = call(pack_kernel, [VMEM], mine_sds)(core)
     ids = exchange(wanted.reshape(owners, 2), "own").reshape(slots)
-    spread = jnp.broadcast_to(mine[None], (groups,) + mine.shape).reshape((local_count,) + packed_shape)
-    tables = exchange(spread, "grp")
-    outgoing = call(pick_kernel, [SMEM, VMEM], slot_sds)(ids, tables)
-    got = exchange(outgoing, "own")
+    got = exchange(pick(ids, *spread(mine, groups)), "own")
     grads = call(
         grad_kernel,
         [SMEM, SMEM, VMEM, VMEM, VMEM, VMEM],
@@ -140,22 +177,23 @@
         [pltpu.VMEM((tiles, rows), F32)],
     )(slot, tile_fill, left_t, right_t, values, got)
     got_grads = exchange(grads, "own")
-    partial = call(
+    near, far = call(
         sum_kernel,
         [SMEM, VMEM],
-        sds((local_count,) + packed_shape, BF16),
+        (
+            sds((local_count // 2,) + packed_shape, F32),
+            sds((local_count // 2,) + packed_shape, BF16),
+        ),
         [pltpu.VMEM((local_count,) + packed_shape, F32)],
     )(ids, got_grads)
-    parts = exchange(partial, "grp").reshape((groups, per_device) + packed_shape)
+    keep, *send = call(join_kernel, [VMEM] * 2, (keep_sds,) + (mine_sds,) * (chips - 1))(
+        near, swap(far, groups)
+    )
+    parts = [shift(x, groups, k + 1) for k, x in enumerate(send)]
     new_mine, new_core = call(
-        update_kernel,
-        [VMEM, VMEM],
-        (sds((per_device,) + packed_shape, BF16), sds(core.shape, BF16)),
-    )(mine, parts)
-    new_spread = jnp.broadcast_to(new_mine[None], (groups,) + mine.shape).reshape(spread.shape)
-    new_tables = exchange(new_spread, "grp")
-    new_outgoing = call(pick_kernel, [SMEM, VMEM], slot_sds)(ids, new_tables)
-    new_got = exchange(new_outgoing, "own")
+        update_kernel, [VMEM] * (chips + 1), (mine_sds, sds(core.shape, BF16))
+    )(mine, keep, *parts)
+    new_got = exchange(pick(ids, *spread(new_mine, groups)), "own")
     new_left_t = call(refresh_kernel, [SMEM, VMEM, VMEM], sds(left_t.shape, BF16))(
         slot, left_t, new_got
     )

time: 318 us -> 315 us (level)
  starting transfers between devices: 23 us -> 51.3 us
  waiting for transfers between devices: 28.7 us -> 8.31 us
  blocking collectives: 227 us -> 215 us
    ppermute x0 -> x18, starting transfers between devices: none -> 51.3 us  [the longest x9 32.6 us: shift(): lax.ppermute(x, 'grp', [(g, (g + 2 * step) % groups) for g in range(group...]
    all_to_all x2 -> x0, waiting for transfers between devices: 28.7 us -> none  [exchange(): return lax.all_to_all(x, axis, split_axis=0, concat_axis=0, tiled=True)]
    all_to_all x2 -> x0, starting transfers between devices: 23 us -> none  [exchange(): return lax.all_to_all(x, axis, split_axis=0, concat_axis=0, tiled=True)]
    all_to_all x5 -> x4, blocking collectives: 227 us -> 215 us  [exchange(): return lax.all_to_all(x, axis, split_axis=0, concat_axis=0, tiled=True)]
    ppermute x0 -> x18, waiting for transfers between devices: none -> 8.31 us  [the longest x9 5.07 us: shift(): lax.ppermute(x, 'grp', [(g, (g + 2 * step) % groups) for g in range(group...]
    broadcast_in_dim x2 -> x0, local copies, waits for them, and re-layouts: 3.33 us -> none  [the longest x1 2.2 us: body(): jnp.broadcast_to(mine[None], (groups,) + mine.shape)]
    pallas_call x5 -> x6, Pallas kernels: 13.7 us -> 16.3 us  [the longest x1 4.22 us: body(): call(sum_kernel, [SMEM, VMEM], (sds((local_count // 2,) + packed_shape, F...]
  transfers between devices with their start and end apart: 2 -> 18, of which waited for: 2 -> 5; matrix products, arithmetic and copies ran while one was open for 1% -> 1% of each run, Pallas kernels for 1% -> 0%
where the time goes in v2:
time: 315 us; the launch traced here: 314 us
  blocking collectives  215 us (68%)
  starting transfers between devices  51.3 us (16%)
  Pallas kernels  30.9 us (10%)
  waiting for transfers between devices  8.31 us (3%)
  local copies, waits for them, and re-layouts  4.9 us (2%)
    all_to_all x4, blocking collectives, exchange(): return lax.all_to_all(x, axis, split_axis=0, concat_axis=0, tiled=True)  215 us
    ppermute x9, starting transfers between devices, shift(): lax.ppermute(x, 'grp', [(g, (g + 2 * step) % groups) for g in range(group...  32.6 us
    ppermute x9, starting transfers between devices, swap(): return lax.ppermute(x, 'grp', [(g, g ^ 1) for g in range(groups)])  18.7 us
    pallas_call x1, Pallas kernels, body(): call(grad_kernel, [SMEM, SMEM, VMEM, VMEM, VMEM, VMEM], slot_sds, [pltpu....  10.3 us
  transfers between devices with their start and end apart: 18, of which 5 were waited for; matrix products, arithmetic and copies ran while one was open for 1% of the time, Pallas kernels for 0%

profile of v2, /device:TPU:8, one launch (start us, length us, event | category | flops | bytes accessed | tf_op | source)
XLA Modules:
  0.0 314.0 jit_solution(4332362621438056058)
XLA Ops:
  2.5 1.9 collective-permute-start.3
  4.4 3.4 %collective-permute-start.2 = (bf16[20,32,128]{2,1,0:T(8,128)(2,1)}, bf16[20,32,128]{2,1,0:T(8,128)(2,1)S(1)}, u32[]{:S(2)}, u32[]{:S(2)}) collective-permute-start(bf16[20,32,128]{2,1,0:T(8,128)(2,1)} %shard_map.77.refs_0_.table_ref), channel_id=1, source_target_pairs={{0,128},{64,192},{128,256},{192,320},{256,384},{320,448},{384,0},{... | collective-permute-start | bytes 491528 | tf_op jit(solution)/shard_map/ppermute | solution.py:126
  7.8 4.6 %collective-permute-start.1 = (bf16[20,32,128]{2,1,0:T(8,128)(2,1)}, bf16[20,32,128]{2,1,0:T(8,128)(2,1)S(1)}, u32[]{:S(2)}, u32[]{:S(2)}) collective-permute-start(bf16[20,32,128]{2,1,0:T(8,128)(2,1)} %shard_map.77.refs_0_.table_ref), channel_id=1, source_target_pairs={{0,256},{64,320},{128,384},{192,448},{256,0},{320,64},{384,128},{4... | collective-permute-start | bytes 491528 | tf_op jit(solution)/shard_map/ppermute | solution.py:126
  12.5 3.3 %collective-permute-start = (bf16[20,32,128]{2,1,0:T(8,128)(2,1)}, bf16[20,32,128]{2,1,0:T(8,128)(2,1)S(1)}, u32[]{:S(2)}, u32[]{:S(2)}) collective-permute-start(bf16[20,32,128]{2,1,0:T(8,128)(2,1)} %shard_map.77.refs_0_.table_ref), channel_id=1, source_target_pairs={{0,384},{64,448},{128,0},{192,64},{256,128},{320,192},{384,256},{4... | collective-permute-start | bytes 491528 | tf_op jit(solution)/shard_map/ppermute | solution.py:126
  16.8 1.9 collective-permute-start.6
  18.8 2.3 collective-permute-start.5
  21.1 2.0 collective-permute-start.4
  24.1 32.3 %all_to_all.24 = s32[64,1,2]{2,1,0:T(1,128)S(1)} all-to-all(s32[64,1,2]{2,1,0:T(1,128)S(1)} %bitcast.8), channel_id=1, replica_groups=mesh['grp'=8,'own'=64] {'own'}, dimensions={0} | all-to-all | bytes 1024 | tf_op jit(solution)/shard_map/all_to_all | solution.py:122
  59.8 2.7 shard_map.78
  62.6 60.8 %all_to_all.25.slice_ref = bf16[128,32,128]{2,1,0:T(8,128)(2,1)} all-to-all(bf16[128,32,128]{2,1,0:T(8,128)(2,1)} %shard_map.78), channel_id=1, replica_groups=mesh['grp'=8,'own'=64] {'own'}, dimensions={0} | all-to-all | bytes 2097152 | tf_op jit(solution)/shard_map/all_to_all | solution.py:122
  123.4 10.3 %shard_map.79 = bf16[128,32,128]{2,1,0:T(8,128)(2,1)} custom-call(s32[64]{0:T(128)} %copy-done.18, s32[64]{0:T(128)} %fill_ref.1, bf16[64,64,128]{2,1,0:T(8,128)(2,1)} %bitcast.4, bf16[64,64,128]{2,1,0:T(8,128)(2,1)} %bitcast.6, bf16[64,128]{1,0:T(8,128)(2,1)} %value_ref.1, bf16[128,32,128]{2,1,0:T(8,128)(2,1)} %all_to_all.25.slice_ref), custom_call_target="tpu_custom_call" | custom-call | flops 1000000 | bytes 4000000 | tf_op jit(solution)/shard_map/pallas_call | solution.py:173
  133.6 60.3 %all_to_all.26.grad_ref = bf16[128,32,128]{2,1,0:T(8,128)(2,1)} all-to-all(bf16[128,32,128]{2,1,0:T(8,128)(2,1)} %shard_map.79), channel_id=1, replica_groups=mesh['grp'=8,'own'=64] {'own'}, dimensions={0} | all-to-all | bytes 2097152 | tf_op jit(solution)/shard_map/all_to_all | solution.py:122
  193.9 4.2 %shard_map.80 = (f32[80,32,128]{2,1,0:T(8,128)}, bf16[80,32,128]{2,1,0:T(8,128)(2,1)}) custom-call(s32[128]{0:T(128)} %reshape.16.ids_ref, bf16[128,32,128]{2,1,0:T(8,128)(2,1)} %all_to_all.26.grad_ref), custom_call_target="tpu_custom_call" | custom-call | flops 1000000 | bytes 4000000 | tf_op jit(solution)/shard_map/pallas_call | solution.py:180
  198.2 1.9 collective-permute-start.7
  200.1 2.3 collective-permute-done.7.other_ref
  203.2 2.4 shard_map.81
  205.6 3.5 %collective-permute-start.8 = (bf16[20,32,128]{2,1,0:T(8,128)(2,1)}, bf16[20,32,128]{2,1,0:T(8,128)(2,1)S(1)}, u32[]{:S(2)}, u32[]{:S(2)}) collective-permute-start(bf16[20,32,128]{2,1,0:T(8,128)(2,1)} %get-tuple-element.13), channel_id=1, source_target_pairs={{0,128},{64,192},{128,256},{192,320},{256,384},{320,448},{384,0},{... | collective-permute-start | bytes 491528 | tf_op jit(solution)/shard_map/ppermute | solution.py:126
  209.1 3.9 %collective-permute-start.9 = (bf16[20,32,128]{2,1,0:T(8,128)(2,1)}, bf16[20,32,128]{2,1,0:T(8,128)(2,1)S(1)}, u32[]{:S(2)}, u32[]{:S(2)}) collective-permute-start(bf16[20,32,128]{2,1,0:T(8,128)(2,1)} %get-tuple-element.14), channel_id=1, source_target_pairs={{0,256},{64,320},{128,384},{192,448},{256,0},{320,64},{384,128},{4... | collective-permute-start | bytes 491528 | tf_op jit(solution)/shard_map/ppermute | solution.py:126
  213.0 3.2 %collective-permute-start.10 = (bf16[20,32,128]{2,1,0:T(8,128)(2,1)}, bf16[20,32,128]{2,1,0:T(8,128)(2,1)S(1)}, u32[]{:S(2)}, u32[]{:S(2)}) collective-permute-start(bf16[20,32,128]{2,1,0:T(8,128)(2,1)} %get-tuple-element.15), channel_id=1, source_target_pairs={{0,384},{64,448},{128,0},{192,64},{256,128},{320,192},{384,256},{4... | collective-permute-start | bytes 491528 | tf_op jit(solution)/shard_map/ppermute | solution.py:126
  216.2 2.8 collective-permute-done.9.refs_1_
  219.0 2.1 collective-permute-done.10.refs_2_
  221.8 2.4 shard_map.82
  224.2 3.5 %collective-permute-start.13 = (bf16[20,32,128]{2,1,0:T(8,128)(2,1)}, bf16[20,32,128]{2,1,0:T(8,128)(2,1)S(1)}, u32[]{:S(2)}, u32[]{:S(2)}) collective-permute-start(bf16[20,32,128]{2,1,0:T(8,128)(2,1)} %get-tuple-element.17.refs_0_), channel_id=1, source_target_pairs={{0,128},{64,192},{128,256},{192,320},{256,384},{320,448},{384,0},{... | collective-permute-start | bytes 491528 | tf_op jit(solution)/shard_map/ppermute | solution.py:126
  227.7 4.4 %collective-permute-start.12 = (bf16[20,32,128]{2,1,0:T(8,128)(2,1)}, bf16[20,32,128]{2,1,0:T(8,128)(2,1)S(1)}, u32[]{:S(2)}, u32[]{:S(2)}) collective-permute-start(bf16[20,32,128]{2,1,0:T(8,128)(2,1)} %get-tuple-element.17.refs_0_), channel_id=1, source_target_pairs={{0,256},{64,320},{128,384},{192,448},{256,0},{320,64},{384,128},{4... | collective-permute-start | bytes 491528 | tf_op jit(solution)/shard_map/ppermute | solution.py:126
  232.1 2.7 collective-permute-start.11
  234.8 1.9 collective-permute-start.14
  236.7 2.4 collective-permute-start.17
  239.2 1.9 collective-permute-start.16
  241.1 2.4 collective-permute-start.15
  245.2 2.7 shard_map.83
  247.9 61.8 %all_to_all.27.slice_ref = bf16[128,32,128]{2,1,0:T(8,128)(2,1)} all-to-all(bf16[128,32,128]{2,1,0:T(8,128)(2,1)} %shard_map.83), channel_id=1, replica_groups=mesh['grp'=8,'own'=64] {'own'}, dimensions={0} | all-to-all | bytes 2097152 | tf_op jit(solution)/shard_map/all_to_all | solution.py:122
  309.7 4.3 %shard_map.84 = bf16[64,64,128]{2,1,0:T(8,128)(2,1)} custom-call(s32[64]{0:T(128)} %copy-done.18, bf16[64,64,128]{2,1,0:T(8,128)(2,1)} %bitcast.5, bf16[128,32,128]{2,1,0:T(8,128)(2,1)} %all_to_all.27.slice_ref), custom_call_target="tpu_custom_call" | custom-call | flops 1000000 | bytes 4000000 | tf_op jit(solution)/shard_map/pallas_call | solution.py:197
  (63 shorter events, 10.3 us)
Async XLA Ops:
  2.5 55.9 %collective-permute-start.3 = (bf16[20,32,128]{2,1,0:T(8,128)(2,1)}, bf16[20,32,128]{2,1,0:T(8,128)(2,1)S(1)}, u32[]{:S(2)}, u32[]{:S(2)}) collective-permute-start(bf16[20,32,128]{2,1,0:T(8,128)(2,1)} %shard_map.77.refs_0_.table_ref), channel_id=1, source_target_pairs={{0,64},{64,0},{128,192},{192,128},{256,320},{320,256},{384,448},{4... | collective-permute-start | bytes 491528 | tf_op jit(solution)/shard_map/ppermute | solution.py:130
  4.4 12.3 %collective-permute-start.2 = (bf16[20,32,128]{2,1,0:T(8,128)(2,1)}, bf16[20,32,128]{2,1,0:T(8,128)(2,1)S(1)}, u32[]{:S(2)}, u32[]{:S(2)}) collective-permute-start(bf16[20,32,128]{2,1,0:T(8,128)(2,1)} %shard_map.77.refs_0_.table_ref), channel_id=1, source_target_pairs={{0,128},{64,192},{128,256},{192,320},{256,384},{320,448},{384,0},{... | collective-permute-start | bytes 491528 | tf_op jit(solution)/shard_map/ppermute | solution.py:126
  7.8 11.0 %collective-permute-start.1 = (bf16[20,32,128]{2,1,0:T(8,128)(2,1)}, bf16[20,32,128]{2,1,0:T(8,128)(2,1)S(1)}, u32[]{:S(2)}, u32[]{:S(2)}) collective-permute-start(bf16[20,32,128]{2,1,0:T(8,128)(2,1)} %shard_map.77.refs_0_.table_ref), channel_id=1, source_target_pairs={{0,256},{64,320},{128,384},{192,448},{256,0},{320,64},{384,128},{4... | collective-permute-start | bytes 491528 | tf_op jit(solution)/shard_map/ppermute | solution.py:126
  12.5 8.6 %collective-permute-start = (bf16[20,32,128]{2,1,0:T(8,128)(2,1)}, bf16[20,32,128]{2,1,0:T(8,128)(2,1)S(1)}, u32[]{:S(2)}, u32[]{:S(2)}) collective-permute-start(bf16[20,32,128]{2,1,0:T(8,128)(2,1)} %shard_map.77.refs_0_.table_ref), channel_id=1, source_target_pairs={{0,384},{64,448},{128,0},{192,64},{256,128},{320,192},{384,256},{4... | collective-permute-start | bytes 491528 | tf_op jit(solution)/shard_map/ppermute | solution.py:126
  16.7 106.6 %copy-start.18 = (s32[64]{0:T(128)}, s32[64]{0:T(128)S(1)}, u32[]{:S(2)}) copy-start(s32[64]{0:T(128)S(1)} %multiply_add_fusion.slot_ref) | copy-start | bytes 772
  16.7 41.7 %copy-start.2 = (bf16[20,32,128]{2,1,0:T(8,128)(2,1)}, bf16[20,32,128]{2,1,0:T(8,128)(2,1)S(1)}, u32[]{:S(2)}) copy-start(bf16[20,32,128]{2,1,0:T(8,128)(2,1)S(1)} %collective-permute-done.2.refs_3_) | copy-start | bytes 491524
  16.8 41.6 %collective-permute-start.6 = (bf16[20,32,128]{2,1,0:T(8,128)(2,1)S(1)}, bf16[20,32,128]{2,1,0:T(8,128)(2,1)S(1)}, u32[]{:S(2)}, u32[]{:S(2)}) collective-permute-start(bf16[20,32,128]{2,1,0:T(8,128)(2,1)S(1)} %collective-permute-done.2.refs_3_), channel_id=1, source_target_pairs={{0,64},{64,0},{128,192},{192,128},{256,320},{320,256},{384,448},{4... | collective-permute-start | bytes 491528 | tf_op jit(solution)/shard_map/ppermute | solution.py:130
  18.8 39.6 %copy-start.3 = (bf16[20,32,128]{2,1,0:T(8,128)(2,1)}, bf16[20,32,128]{2,1,0:T(8,128)(2,1)S(1)}, u32[]{:S(2)}) copy-start(bf16[20,32,128]{2,1,0:T(8,128)(2,1)S(1)} %collective-permute-done.1.refs_2_) | copy-start | bytes 491524
  18.8 39.6 %collective-permute-start.5 = (bf16[20,32,128]{2,1,0:T(8,128)(2,1)S(1)}, bf16[20,32,128]{2,1,0:T(8,128)(2,1)S(1)}, u32[]{:S(2)}, u32[]{:S(2)}) collective-permute-start(bf16[20,32,128]{2,1,0:T(8,128)(2,1)S(1)} %collective-permute-done.1.refs_2_), channel_id=1, source_target_pairs={{0,64},{64,0},{128,192},{192,128},{256,320},{320,256},{384,448},{4... | collective-permute-start | bytes 491528 | tf_op jit(solution)/shard_map/ppermute | solution.py:130
  21.1 37.3 %copy-start.4 = (bf16[20,32,128]{2,1,0:T(8,128)(2,1)}, bf16[20,32,128]{2,1,0:T(8,128)(2,1)S(1)}, u32[]{:S(2)}) copy-start(bf16[20,32,128]{2,1,0:T(8,128)(2,1)S(1)} %collective-permute-done.refs_1_) | copy-start | bytes 491524
  21.1 37.3 %collective-permute-start.4 = (bf16[20,32,128]{2,1,0:T(8,128)(2,1)S(1)}, bf16[20,32,128]{2,1,0:T(8,128)(2,1)S(1)}, u32[]{:S(2)}, u32[]{:S(2)}) collective-permute-start(bf16[20,32,128]{2,1,0:T(8,128)(2,1)S(1)} %collective-permute-done.refs_1_), channel_id=1, source_target_pairs={{0,64},{64,0},{128,192},{192,128},{256,320},{320,256},{384,448},{4... | collective-permute-start | bytes 491528 | tf_op jit(solution)/shard_map/ppermute | solution.py:130
  58.4 0.8 copy-start.8
  198.2 4.2 %collective-permute-start.7 = (bf16[80,32,128]{2,1,0:T(8,128)(2,1)}, bf16[80,32,128]{2,1,0:T(8,128)(2,1)S(1)}, u32[]{:S(2)}, u32[]{:S(2)}) collective-permute-start(bf16[80,32,128]{2,1,0:T(8,128)(2,1)} %get-tuple-element.11), channel_id=1, source_target_pairs={{0,64},{64,0},{128,192},{192,128},{256,320},{320,256},{384,448},{4... | collective-permute-start | bytes 1966088 | tf_op jit(solution)/shard_map/ppermute | solution.py:130
  202.4 0.8 copy-start
  205.6 10.6 %collective-permute-start.8 = (bf16[20,32,128]{2,1,0:T(8,128)(2,1)}, bf16[20,32,128]{2,1,0:T(8,128)(2,1)S(1)}, u32[]{:S(2)}, u32[]{:S(2)}) collective-permute-start(bf16[20,32,128]{2,1,0:T(8,128)(2,1)} %get-tuple-element.13), channel_id=1, source_target_pairs={{0,128},{64,192},{128,256},{192,320},{256,384},{320,448},{384,0},{... | collective-permute-start | bytes 491528 | tf_op jit(solution)/shard_map/ppermute | solution.py:126
  209.1 9.9 %collective-permute-start.9 = (bf16[20,32,128]{2,1,0:T(8,128)(2,1)}, bf16[20,32,128]{2,1,0:T(8,128)(2,1)S(1)}, u32[]{:S(2)}, u32[]{:S(2)}) collective-permute-start(bf16[20,32,128]{2,1,0:T(8,128)(2,1)} %get-tuple-element.14), channel_id=1, source_target_pairs={{0,256},{64,320},{128,384},{192,448},{256,0},{320,64},{384,128},{4... | collective-permute-start | bytes 491528 | tf_op jit(solution)/shard_map/ppermute | solution.py:126
  213.0 8.1 %collective-permute-start.10 = (bf16[20,32,128]{2,1,0:T(8,128)(2,1)}, bf16[20,32,128]{2,1,0:T(8,128)(2,1)S(1)}, u32[]{:S(2)}, u32[]{:S(2)}) collective-permute-start(bf16[20,32,128]{2,1,0:T(8,128)(2,1)} %get-tuple-element.15), channel_id=1, source_target_pairs={{0,384},{64,448},{128,0},{192,64},{256,128},{320,192},{384,256},{4... | collective-permute-start | bytes 491528 | tf_op jit(solution)/shard_map/ppermute | solution.py:126
  216.2 4.9 %copy-start.15 = (bf16[20,32,128]{2,1,0:T(8,128)(2,1)}, bf16[20,32,128]{2,1,0:T(8,128)(2,1)S(1)}, u32[]{:S(2)}) copy-start(bf16[20,32,128]{2,1,0:T(8,128)(2,1)S(1)} %collective-permute-done.8.refs_0_) | copy-start | bytes 491524
  219.0 2.1 copy-start.16
  224.2 12.5 %collective-permute-start.13 = (bf16[20,32,128]{2,1,0:T(8,128)(2,1)}, bf16[20,32,128]{2,1,0:T(8,128)(2,1)S(1)}, u32[]{:S(2)}, u32[]{:S(2)}) collective-permute-start(bf16[20,32,128]{2,1,0:T(8,128)(2,1)} %get-tuple-element.17.refs_0_), channel_id=1, source_target_pairs={{0,128},{64,192},{128,256},{192,320},{256,384},{320,448},{384,0},{... | collective-permute-start | bytes 491528 | tf_op jit(solution)/shard_map/ppermute | solution.py:126
  227.7 11.4 %collective-permute-start.12 = (bf16[20,32,128]{2,1,0:T(8,128)(2,1)}, bf16[20,32,128]{2,1,0:T(8,128)(2,1)S(1)}, u32[]{:S(2)}, u32[]{:S(2)}) collective-permute-start(bf16[20,32,128]{2,1,0:T(8,128)(2,1)} %get-tuple-element.17.refs_0_), channel_id=1, source_target_pairs={{0,256},{64,320},{128,384},{192,448},{256,0},{320,64},{384,128},{4... | collective-permute-start | bytes 491528 | tf_op jit(solution)/shard_map/ppermute | solution.py:126
  232.1 9.0 %collective-permute-start.11 = (bf16[20,32,128]{2,1,0:T(8,128)(2,1)}, bf16[20,32,128]{2,1,0:T(8,128)(2,1)S(1)}, u32[]{:S(2)}, u32[]{:S(2)}) collective-permute-start(bf16[20,32,128]{2,1,0:T(8,128)(2,1)} %get-tuple-element.17.refs_0_), channel_id=1, source_target_pairs={{0,384},{64,448},{128,0},{192,64},{256,128},{320,192},{384,256},{4... | collective-permute-start | bytes 491528 | tf_op jit(solution)/shard_map/ppermute | solution.py:126
  234.8 8.7 %collective-permute-start.14 = (bf16[20,32,128]{2,1,0:T(8,128)(2,1)}, bf16[20,32,128]{2,1,0:T(8,128)(2,1)S(1)}, u32[]{:S(2)}, u32[]{:S(2)}) collective-permute-start(bf16[20,32,128]{2,1,0:T(8,128)(2,1)} %get-tuple-element.17.refs_0_), channel_id=1, source_target_pairs={{0,64},{64,0},{128,192},{192,128},{256,320},{320,256},{384,448},{4... | collective-permute-start | bytes 491528 | tf_op jit(solution)/shard_map/ppermute | solution.py:130
  236.7 7.8 %copy-start.6 = (bf16[20,32,128]{2,1,0:T(8,128)(2,1)}, bf16[20,32,128]{2,1,0:T(8,128)(2,1)S(1)}, u32[]{:S(2)}) copy-start(bf16[20,32,128]{2,1,0:T(8,128)(2,1)S(1)} %collective-permute-done.13.refs_3_) | copy-start | bytes 491524
  236.7 6.8 %collective-permute-start.17 = (bf16[20,32,128]{2,1,0:T(8,128)(2,1)S(1)}, bf16[20,32,128]{2,1,0:T(8,128)(2,1)S(1)}, u32[]{:S(2)}, u32[]{:S(2)}) collective-permute-start(bf16[20,32,128]{2,1,0:T(8,128)(2,1)S(1)} %collective-permute-done.13.refs_3_), channel_id=1, source_target_pairs={{0,64},{64,0},{128,192},{192,128},{256,320},{320,256},{384,448},{4... | collective-permute-start | bytes 491528 | tf_op jit(solution)/shard_map/ppermute | solution.py:130
  239.2 5.4 %copy-start.7 = (bf16[20,32,128]{2,1,0:T(8,128)(2,1)}, bf16[20,32,128]{2,1,0:T(8,128)(2,1)S(1)}, u32[]{:S(2)}) copy-start(bf16[20,32,128]{2,1,0:T(8,128)(2,1)S(1)} %collective-permute-done.12.refs_2_) | copy-start | bytes 491524
  239.2 4.4 %collective-permute-start.16 = (bf16[20,32,128]{2,1,0:T(8,128)(2,1)S(1)}, bf16[20,32,128]{2,1,0:T(8,128)(2,1)S(1)}, u32[]{:S(2)}, u32[]{:S(2)}) collective-permute-start(bf16[20,32,128]{2,1,0:T(8,128)(2,1)S(1)} %collective-permute-done.12.refs_2_), channel_id=1, source_target_pairs={{0,64},{64,0},{128,192},{192,128},{256,320},{320,256},{384,448},{4... | collective-permute-start | bytes 491528 | tf_op jit(solution)/shard_map/ppermute | solution.py:130
  241.1 3.4 %copy-start.9 = (bf16[20,32,128]{2,1,0:T(8,128)(2,1)}, bf16[20,32,128]{2,1,0:T(8,128)(2,1)S(1)}, u32[]{:S(2)}) copy-start(bf16[20,32,128]{2,1,0:T(8,128)(2,1)S(1)} %collective-permute-done.11.refs_1_) | copy-start | bytes 491524
  241.1 3.4 %collective-permute-start.15 = (bf16[20,32,128]{2,1,0:T(8,128)(2,1)S(1)}, bf16[20,32,128]{2,1,0:T(8,128)(2,1)S(1)}, u32[]{:S(2)}, u32[]{:S(2)}) collective-permute-start(bf16[20,32,128]{2,1,0:T(8,128)(2,1)S(1)} %collective-permute-done.11.refs_1_), channel_id=1, source_target_pairs={{0,64},{64,0},{128,192},{192,128},{256,320},{320,256},{384,448},{4... | collective-permute-start | bytes 491528 | tf_op jit(solution)/shard_map/ppermute | solution.py:130
  243.5 1.0 copy-start.10
  243.6 1.0 copy-start.12
  243.6 1.0 copy-start.13
  (5 other events, 3.4 us)

commit v3 on v1

v3 whole, which is shorter than its diff:
```python
import functools

import jax
import jax.numpy as jnp
from jax import lax
from jax.experimental import pallas as pl
from jax.experimental.pallas import tpu as pltpu
from jax.sharding import PartitionSpec as P


VMEM = pl.BlockSpec(memory_space=pltpu.VMEM)
SMEM = pl.BlockSpec(memory_space=pltpu.SMEM)
BF16 = jnp.bfloat16
F32 = jnp.float32


def pack(square):
    half = square.shape[0] // 2
    return jnp.concatenate([square[:half], square[half:]], axis=1)


def unpack(packed):
    width = packed.shape[1] // 2
    return jnp.concatenate([packed[:, :width], packed[:, width:]], axis=0)


def pack_kernel(core_ref, out_ref):
    for i in range(core_ref.shape[0]):
        out_ref[i] = pack(core_ref[i].astype(F32).T).astype(BF16)


def index_kernel(owners, groups, per_device, tile_slice_ref, slot_ref, wanted_ref, count_ref):
    dead = groups * per_device

    def clear(c, carry):
        count_ref[c] = 0
        wanted_ref[c, 0, 0] = dead
        wanted_ref[c, 0, 1] = dead
        return carry

    def place(t, carry):
        block = tile_slice_ref[t] // per_device
        owner = block % owners
        group = block // owners
        rank = count_ref[owner]
        count_ref[owner] = rank + 1
        slot_ref[t] = 2 * owner + rank
        wanted_ref[owner, 0, rank] = group * per_device + tile_slice_ref[t] % per_device
        return carry

    lax.fori_loop(0, owners, clear, 0, unroll=8)
    lax.fori_loop(0, slot_ref.shape[0], place, 0, unroll=4)


def pick_rows(ids_ref, table_ref, out_ref):
    table_ref[table_ref.shape[0] - 1] = jnp.zeros(table_ref.shape[1:], BF16)

    def step(k, carry):
        rows = [table_ref[ids_ref[4 * k + i // 2, 0, i % 2]] for i in range(8)]
        for i, row in enumerate(rows):
            out_ref[8 * k + i] = row
        return carry

    lax.fori_loop(0, out_ref.shape[0] // 8, step, 0, unroll=2)


def rotated_kernel(me_ref, ids_ref, *refs):
    pieces, out_ref, table_ref = refs[:-2], refs[-2], refs[-1]
    groups, size = len(pieces), pieces[0].shape[0]
    for i, piece in enumerate(pieces):
        core, step = divmod(i, groups // 2)
        place = lax.rem((me_ref[0] ^ core) + 2 * step, groups)
        table_ref[pl.ds(place * size, size)] = piece[...]
    pick_rows(ids_ref, table_ref, out_ref)


def sided_kernel(me_ref, ids_ref, near_ref, far_ref, out_ref, table_ref):
    size = near_ref.shape[1]
    side = lax.rem(me_ref[0], 2)
    for x in range(near_ref.shape[0]):
        table_ref[pl.ds((2 * x + side) * size, size)] = near_ref[x]
        table_ref[pl.ds((2 * x + 1 - side) * size, size)] = far_ref[x]
    pick_rows(ids_ref, table_ref, out_ref)


def grad_kernel(slot_ref, fill_ref, left_ref, right_ref, value_ref, slice_ref, out_ref, value_scr):
    value_scr[...] = value_ref[...].astype(F32)
    lanes = lax.broadcasted_iota(jnp.int32, (1, left_ref.shape[2]), 1)
    wide = 8

    def step(k, carry):
        tiles = [wide * k + i for i in range(wide)]
        slots = [slot_ref[t] for t in tiles]
        projected = [
            jnp.dot(unpack(slice_ref[slot]), left_ref[t], preferred_element_type=F32)
            for t, slot in zip(tiles, slots)
        ]
        grads = []
        for t, proj in zip(tiles, projected):
            predicted = jnp.sum(proj * right_ref[t].astype(F32), axis=0, keepdims=True)
            residual = jnp.where(
                lanes < fill_ref[t], predicted - value_scr[pl.ds(t, 1), :], 0.0
            )
            weighted = (residual * left_ref[t].astype(F32)).astype(BF16)
            grads.append(
                lax.dot_general(
                    right_ref[t],
                    weighted,
                    (((1,), (1,)), ((), ())),
                    preferred_element_type=F32,
                )
            )
        for slot, grad in zip(slots, grads):
            out_ref[slot] = pack(grad).astype(BF16)
        return carry

    lax.fori_loop(0, left_ref.shape[0] // wide, step, 0)


def sum_kernel(ids_ref, grad_ref, me_ref, near_ref, far_ref, acc_ref):
    acc_ref[...] = jnp.zeros_like(acc_ref)

    def step(c, carry):
        for r in range(2):
            acc_ref[ids_ref[c, 0, r]] += grad_ref[2 * c + r].astype(F32)
        return carry

    lax.fori_loop(0, grad_ref.shape[0] // 2, step, 0, unroll=4)
    per_device = near_ref.shape[1]
    side = lax.rem(me_ref[0], 2)
    for x in range(near_ref.shape[0]):
        near_ref[x] = acc_ref[pl.ds((2 * x + side) * per_device, per_device)]
        far_ref[x] = acc_ref[pl.ds((2 * x + 1 - side) * per_device, per_device)].astype(BF16)


def join_kernel(near_ref, other_ref, out_ref):
    out_ref[...] = (near_ref[...] + other_ref[...].astype(F32)).astype(BF16)


def update_kernel(table_ref, part_ref, packed_ref, out_ref):
    total = jnp.sum(part_ref[...].astype(F32), axis=0)
    packed = (table_ref[...].astype(F32) - total).astype(BF16)
    for x in range(packed_ref.shape[0]):
        packed_ref[x] = packed
    for i in range(out_ref.shape[0]):
        out_ref[i] = unpack(packed[i].astype(F32)).T.astype(BF16)


def refresh_kernel(slot_ref, left_ref, slice_ref, out_ref):
    wide = 8

    def step(k, carry):
        tiles = [wide * k + i for i in range(wide)]
        fresh = [
            jnp.dot(unpack(slice_ref[slot_ref[t]]), left_ref[t], preferred_element_type=F32)
            for t in tiles
        ]
        for t, value in zip(tiles, fresh):
            out_ref[t] = value.astype(BF16)
        return carry

    lax.fori_loop(0, left_ref.shape[0] // wide, step, 0)


def call(kernel, in_specs, outs, scratch=(), out_specs=None, flops=10**6, moved=4 * 10**6):
    many = isinstance(outs, tuple)
    return pl.pallas_call(
        kernel,
        out_shape=outs,
        in_specs=in_specs,
        out_specs=out_specs or ((VMEM,) * len(outs) if many else VMEM),
        scratch_shapes=list(scratch),
        cost_estimate=pl.CostEstimate(flops=flops, bytes_accessed=moved, transcendentals=0),
    )


def exchange(x, axis):
    return lax.all_to_all(x, axis, split_axis=0, concat_axis=0, tiled=True)


def shift(x, groups, step):
    return lax.ppermute(x, "grp", [(g, (g + 2 * step) % groups) for g in range(groups)])


def swap(x, groups):
    return lax.ppermute(x, "grp", [(g, g ^ 1) for g in range(groups)])


def spread(mine, groups):
    near = [mine] + [shift(mine, groups, -k) for k in range(1, groups // 2)]
    return near + [swap(piece, groups) for piece in near]


def body(left, right, values, core, tile_slice, tile_fill):
    owners = lax.axis_size("own")
    groups = lax.axis_size("grp")
    chips = groups // 2
    tiles, rows, rank = left.shape
    per_device = core.shape[0]
    local_count = groups * per_device
    slots = 2 * owners
    packed_shape = (rank // 2, 2 * rank)
    along_x = [[2 * x + side for x in range(chips)] for side in range(2)]

    left_t = jnp.swapaxes(left, 1, 2)
    right_t = jnp.swapaxes(right, 1, 2)
    sds = jax.ShapeDtypeStruct
    slot_sds = sds((slots,) + packed_shape, BF16)
    mine_sds = sds((per_device,) + packed_shape, BF16)
    chip_shape = (chips, per_device) + packed_shape
    table_scr = pltpu.VMEM((local_count + 1,) + packed_shape, BF16)

    def exchange_x(x):
        return lax.all_to_all(
            x, "grp", split_axis=0, concat_axis=0, tiled=True, axis_index_groups=along_x
        )

    me = lax.axis_index("grp").astype(jnp.int32).reshape(1)

    slot, wanted = call(
        functools.partial(index_kernel, owners, groups, per_device),
        [SMEM],
        (sds((tiles,), jnp.int32), sds((owners, 1, 128), jnp.int32)),
        [pltpu.SMEM((owners,), jnp.int32)],
        (SMEM, SMEM),
    )(tile_slice)
    ids = exchange(wanted, "own")
    mine = call(pack_kernel, [VMEM], mine_sds)(core)
    pieces = spread(mine, groups)
    outgoing = call(
        rotated_kernel, [SMEM] * 2 + [VMEM] * groups, slot_sds, [table_scr]
    )(me, ids, *pieces)
    got = exchange(outgoing, "own")
    grads = call(
        grad_kernel,
        [SMEM, SMEM, VMEM, VMEM, VMEM, VMEM],
        slot_sds,
        [pltpu.VMEM((tiles, rows), F32)],
    )(slot, tile_fill, left_t, right_t, values, got)
    got_grads = exchange(grads, "own")
    near, far = call(
        sum_kernel,
        [SMEM, VMEM, SMEM],
        (sds(chip_shape, F32), sds(chip_shape, BF16)),
        [pltpu.VMEM((local_count + 1,) + packed_shape, F32)],
    )(ids, got_grads, me)
    joined = call(join_kernel, [VMEM] * 2, sds(chip_shape, BF16))(near, swap(far, groups))
    new_spread, new_core = call(
        update_kernel, [VMEM] * 2, (sds(chip_shape, BF16), sds(core.shape, BF16))
    )(mine, exchange_x(joined))
    new_near = exchange_x(new_spread)
    new_far = swap(new_near, groups)
    outgoing = call(sided_kernel, [SMEM, SMEM, VMEM, VMEM], slot_sds, [table_scr])(
        me, ids, new_near, new_far
    )
    new_got = exchange(outgoing, "own")
    new_left_t = call(refresh_kernel, [SMEM, VMEM, VMEM], sds(left_t.shape, BF16))(
        slot, left_t, new_got
    )
    return (new_core, jnp.swapaxes(new_left_t, 1, 2))


def solution(mesh):
    spec3 = P(("grp", "own"), None, None)
    spec2 = P(("grp", "own"), None)
    spec1 = P(("grp", "own"))
    return jax.shard_map(
        body,
        mesh=mesh,
        in_specs=(spec3, spec3, spec2, spec3, spec1, spec1),
        out_specs=(spec3, spec3),
        check_vma=False,
    )
```

time: 318 us -> 306 us (0.962)
  starting transfers between devices: 23 us -> 42.6 us
  blocking collectives: 227 us -> 212 us
  waiting for transfers between devices: 28.7 us -> 18.1 us
  local copies, waits for them, and re-layouts: 6.32 us -> 2.46 us
    all_to_all x5 -> x3, blocking collectives: 227 us -> 182 us  [exchange(): return lax.all_to_all(x, axis, split_axis=0, concat_axis=0, tiled=True)]
    all_to_all x0 -> x2, blocking collectives: none -> 29.7 us  [exchange_x(): lax.all_to_all(x, 'grp', split_axis=0, concat_axis=0, tiled=True, axis_in...]
    ppermute x0 -> x9, starting transfers between devices: none -> 23.8 us  [the longest x6 12.5 us: swap(): return lax.ppermute(x, 'grp', [(g, g ^ 1) for g in range(groups)])]
    all_to_all x2 -> x1, waiting for transfers between devices: 28.7 us -> 13.7 us  [exchange(): return lax.all_to_all(x, axis, split_axis=0, concat_axis=0, tiled=True)]
    pallas_call x5 -> x7, Pallas kernels: 13.7 us -> 18.3 us  [the longest x1 3.39 us: body(): call(sum_kernel, [SMEM, VMEM, SMEM], (sds(chip_shape, F32), sds(chip_shap...]
    ppermute x0 -> x9, waiting for transfers between devices: none -> 4.36 us  [the longest x6 4.35 us: swap(): return lax.ppermute(x, 'grp', [(g, g ^ 1) for g in range(groups)])]
    all_to_all x2 -> x1, starting transfers between devices: 23 us -> 18.7 us  [exchange(): return lax.all_to_all(x, axis, split_axis=0, concat_axis=0, tiled=True)]
    pallas_call x1, Pallas kernels: 10.3 us -> 6.79 us  [body(): call(grad_kernel, [SMEM, SMEM, VMEM, VMEM, VMEM, VMEM], slot_sds, [pltpu....]
  transfers between devices with their start and end apart: 2 -> 10, of which waited for: 2 -> 3; matrix products, arithmetic and copies ran while one was open for 1% -> 0% of each run, Pallas kernels for 1% -> 1%
where the time goes in v3:
time: 306 us; the launch traced here: 305 us
  blocking collectives  212 us (69%)
  starting transfers between devices  42.6 us (14%)
  Pallas kernels  29.5 us (10%)
  waiting for transfers between devices  18.1 us (6%)
    all_to_all x3, blocking collectives, exchange(): return lax.all_to_all(x, axis, split_axis=0, concat_axis=0, tiled=True)  182 us
    all_to_all x2, blocking collectives, exchange_x(): lax.all_to_all(x, 'grp', split_axis=0, concat_axis=0, tiled=True, axis_in...  29.7 us
    all_to_all x1, starting transfers between devices, exchange(): return lax.all_to_all(x, axis, split_axis=0, concat_axis=0, tiled=True)  18.7 us
    all_to_all x1, waiting for transfers between devices, exchange(): return lax.all_to_all(x, axis, split_axis=0, concat_axis=0, tiled=True)  13.7 us
    ppermute x6, starting transfers between devices, swap(): return lax.ppermute(x, 'grp', [(g, g ^ 1) for g in range(groups)])  12.5 us
    ppermute x3, starting transfers between devices, shift(): lax.ppermute(x, 'grp', [(g, (g + 2 * step) % groups) for g in range(group...  11.4 us
    pallas_call x1, Pallas kernels, body(): call(grad_kernel, [SMEM, SMEM, VMEM, VMEM, VMEM, VMEM], slot_sds, [pltpu....  6.79 us
  transfers between devices with their start and end apart: 10, of which 3 were waited for; matrix products, arithmetic and copies ran while one was open for 0% of the time, Pallas kernels for 1%

profile of v3, /device:TPU:8, one launch (start us, length us, event | category | flops | bytes accessed | tf_op | source)
XLA Modules:
  0.0 305.5 jit_solution(2761805297686592867)
XLA Ops:
  0.6 1.9 shard_map.77.refs_0_.table_ref
  2.5 3.4 %collective-permute-start.2 = (bf16[20,32,128]{2,1,0:T(8,128)(2,1)}, bf16[20,32,128]{2,1,0:T(8,128)(2,1)S(1)}, u32[]{:S(2)}, u32[]{:S(2)}) collective-permute-start(bf16[20,32,128]{2,1,0:T(8,128)(2,1)} %shard_map.77.refs_0_.table_ref), channel_id=1, source_target_pairs={{0,128},{64,192},{128,256},{192,320},{256,384},{320,448},{384,0},{... | collective-permute-start | bytes 491528 | tf_op jit(solution)/shard_map/ppermute | solution.py:182
  5.9 4.6 %collective-permute-start.1 = (bf16[20,32,128]{2,1,0:T(8,128)(2,1)}, bf16[20,32,128]{2,1,0:T(8,128)(2,1)S(1)}, u32[]{:S(2)}, u32[]{:S(2)}) collective-permute-start(bf16[20,32,128]{2,1,0:T(8,128)(2,1)} %shard_map.77.refs_0_.table_ref), channel_id=1, source_target_pairs={{0,256},{64,320},{128,384},{192,448},{256,0},{320,64},{384,128},{4... | collective-permute-start | bytes 491528 | tf_op jit(solution)/shard_map/ppermute | solution.py:182
  10.5 3.3 %collective-permute-start = (bf16[20,32,128]{2,1,0:T(8,128)(2,1)}, bf16[20,32,128]{2,1,0:T(8,128)(2,1)S(1)}, u32[]{:S(2)}, u32[]{:S(2)}) collective-permute-start(bf16[20,32,128]{2,1,0:T(8,128)(2,1)} %shard_map.77.refs_0_.table_ref), channel_id=1, source_target_pairs={{0,384},{64,448},{128,0},{192,64},{256,128},{320,192},{384,256},{4... | collective-permute-start | bytes 491528 | tf_op jit(solution)/shard_map/ppermute | solution.py:182
  13.9 1.9 collective-permute-start.3
  15.8 2.4 collective-permute-start.6
  18.3 1.9 collective-permute-start.5
  20.2 2.4 collective-permute-start.4
  22.6 3.1 %shard_map.78 = (s32[64]{0:T(128)}, s32[64,1,128]{2,1,0:T(1,128)}) custom-call(s32[64]{0:T(128)} %tile_slice_ref.1), custom_call_target="tpu_custom_call" | custom-call | flops 1000000 | bytes 4000000 | tf_op jit(solution)/shard_map/pallas_call | solution.py:220
  25.8 18.7 %all-to-all-start = ((s32[64,1,128]{2,1,0:T(1,128)}), s32[64,1,128]{2,1,0:T(1,128)S(1)}, u32[]{:S(2)}, u32[]{:S(2)}) async-start(s32[64,1,128]{2,1,0:T(1,128)} %get-tuple-element.8), calls=%async_computation | async-start | bytes 65536 | tf_op jit(solution)/shard_map/all_to_all | solution.py:178
  44.5 13.7 %all-to-all-done.ids_ref = s32[64,1,128]{2,1,0:T(1,128)S(1)} async-done(((s32[64,1,128]{2,1,0:T(1,128)}), s32[64,1,128]{2,1,0:T(1,128)S(1)}, u32[]{:S(2)}, u32[]{:S(2)}) %all-to-all-start) | async-done | bytes 32800 | tf_op jit(solution)/shard_map/all_to_all | solution.py:178
  58.3 0.5 copy-done.3
  58.9 0.1 copy-done.7
  59.0 0.1 copy-done.9
  59.1 2.6 shard_map.79
  61.7 60.4 %all_to_all.30.slice_ref = bf16[128,32,128]{2,1,0:T(8,128)(2,1)} all-to-all(bf16[128,32,128]{2,1,0:T(8,128)(2,1)} %shard_map.79), channel_id=1, replica_groups=mesh['grp'=8,'own'=64] {'own'}, dimensions={0} | all-to-all | bytes 2097152 | tf_op jit(solution)/shard_map/all_to_all | solution.py:178
  122.2 6.8 %shard_map.80 = bf16[128,32,128]{2,1,0:T(8,128)(2,1)} custom-call(s32[64]{0:T(128)} %get-tuple-element.9.slot_ref, s32[64]{0:T(128)} %fill_ref.1, bf16[64,64,128]{2,1,0:T(8,128)(2,1)} %bitcast.4, bf16[64,64,128]{2,1,0:T(8,128)(2,1)} %bitcast.6, bf16[64,128]{1,0:T(8,128)(2,1)} %value_ref.1, bf16[128,32,128]{2,1,0:T(8,128)(2,1)} %all_to_all.30.slice_ref), custom_call_target="tpu_custom_call" | custom-call | flops 1000000 | bytes 4000000 | tf_op jit(solution)/shard_map/pallas_call | solution.py:234
  129.0 60.3 %all_to_all.31.grad_ref = bf16[128,32,128]{2,1,0:T(8,128)(2,1)} all-to-all(bf16[128,32,128]{2,1,0:T(8,128)(2,1)} %shard_map.80), channel_id=1, replica_groups=mesh['grp'=8,'own'=64] {'own'}, dimensions={0} | all-to-all | bytes 2097152 | tf_op jit(solution)/shard_map/all_to_all | solution.py:178
  189.3 3.4 %shard_map.81 = (f32[4,20,32,128]{3,2,1,0:T(8,128)}, bf16[4,20,32,128]{3,2,1,0:T(8,128)(2,1)}) custom-call(s32[64,1,128]{2,1,0:T(1,128)} %copy-done.3, bf16[128,32,128]{2,1,0:T(8,128)(2,1)} %all_to_all.31.grad_ref, s32[1]{0:T(128)} %bitcast.2.me_ref), custom_call_target="tpu_custom_call" | custom-call | flops 1000000 | bytes 4000000 | tf_op jit(solution)/shard_map/pallas_call | solution.py:241
  192.6 1.9 collective-permute-start.7
  194.6 2.3 collective-permute-done.7.other_ref
  196.8 0.8 copy-done.1
  197.7 2.5 shard_map.82
  200.1 15.7 %all_to_all.32.part_ref = bf16[4,20,32,128]{3,2,1,0:T(8,128)(2,1)} all-to-all(bf16[4,20,32,128]{3,2,1,0:T(8,128)(2,1)} %shard_map.82), channel_id=1, replica_groups={{0,128,256,384},{64,192,320,448},{1,129,257,385},{65,193,321,449},{2,13..., dimensions={0} | all-to-all | bytes 1310720 | tf_op jit(solution)/shard_map/all_to_all | solution.py:214
  215.8 2.3 shard_map.83
  218.2 14.1 %all_to_all.33.near_ref = bf16[4,20,32,128]{3,2,1,0:T(8,128)(2,1)S(1)} all-to-all(bf16[4,20,32,128]{3,2,1,0:T(8,128)(2,1)} %get-tuple-element.13), channel_id=1, replica_groups={{0,128,256,384},{64,192,320,448},{1,129,257,385},{65,193,321,449},{2,13..., dimensions={0} | all-to-all | bytes 1310720 | tf_op jit(solution)/shard_map/all_to_all | solution.py:214
  232.2 1.9 collective-permute-start.8
  234.1 2.1 collective-permute-done.8.far_ref
  236.2 0.8 copy-done.2
  237.1 2.5 shard_map.84
  239.6 61.6 %all_to_all.34.slice_ref = bf16[128,32,128]{2,1,0:T(8,128)(2,1)} all-to-all(bf16[128,32,128]{2,1,0:T(8,128)(2,1)} %shard_map.84), channel_id=1, replica_groups=mesh['grp'=8,'own'=64] {'own'}, dimensions={0} | all-to-all | bytes 2097152 | tf_op jit(solution)/shard_map/all_to_all | solution.py:178
  301.1 4.3 %shard_map.85 = bf16[64,64,128]{2,1,0:T(8,128)(2,1)} custom-call(s32[64]{0:T(128)} %get-tuple-element.9.slot_ref, bf16[64,64,128]{2,1,0:T(8,128)(2,1)} %bitcast.5, bf16[128,32,128]{2,1,0:T(8,128)(2,1)} %all_to_all.34.slice_ref), custom_call_target="tpu_custom_call" | custom-call | flops 1000000 | bytes 4000000 | tf_op jit(solution)/shard_map/pallas_call | solution.py:257
  (24 shorter events, 0.1 us)
Async XLA Ops:
  2.5 13.3 %collective-permute-start.2 = (bf16[20,32,128]{2,1,0:T(8,128)(2,1)}, bf16[20,32,128]{2,1,0:T(8,128)(2,1)S(1)}, u32[]{:S(2)}, u32[]{:S(2)}) collective-permute-start(bf16[20,32,128]{2,1,0:T(8,128)(2,1)} %shard_map.77.refs_0_.table_ref), channel_id=1, source_target_pairs={{0,128},{64,192},{128,256},{192,320},{256,384},{320,448},{384,0},{... | collective-permute-start | bytes 491528 | tf_op jit(solution)/shard_map/ppermute | solution.py:182
  5.9 12.4 %collective-permute-start.1 = (bf16[20,32,128]{2,1,0:T(8,128)(2,1)}, bf16[20,32,128]{2,1,0:T(8,128)(2,1)S(1)}, u32[]{:S(2)}, u32[]{:S(2)}) collective-permute-start(bf16[20,32,128]{2,1,0:T(8,128)(2,1)} %shard_map.77.refs_0_.table_ref), channel_id=1, source_target_pairs={{0,256},{64,320},{128,384},{192,448},{256,0},{320,64},{384,128},{4... | collective-permute-start | bytes 491528 | tf_op jit(solution)/shard_map/ppermute | solution.py:182
  10.5 9.7 %collective-permute-start = (bf16[20,32,128]{2,1,0:T(8,128)(2,1)}, bf16[20,32,128]{2,1,0:T(8,128)(2,1)S(1)}, u32[]{:S(2)}, u32[]{:S(2)}) collective-permute-start(bf16[20,32,128]{2,1,0:T(8,128)(2,1)} %shard_map.77.refs_0_.table_ref), channel_id=1, source_target_pairs={{0,384},{64,448},{128,0},{192,64},{256,128},{320,192},{384,256},{4... | collective-permute-start | bytes 491528 | tf_op jit(solution)/shard_map/ppermute | solution.py:182
  13.9 44.4 %collective-permute-start.3 = (bf16[20,32,128]{2,1,0:T(8,128)(2,1)}, bf16[20,32,128]{2,1,0:T(8,128)(2,1)S(1)}, u32[]{:S(2)}, u32[]{:S(2)}) collective-permute-start(bf16[20,32,128]{2,1,0:T(8,128)(2,1)} %shard_map.77.refs_0_.table_ref), channel_id=1, source_target_pairs={{0,64},{64,0},{128,192},{192,128},{256,320},{320,256},{384,448},{4... | collective-permute-start | bytes 491528 | tf_op jit(solution)/shard_map/ppermute | solution.py:186
  15.8 42.5 %copy-start.4 = (bf16[20,32,128]{2,1,0:T(8,128)(2,1)}, bf16[20,32,128]{2,1,0:T(8,128)(2,1)S(1)}, u32[]{:S(2)}) copy-start(bf16[20,32,128]{2,1,0:T(8,128)(2,1)S(1)} %collective-permute-done.2.refs_3_) | copy-start | bytes 491524
  15.8 42.4 %collective-permute-start.6 = (bf16[20,32,128]{2,1,0:T(8,128)(2,1)S(1)}, bf16[20,32,128]{2,1,0:T(8,128)(2,1)S(1)}, u32[]{:S(2)}, u32[]{:S(2)}) collective-permute-start(bf16[20,32,128]{2,1,0:T(8,128)(2,1)S(1)} %collective-permute-done.2.refs_3_), channel_id=1, source_target_pairs={{0,64},{64,0},{128,192},{192,128},{256,320},{320,256},{384,448},{4... | collective-permute-start | bytes 491528 | tf_op jit(solution)/shard_map/ppermute | solution.py:186
  18.3 40.1 %copy-start.5 = (bf16[20,32,128]{2,1,0:T(8,128)(2,1)}, bf16[20,32,128]{2,1,0:T(8,128)(2,1)S(1)}, u32[]{:S(2)}) copy-start(bf16[20,32,128]{2,1,0:T(8,128)(2,1)S(1)} %collective-permute-done.1.refs_2_) | copy-start | bytes 491524
  18.3 40.0 %collective-permute-start.5 = (bf16[20,32,128]{2,1,0:T(8,128)(2,1)S(1)}, bf16[20,32,128]{2,1,0:T(8,128)(2,1)S(1)}, u32[]{:S(2)}, u32[]{:S(2)}) collective-permute-start(bf16[20,32,128]{2,1,0:T(8,128)(2,1)S(1)} %collective-permute-done.1.refs_2_), channel_id=1, source_target_pairs={{0,64},{64,0},{128,192},{192,128},{256,320},{320,256},{384,448},{4... | collective-permute-start | bytes 491528 | tf_op jit(solution)/shard_map/ppermute | solution.py:186
  20.2 38.1 %copy-start.6 = (bf16[20,32,128]{2,1,0:T(8,128)(2,1)}, bf16[20,32,128]{2,1,0:T(8,128)(2,1)S(1)}, u32[]{:S(2)}) copy-start(bf16[20,32,128]{2,1,0:T(8,128)(2,1)S(1)} %collective-permute-done.refs_1_) | copy-start | bytes 491524
  20.2 38.1 %collective-permute-start.4 = (bf16[20,32,128]{2,1,0:T(8,128)(2,1)S(1)}, bf16[20,32,128]{2,1,0:T(8,128)(2,1)S(1)}, u32[]{:S(2)}, u32[]{:S(2)}) collective-permute-start(bf16[20,32,128]{2,1,0:T(8,128)(2,1)S(1)} %collective-permute-done.refs_1_), channel_id=1, source_target_pairs={{0,64},{64,0},{128,192},{192,128},{256,320},{320,256},{384,448},{4... | collective-permute-start | bytes 491528 | tf_op jit(solution)/shard_map/ppermute | solution.py:186
  25.8 32.5 %all-to-all-start = ((s32[64,1,128]{2,1,0:T(1,128)}), s32[64,1,128]{2,1,0:T(1,128)S(1)}, u32[]{:S(2)}, u32[]{:S(2)}) async-start(s32[64,1,128]{2,1,0:T(1,128)} %get-tuple-element.8), calls=%async_computation | async-start | bytes 65536 | tf_op jit(solution)/shard_map/all_to_all | solution.py:178
  58.3 0.6 copy-start.3
  58.3 0.7 copy-start.7
  58.3 0.7 copy-start.8
  58.3 0.8 copy-start.9
  58.3 0.8 copy-start.10
  192.6 4.2 %collective-permute-start.7 = (bf16[4,20,32,128]{3,2,1,0:T(8,128)(2,1)}, bf16[4,20,32,128]{3,2,1,0:T(8,128)(2,1)S(1)}, u32[]{:S(2)}, u32[]{:S(2)}) collective-permute-start(bf16[4,20,32,128]{3,2,1,0:T(8,128)(2,1)} %get-tuple-element.11), channel_id=1, source_target_pairs={{0,64},{64,0},{128,192},{192,128},{256,320},{320,256},{384,448},{4... | collective-permute-start | bytes 1966088 | tf_op jit(solution)/shard_map/ppermute | solution.py:186
  196.8 0.8 copy-start.1
  232.2 4.0 %copy-start = (bf16[4,20,32,128]{3,2,1,0:T(8,128)(2,1)}, bf16[4,20,32,128]{3,2,1,0:T(8,128)(2,1)S(1)}, u32[]{:S(2)}) copy-start(bf16[4,20,32,128]{3,2,1,0:T(8,128)(2,1)S(1)} %all_to_all.33.near_ref) | copy-start | bytes 1966084
  232.2 4.0 %collective-permute-start.8 = (bf16[4,20,32,128]{3,2,1,0:T(8,128)(2,1)S(1)}, bf16[4,20,32,128]{3,2,1,0:T(8,128)(2,1)S(1)}, u32[]{:S(2)}, u32[]{:S(2)}) collective-permute-start(bf16[4,20,32,128]{3,2,1,0:T(8,128)(2,1)S(1)} %all_to_all.33.near_ref), channel_id=1, source_target_pairs={{0,64},{64,0},{128,192},{192,128},{256,320},{320,256},{384,448},{4... | collective-permute-start | bytes 1966088 | tf_op jit(solution)/shard_map/ppermute | solution.py:186
  236.2 0.9 copy-start.2

commit v4 on v3

v4 whole, which is shorter than its diff:
```python
import functools

import jax
import jax.numpy as jnp
from jax import lax
from jax.experimental import pallas as pl
from jax.experimental.pallas import tpu as pltpu
from jax.sharding import PartitionSpec as P


VMEM = pl.BlockSpec(memory_space=pltpu.VMEM)
SMEM = pl.BlockSpec(memory_space=pltpu.SMEM)
BF16 = jnp.bfloat16
F32 = jnp.float32
WIDE = 8


def pack(block):
    half = block.shape[0] // 2
    return jnp.concatenate([block[:half], block[half:]], axis=1)


def unpack(packed):
    width = packed.shape[1] // 2
    return jnp.concatenate([packed[:, :width], packed[:, width:]], axis=0)


def pack_both(square):
    half = square.shape[0] // 2
    return jnp.concatenate([pack(square[:half]), pack(square[half:])], axis=0)


def unpack_both(packed):
    half = packed.shape[0] // 2
    return jnp.concatenate([unpack(packed[:half]), unpack(packed[half:])], axis=0)


def index_kernel(owners, groups, per_device, tile_slice_ref, slot_ref, wanted_ref, count_ref):
    dead = groups * per_device

    def clear(c, carry):
        count_ref[c] = 0
        wanted_ref[c, 0, 0] = dead
        wanted_ref[c, 0, 1] = dead
        return carry

    def place(t, carry):
        block = lax.div(tile_slice_ref[t], per_device)
        owner = lax.rem(block, owners)
        group = lax.div(block, owners)
        rank = count_ref[owner]
        count_ref[owner] = rank + 1
        slot_ref[t] = 2 * owner + rank
        wanted_ref[owner, 0, rank] = group * per_device + tile_slice_ref[t] - block * per_device
        return carry

    lax.fori_loop(0, owners, clear, 0, unroll=8)
    lax.fori_loop(0, slot_ref.shape[0], place, 0, unroll=8)


def pack_kernel(me_ref, core_ref, other_ref, out_ref):
    size = core_ref.shape[0]
    side = lax.rem(me_ref[0], 2)
    for i in range(size):
        out_ref[side * size + i] = pack_both(core_ref[i].astype(F32).T).astype(BF16)
        out_ref[(1 - side) * size + i] = pack_both(other_ref[i].astype(F32).T).astype(BF16)


def pick_kernel(me_ref, ids_ref, *refs):
    pieces, out_ref, table_ref = refs[:-2], refs[-2], refs[-1]
    chips, size = len(pieces), pieces[0].shape[0]
    for k, piece in enumerate(pieces):
        place = lax.rem(lax.div(me_ref[0], 2) + k, chips)
        table_ref[pl.ds(place * size, size)] = piece[...]
    table_ref[chips * size] = jnp.zeros(table_ref.shape[1:], BF16)

    def step(k, carry):
        rows = [table_ref[ids_ref[4 * k + i // 2, 0, i % 2]] for i in range(8)]
        for i, row in enumerate(rows):
            out_ref[8 * k + i] = row
        return carry

    lax.fori_loop(0, out_ref.shape[0] // 8, step, 0, unroll=2)


def gradient_half(half, right, left, residual):
    weighted = (residual * left.astype(F32)).astype(BF16)
    rows = right.shape[0] // 2
    return lax.dot_general(
        right[half * rows : (half + 1) * rows],
        weighted,
        (((1,), (1,)), ((), ())),
        preferred_element_type=F32,
    )


def first_kernel(slot_ref, fill_ref, left_ref, right_ref, value_ref, slice_ref, out_ref, res_ref, value_scr):
    value_scr[...] = value_ref[...].astype(F32)
    lanes = lax.broadcasted_iota(jnp.int32, (1, left_ref.shape[2]), 1)

    def step(k, carry):
        tiles = [WIDE * k + i for i in range(WIDE)]
        slots = [slot_ref[t] for t in tiles]
        projected = [
            jnp.dot(unpack_both(slice_ref[slot]), left_ref[t], preferred_element_type=F32)
            for t, slot in zip(tiles, slots)
        ]
        grads = []
        for t, proj in zip(tiles, projected):
            predicted = jnp.sum(proj * right_ref[t].astype(F32), axis=0, keepdims=True)
            residual = jnp.where(
                lanes < fill_ref[t], predicted - value_scr[pl.ds(t, 1), :], 0.0
            )
            res_ref[pl.ds(t, 1), :] = residual
            grads.append(gradient_half(0, right_ref[t], left_ref[t], residual))
        for slot, grad in zip(slots, grads):
            out_ref[slot] = pack(grad).astype(BF16)
        return carry

    lax.fori_loop(0, left_ref.shape[0] // WIDE, step, 0)


def other_kernel(slot_ref, left_ref, right_ref, res_ref, out_ref):
    def step(k, carry):
        tiles = [WIDE * k + i for i in range(WIDE)]
        grads = [
            gradient_half(1, right_ref[t], left_ref[t], res_ref[pl.ds(t, 1), :]) for t in tiles
        ]
        for t, grad in zip(tiles, grads):
            out_ref[slot_ref[t]] = pack(grad).astype(BF16)
        return carry

    lax.fori_loop(0, left_ref.shape[0] // WIDE, step, 0)


def sum_kernel(chips, me_ref, ids_ref, grad_ref, out_ref, acc_ref):
    acc_ref[...] = jnp.zeros_like(acc_ref)

    def step(c, carry):
        for r in range(2):
            acc_ref[ids_ref[c, 0, r]] += grad_ref[2 * c + r].astype(F32)
        return carry

    lax.fori_loop(0, grad_ref.shape[0] // 2, step, 0, unroll=4)
    size = out_ref.shape[0] // chips
    for k in range(chips):
        place = lax.rem(lax.div(me_ref[0], 2) + k, chips)
        out_ref[pl.ds(k * size, size)] = acc_ref[pl.ds(place * size, size)].astype(BF16)


def join_kernel(part_ref, other_ref, keep_ref, *send_refs):
    size = keep_ref.shape[0]
    keep_ref[...] = part_ref[:size].astype(F32) + other_ref[:size].astype(F32)
    for i, send_ref in enumerate(send_refs):
        rows = pl.ds((i + 1) * size, size)
        send_ref[...] = (part_ref[rows].astype(F32) + other_ref[rows].astype(F32)).astype(BF16)


def update_kernel(half, table_ref, keep_ref, *refs):
    parts, new_ref = refs[:-1], refs[-1]
    rows = new_ref.shape[1]
    total = keep_ref[...]
    for part in parts:
        total += part[...].astype(F32)
    table = table_ref[:, half * rows : (half + 1) * rows, :]
    new_ref[...] = (table.astype(F32) - total).astype(BF16)


def core_kernel(me_ref, new_a_ref, new_b_ref, out_ref):
    size = out_ref.shape[0]
    side = lax.rem(me_ref[0], 2)
    for i in range(size):
        packed = jnp.concatenate([new_a_ref[side * size + i], new_b_ref[side * size + i]], axis=0)
        out_ref[i] = unpack_both(packed.astype(F32)).T.astype(BF16)


def refresh_kernel(slot_ref, left_ref, slice_ref, *refs):
    out_ref = refs[-1]

    def step(k, carry):
        tiles = [WIDE * k + i for i in range(WIDE)]
        fresh = [
            jnp.dot(unpack(slice_ref[slot_ref[t]]), left_ref[t], preferred_element_type=F32)
            for t in tiles
        ]
        for t, value in zip(tiles, fresh):
            out_ref[t] = value.astype(BF16)
        return carry

    lax.fori_loop(0, left_ref.shape[0] // WIDE, step, 0)


def call(kernel, in_specs, outs, scratch=(), out_specs=None):
    many = isinstance(outs, tuple)
    return pl.pallas_call(
        kernel,
        out_shape=outs,
        in_specs=in_specs,
        out_specs=out_specs or ((VMEM,) * len(outs) if many else VMEM),
        scratch_shapes=list(scratch),
        cost_estimate=pl.CostEstimate(flops=10**6, bytes_accessed=4 * 10**6, transcendentals=0),
    )


def refresh(half, slot, left_t, slices, prior=None):
    tiles, rank, rows = left_t.shape
    specs = [SMEM, VMEM, VMEM] + ([] if prior is None else [pl.BlockSpec(memory_space=pl.ANY)])
    args = (slot, left_t, slices) + (() if prior is None else (prior,))
    return pl.pallas_call(
        refresh_kernel,
        grid=(1,),
        out_shape=jax.ShapeDtypeStruct(left_t.shape, BF16),
        in_specs=specs,
        out_specs=pl.BlockSpec((tiles, rank // 2, rows), lambda i: (0, half, 0)),
        input_output_aliases={} if prior is None else {3: 0},
        cost_estimate=pl.CostEstimate(flops=10**6, bytes_accessed=3 * 10**6, transcendentals=0),
    )(*args)


def exchange(x):
    return lax.all_to_all(x, "own", split_axis=0, concat_axis=0, tiled=True)


def shift(x, groups, step):
    return lax.ppermute(x, "grp", [(g, (g + 2 * step) % groups) for g in range(groups)])


def swap(x, groups):
    return lax.ppermute(x, "grp", [(g, g ^ 1) for g in range(groups)])


def spread(block, groups):
    return [block] + [shift(block, groups, -k) for k in range(1, groups // 2)]


def body(left, right, values, core, tile_slice, tile_fill):
    owners = lax.axis_size("own")
    groups = lax.axis_size("grp")
    chips = groups // 2
    tiles, rows, rank = left.shape
    per_device = core.shape[0]
    local_count = groups * per_device
    slots = 2 * owners
    sds = jax.ShapeDtypeStruct
    half_shape = (rank // 4, 2 * rank)
    full_shape = (rank // 2, 2 * rank)
    half_slots = sds((slots,) + half_shape, BF16)
    half_scr = pltpu.VMEM((local_count + 1,) + half_shape, BF16)
    full_scr = pltpu.VMEM((local_count + 1,) + full_shape, BF16)
    sum_scr = pltpu.VMEM((local_count + 1,) + half_shape, F32)
    block_sds = sds((2 * per_device,) + half_shape, BF16)
    keep_sds = sds((2 * per_device,) + half_shape, F32)
    pick_specs = [SMEM] * 2 + [VMEM] * chips

    left_t = jnp.swapaxes(left, 1, 2)
    right_t = jnp.swapaxes(right, 1, 2)
    me = lax.axis_index("grp").astype(jnp.int32).reshape(1)

    def chain(half, ids, table, got):
        part = call(
            functools.partial(sum_kernel, chips),
            [SMEM, SMEM, VMEM],
            sds((local_count,) + half_shape, BF16),
            [sum_scr],
        )(me, ids, got)
        keep, *send = call(join_kernel, [VMEM] * 2, (keep_sds,) + (block_sds,) * (chips - 1))(
            part, swap(part, groups)
        )
        parts = [shift(x, groups, k + 1) for k, x in enumerate(send)]
        new = call(
            functools.partial(update_kernel, half), [VMEM] * (chips + 1), block_sds
        )(table, keep, *parts)
        pieces = spread(new, groups)
        return new, call(pick_kernel, pick_specs, half_slots, [half_scr])(me, ids, *pieces)

    slot, wanted = call(
        functools.partial(index_kernel, owners, groups, per_device),
        [SMEM],
        (sds((tiles,), jnp.int32), sds((owners, 1, 128), jnp.int32)),
        [pltpu.SMEM((owners,), jnp.int32)],
        (SMEM, SMEM),
    )(tile_slice)
    other_core = swap(core, groups)
    ids = exchange(wanted)
    table = call(
        pack_kernel, [SMEM, VMEM, VMEM], sds((2 * per_device,) + full_shape, BF16)
    )(me, core, other_core)
    pieces = spread(table, groups)
    outgoing = call(pick_kernel, pick_specs, sds((slots,) + full_shape, BF16), [full_scr])(
        me, ids, *pieces
    )
    got = exchange(outgoing)
    grad_a, residual = call(
        first_kernel,
        [SMEM] * 2 + [VMEM] * 4,
        (half_slots, sds((tiles, rows), F32)),
        [pltpu.VMEM((tiles, rows), F32)],
    )(slot, tile_fill, left_t, right_t, values, got)
    got_a = exchange(grad_a)
    grad_b = call(other_kernel, [SMEM] + [VMEM] * 3, half_slots)(slot, left_t, right_t, residual)
    got_b = exchange(grad_b)
    new_a, out_a = chain(0, ids, table, got_a)
    slices_a = exchange(out_a)
    new_b, out_b = chain(1, ids, table, got_b)
    slices_b = exchange(out_b)
    new_left_t = refresh(0, slot, left_t, slices_a)
    new_core = call(core_kernel, [SMEM, VMEM, VMEM], sds(core.shape, BF16))(me, new_a, new_b)
    new_left_t = refresh(1, slot, left_t, slices_b, new_left_t)
    return (new_core, jnp.swapaxes(new_left_t, 1, 2))


def solution(mesh):
    spec3 = P(("grp", "own"), None, None)
    spec2 = P(("grp", "own"), None)
    spec1 = P(("grp", "own"))
    return jax.shard_map(
        body,
        mesh=mesh,
        in_specs=(spec3, spec3, spec2, spec3, spec1, spec1),
        out_specs=(spec3, spec3),
        check_vma=False,
    )
```

time: 306 us -> 334 us (1.092)
  blocking collectives: 212 us -> 92.2 us
  waiting for transfers between devices: 18.1 us -> 86.2 us
  starting transfers between devices: 42.6 us -> 96.7 us
  Pallas kernels: 29.5 us -> 46.6 us
  local copies, waits for them, and re-layouts: 2.46 us -> 9.83 us
    all_to_all x5 -> x2, blocking collectives: 212 us -> 92.2 us  [exchange(): return lax.all_to_all(x, 'own', split_axis=0, concat_axis=0, tiled=True)]
    all_to_all x1 -> x4, waiting for transfers between devices: 13.7 us -> 52.8 us  [exchange(): return lax.all_to_all(x, 'own', split_axis=0, concat_axis=0, tiled=True)]
    ppermute x3 -> x15, starting transfers between devices: 11.4 us -> 48.8 us  [shift(): lax.ppermute(x, 'grp', [(g, (g + 2 * step) % groups) for g in range(group...]
    ppermute x3 -> x15, waiting for transfers between devices: 0.01 us -> 27.1 us  [shift(): lax.ppermute(x, 'grp', [(g, (g + 2 * step) % groups) for g in range(group...]
    all_to_all x1 -> x4, starting transfers between devices: 18.7 us -> 42.1 us  [exchange(): return lax.all_to_all(x, 'own', split_axis=0, concat_axis=0, tiled=True)]
    pallas_call x8 -> x15, Pallas kernels: 26.4 us -> 44 us  [the longest x2 7.86 us: refresh(): pl.pallas_call(refresh_kernel, grid=(1,), out_shape=jax.ShapeDtypeStruct(...]
    unnamed x22 -> x44, local copies, waits for them, and re-layouts: 2.46 us -> 9.83 us
    ppermute x6 -> x3, starting transfers between devices: 12.5 us -> 5.74 us  [swap(): return lax.ppermute(x, 'grp', [(g, g ^ 1) for g in range(groups)])]
  transfers between devices with their start and end apart: 10 -> 22, of which waited for: 3 -> 15; matrix products, arithmetic and copies ran while one was open for 0% -> 0% of each run, Pallas kernels for 1% -> 9%
where the time goes in v4:
time: 334 us; the launch traced here: 332 us
  starting transfers between devices  96.7 us (29%)
  blocking collectives  92.2 us (28%)
  waiting for transfers between devices  86.2 us (26%)
  Pallas kernels  46.6 us (14%)
  local copies, waits for them, and re-layouts  9.83 us (3%)
    all_to_all x2, blocking collectives, exchange(): return lax.all_to_all(x, 'own', split_axis=0, concat_axis=0, tiled=True)  92.2 us
    all_to_all x4, waiting for transfers between devices, exchange(): return lax.all_to_all(x, 'own', split_axis=0, concat_axis=0, tiled=True)  52.8 us
    ppermute x15, starting transfers between devices, shift(): lax.ppermute(x, 'grp', [(g, (g + 2 * step) % groups) for g in range(group...  48.8 us
    all_to_all x4, starting transfers between devices, exchange(): return lax.all_to_all(x, 'own', split_axis=0, concat_axis=0, tiled=True)  42.1 us
    ppermute x15, waiting for transfers between devices, shift(): lax.ppermute(x, 'grp', [(g, (g + 2 * step) % groups) for g in range(group...  27.1 us
    unnamed x44, local copies, waits for them, and re-layouts  9.83 us
    pallas_call x2, Pallas kernels, refresh(): pl.pallas_call(refresh_kernel, grid=(1,), out_shape=jax.ShapeDtypeStruct(...  7.86 us
  transfers between devices with their start and end apart: 22, of which 15 were waited for; matrix products, arithmetic and copies ran while one was open for 0% of the time, Pallas kernels for 9%

profile of v4, /device:TPU:8, one launch (start us, length us, event | category | flops | bytes accessed | tf_op | source)
XLA Modules:
  0.0 332.3 jit_solution(18009797458736761930)
XLA Ops:
  7.2 4.7 %collective-permute-start.1 = (bf16[40,32,128]{2,1,0:T(8,128)(2,1)}, bf16[40,32,128]{2,1,0:T(8,128)(2,1)S(1)}, u32[]{:S(2)}, u32[]{:S(2)}) collective-permute-start(bf16[40,32,128]{2,1,0:T(8,128)(2,1)} %shard_map.77.refs_0_.table_ref), channel_id=1, source_target_pairs={{0,384},{64,448},{128,0},{192,64},{256,128},{320,192},{384,256},{4... | collective-permute-start | bytes 983048 | tf_op jit(solution)/shard_map/ppermute | solution.py:225
  11.9 2.7 collective-permute-start.2
  14.6 2.8 collective-permute-start.3
  20.0 32.6 %all_to_all.30.ids_ref = s32[64,1,128]{2,1,0:T(1,128)} all-to-all(s32[64,1,128]{2,1,0:T(1,128)} %get-tuple-element.14), channel_id=1, replica_groups=mesh['grp'=8,'own'=64] {'own'}, dimensions={0} | all-to-all | bytes 65536 | tf_op jit(solution)/shard_map/all_to_all | solution.py:221
  54.1 2.6 shard_map.79
  56.7 59.6 %all_to_all.31.slice_ref = bf16[128,32,128]{2,1,0:T(8,128)(2,1)} all-to-all(bf16[128,32,128]{2,1,0:T(8,128)(2,1)} %shard_map.79), channel_id=1, replica_groups=mesh['grp'=8,'own'=64] {'own'}, dimensions={0} | all-to-all | bytes 2097152 | tf_op jit(solution)/shard_map/all_to_all | solution.py:221
  116.3 6.5 %shard_map.80 = (bf16[128,16,128]{2,1,0:T(8,128)(2,1)}, f32[64,128]{1,0:T(8,128)}) custom-call(s32[64]{0:T(128)} %get-tuple-element.15.slot_ref, s32[64]{0:T(128)} %fill_ref.1, bf16[64,64,128]{2,1,0:T(8,128)(2,1)} %bitcast.4, bf16[64,64,128]{2,1,0:T(8,128)(2,1)} %bitcast.8, bf16[64,128]{1,0:T(8,128)(2,1)} %value_ref.1, ...), custom_call_target="tpu_custom_call" | custom-call | flops 1000000 | bytes 4000000 | tf_op jit(solution)/shard_map/pallas_call | solution.py:293
  122.8 5.9 %all-to-all-start.2 = ((bf16[128,16,128]{2,1,0:T(8,128)(2,1)}), bf16[128,16,128]{2,1,0:T(8,128)(2,1)S(1)}, u32[]{:S(2)}, u32[]{:S(2)}) async-start(bf16[128,16,128]{2,1,0:T(8,128)(2,1)} %get-tuple-element.16), calls=%async_computation.2 | async-start | bytes 1048576 | tf_op jit(solution)/shard_map/all_to_all | solution.py:221
  128.7 4.4 %shard_map.84 = bf16[128,16,128]{2,1,0:T(8,128)(2,1)} custom-call(s32[64]{0:T(128)} %get-tuple-element.15.slot_ref, bf16[64,64,128]{2,1,0:T(8,128)(2,1)} %bitcast.5, bf16[64,64,128]{2,1,0:T(8,128)(2,1)} %bitcast.9, f32[64,128]{1,0:T(8,128)} %get-tuple-element.21.res_ref), custom_call_target="tpu_custom_call" | custom-call | flops 1000000 | bytes 4000000 | tf_op jit(solution)/shard_map/pallas_call | solution.py:300
  133.1 26.4 %all-to-all-done.2.grad_ref = bf16[128,16,128]{2,1,0:T(8,128)(2,1)S(1)} async-done(((bf16[128,16,128]{2,1,0:T(8,128)(2,1)}), bf16[128,16,128]{2,1,0:T(8,128)(2,1)S(1)}, u32[]{:S(2)}, u32[]{:S(2)}) %all-to-all-start.2) | async-done | bytes 524320 | tf_op jit(solution)/shard_map/all_to_all | solution.py:221
  160.3 6.0 %all-to-all-start.3 = ((bf16[128,16,128]{2,1,0:T(8,128)(2,1)}), bf16[128,16,128]{2,1,0:T(8,128)(2,1)S(1)}, u32[]{:S(2)}, u32[]{:S(2)}) async-start(bf16[128,16,128]{2,1,0:T(8,128)(2,1)} %shard_map.84), calls=%async_computation.3 | async-start | bytes 1048576 | tf_op jit(solution)/shard_map/all_to_all | solution.py:221
  166.2 2.7 shard_map.81.part_ref
  176.1 3.7 %collective-permute-start.5 = (bf16[40,16,128]{2,1,0:T(8,128)(2,1)}, bf16[40,16,128]{2,1,0:T(8,128)(2,1)S(1)}, u32[]{:S(2)}, u32[]{:S(2)}) collective-permute-start(bf16[40,16,128]{2,1,0:T(8,128)(2,1)} %get-tuple-element.18), channel_id=1, source_target_pairs={{0,128},{64,192},{128,256},{192,320},{256,384},{320,448},{384,0},{... | collective-permute-start | bytes 491528 | tf_op jit(solution)/shard_map/ppermute | solution.py:225
  179.9 3.9 %collective-permute-start.6 = (bf16[40,16,128]{2,1,0:T(8,128)(2,1)}, bf16[40,16,128]{2,1,0:T(8,128)(2,1)S(1)}, u32[]{:S(2)}, u32[]{:S(2)}) collective-permute-start(bf16[40,16,128]{2,1,0:T(8,128)(2,1)} %get-tuple-element.19), channel_id=1, source_target_pairs={{0,256},{64,320},{128,384},{192,448},{256,0},{320,64},{384,128},{4... | collective-permute-start | bytes 491528 | tf_op jit(solution)/shard_map/ppermute | solution.py:225
  183.8 3.1 collective-permute-start.7
  186.8 2.9 collective-permute-done.6.refs_1_
  194.3 4.6 %collective-permute-start.15 = (bf16[40,16,128]{2,1,0:T(8,128)(2,1)}, bf16[40,16,128]{2,1,0:T(8,128)(2,1)S(1)}, u32[]{:S(2)}, u32[]{:S(2)}) collective-permute-start(bf16[40,16,128]{2,1,0:T(8,128)(2,1)} %shard_map.83.new_a_ref.refs_0_), channel_id=1, source_target_pairs={{0,384},{64,448},{128,0},{192,64},{256,128},{320,192},{384,256},{4... | collective-permute-start | bytes 491528 | tf_op jit(solution)/shard_map/ppermute | solution.py:225
  198.9 3.0 collective-permute-start.16
  205.6 3.9 %collective-permute-done.16.refs_2_ = bf16[40,16,128]{2,1,0:T(8,128)(2,1)S(1)} collective-permute-done((bf16[40,16,128]{2,1,0:T(8,128)(2,1)}, bf16[40,16,128]{2,1,0:T(8,128)(2,1)S(1)}, u32[]{:S(2)}, u32[]{:S(2)}) %collective-permute-start.16) | collective-permute-done | bytes 163872 | tf_op jit(solution)/shard_map/ppermute | solution.py:225
  215.6 15.1 %all-to-all-start.5 = ((bf16[128,16,128]{2,1,0:T(8,128)(2,1)}), bf16[128,16,128]{2,1,0:T(8,128)(2,1)S(1)}, u32[]{:S(2)}, u32[]{:S(2)}) async-start(bf16[128,16,128]{2,1,0:T(8,128)(2,1)} %shard_map.90), calls=%async_computation.5 | async-start | bytes 1048576 | tf_op jit(solution)/shard_map/all_to_all | solution.py:221
  230.7 2.7 shard_map.85.part_ref
  242.6 3.5 %collective-permute-start.10 = (bf16[40,16,128]{2,1,0:T(8,128)(2,1)}, bf16[40,16,128]{2,1,0:T(8,128)(2,1)S(1)}, u32[]{:S(2)}, u32[]{:S(2)}) collective-permute-start(bf16[40,16,128]{2,1,0:T(8,128)(2,1)} %get-tuple-element.24), channel_id=1, source_target_pairs={{0,256},{64,320},{128,384},{192,448},{256,0},{320,64},{384,128},{4... | collective-permute-start | bytes 491528 | tf_op jit(solution)/shard_map/ppermute | solution.py:225
  246.1 3.9 %collective-permute-start.11 = (bf16[40,16,128]{2,1,0:T(8,128)(2,1)}, bf16[40,16,128]{2,1,0:T(8,128)(2,1)S(1)}, u32[]{:S(2)}, u32[]{:S(2)}) collective-permute-start(bf16[40,16,128]{2,1,0:T(8,128)(2,1)} %get-tuple-element.25), channel_id=1, source_target_pairs={{0,384},{64,448},{128,0},{192,64},{256,128},{320,192},{384,256},{4... | collective-permute-start | bytes 491528 | tf_op jit(solution)/shard_map/ppermute | solution.py:225
  250.0 3.8 %collective-permute-done.9.refs_0_ = bf16[40,16,128]{2,1,0:T(8,128)(2,1)S(1)} collective-permute-done((bf16[40,16,128]{2,1,0:T(8,128)(2,1)}, bf16[40,16,128]{2,1,0:T(8,128)(2,1)S(1)}, u32[]{:S(2)}, u32[]{:S(2)}) %collective-permute-start.9) | collective-permute-done | bytes 163872 | tf_op jit(solution)/shard_map/ppermute | solution.py:225
  258.9 4.6 %collective-permute-start.12 = (bf16[40,16,128]{2,1,0:T(8,128)(2,1)}, bf16[40,16,128]{2,1,0:T(8,128)(2,1)S(1)}, u32[]{:S(2)}, u32[]{:S(2)}) collective-permute-start(bf16[40,16,128]{2,1,0:T(8,128)(2,1)} %shard_map.87.new_b_ref.refs_0_), channel_id=1, source_target_pairs={{0,384},{64,448},{128,0},{192,64},{256,128},{320,192},{384,256},{4... | collective-permute-start | bytes 491528 | tf_op jit(solution)/shard_map/ppermute | solution.py:225
  265.5 2.6 collective-permute-start.14
  268.1 2.5 collective-permute-done.12.refs_1_
  270.7 3.4 %collective-permute-done.13.refs_2_ = bf16[40,16,128]{2,1,0:T(8,128)(2,1)S(1)} collective-permute-done((bf16[40,16,128]{2,1,0:T(8,128)(2,1)}, bf16[40,16,128]{2,1,0:T(8,128)(2,1)S(1)}, u32[]{:S(2)}, u32[]{:S(2)}) %collective-permute-start.13) | collective-permute-done | bytes 163872 | tf_op jit(solution)/shard_map/ppermute | solution.py:225
  280.0 15.1 %all-to-all-start.4 = ((bf16[128,16,128]{2,1,0:T(8,128)(2,1)}), bf16[128,16,128]{2,1,0:T(8,128)(2,1)S(1)}, u32[]{:S(2)}, u32[]{:S(2)}) async-start(bf16[128,16,128]{2,1,0:T(8,128)(2,1)} %shard_map.89), calls=%async_computation.4 | async-start | bytes 1048576 | tf_op jit(solution)/shard_map/all_to_all | solution.py:221
  297.3 3.9 %shard_map.91.refs_0_ = bf16[64,64,128]{2,1,0:T(8,128)(2,1)} custom-call(s32[64]{0:T(128)} %get-tuple-element.15.slot_ref, bf16[64,64,128]{2,1,0:T(8,128)(2,1)} %bitcast.6, bf16[128,16,128]{2,1,0:T(8,128)(2,1)} %copy-done.2), custom_call_target="tpu_custom_call" | custom-call | flops 1000000 | bytes 3000000 | tf_op jit(solution)/shard_map/pallas_call | solution.py:209
  301.2 26.4 %all-to-all-done.4.slice_ref = bf16[128,16,128]{2,1,0:T(8,128)(2,1)S(1)} async-done(((bf16[128,16,128]{2,1,0:T(8,128)(2,1)}), bf16[128,16,128]{2,1,0:T(8,128)(2,1)S(1)}, u32[]{:S(2)}, u32[]{:S(2)}) %all-to-all-start.4) | async-done | bytes 524320 | tf_op jit(solution)/shard_map/all_to_all | solution.py:221
  328.4 3.9 %shard_map.92 = bf16[64,64,128]{2,1,0:T(8,128)(2,1)} custom-call(s32[64]{0:T(128)} %get-tuple-element.15.slot_ref, bf16[64,64,128]{2,1,0:T(8,128)(2,1)} %bitcast.7, bf16[128,16,128]{2,1,0:T(8,128)(2,1)} %copy-done.3, bf16[64,64,128]{2,1,0:T(8,128)(2,1)} %shard_map.91.refs_0_), custom_call_target="tpu_custom_call", output_to_operand_aliasing={{}: (3, {})} | custom-call | flops 1000000 | bytes 3000000 | tf_op jit(solution)/shard_map/pallas_call | solution.py:209
  (74 shorter events, 58.1 us)
Async XLA Ops:
  0.6 3.7 %collective-permute-start = (bf16[20,64,64]{2,1,0:T(8,128)(2,1)}, bf16[20,64,64]{2,1,0:T(8,128)(2,1)S(1)}, u32[]{:S(2)}, u32[]{:S(2)}) collective-permute-start(bf16[20,64,64]{2,1,0:T(8,128)(2,1)} %core_ref.1), channel_id=1, source_target_pairs={{0,64},{64,0},{128,192},{192,128},{256,320},{320,256},{384,448},{4... | collective-permute-start | bytes 491528 | tf_op jit(solution)/shard_map/ppermute | solution.py:229
  7.2 45.3 %collective-permute-start.1 = (bf16[40,32,128]{2,1,0:T(8,128)(2,1)}, bf16[40,32,128]{2,1,0:T(8,128)(2,1)S(1)}, u32[]{:S(2)}, u32[]{:S(2)}) collective-permute-start(bf16[40,32,128]{2,1,0:T(8,128)(2,1)} %shard_map.77.refs_0_.table_ref), channel_id=1, source_target_pairs={{0,384},{64,448},{128,0},{192,64},{256,128},{320,192},{384,256},{4... | collective-permute-start | bytes 983048 | tf_op jit(solution)/shard_map/ppermute | solution.py:225
  11.9 40.7 %collective-permute-start.2 = (bf16[40,32,128]{2,1,0:T(8,128)(2,1)}, bf16[40,32,128]{2,1,0:T(8,128)(2,1)S(1)}, u32[]{:S(2)}, u32[]{:S(2)}) collective-permute-start(bf16[40,32,128]{2,1,0:T(8,128)(2,1)} %shard_map.77.refs_0_.table_ref), channel_id=1, source_target_pairs={{0,256},{64,320},{128,384},{192,448},{256,0},{320,64},{384,128},{4... | collective-permute-start | bytes 983048 | tf_op jit(solution)/shard_map/ppermute | solution.py:225
  14.6 38.0 %collective-permute-start.3 = (bf16[40,32,128]{2,1,0:T(8,128)(2,1)}, bf16[40,32,128]{2,1,0:T(8,128)(2,1)S(1)}, u32[]{:S(2)}, u32[]{:S(2)}) collective-permute-start(bf16[40,32,128]{2,1,0:T(8,128)(2,1)} %shard_map.77.refs_0_.table_ref), channel_id=1, source_target_pairs={{0,128},{64,192},{128,256},{192,320},{256,384},{320,448},{384,0},{... | collective-permute-start | bytes 983048 | tf_op jit(solution)/shard_map/ppermute | solution.py:225
  122.8 36.7 %all-to-all-start.2 = ((bf16[128,16,128]{2,1,0:T(8,128)(2,1)}), bf16[128,16,128]{2,1,0:T(8,128)(2,1)S(1)}, u32[]{:S(2)}, u32[]{:S(2)}) async-start(bf16[128,16,128]{2,1,0:T(8,128)(2,1)} %get-tuple-element.16), calls=%async_computation.2 | async-start | bytes 1048576 | tf_op jit(solution)/shard_map/all_to_all | solution.py:221
  160.3 54.6 %all-to-all-start.3 = ((bf16[128,16,128]{2,1,0:T(8,128)(2,1)}), bf16[128,16,128]{2,1,0:T(8,128)(2,1)S(1)}, u32[]{:S(2)}, u32[]{:S(2)}) async-start(bf16[128,16,128]{2,1,0:T(8,128)(2,1)} %shard_map.84), calls=%async_computation.3 | async-start | bytes 1048576 | tf_op jit(solution)/shard_map/all_to_all | solution.py:221
  168.9 4.2 %collective-permute-start.4 = (bf16[160,16,128]{2,1,0:T(8,128)(2,1)}, bf16[160,16,128]{2,1,0:T(8,128)(2,1)S(1)}, u32[]{:S(2)}, u32[]{:S(2)}) collective-permute-start(bf16[160,16,128]{2,1,0:T(8,128)(2,1)} %shard_map.81.part_ref), channel_id=1, source_target_pairs={{0,64},{64,0},{128,192},{192,128},{256,320},{320,256},{384,448},{4... | collective-permute-start | bytes 1966088 | tf_op jit(solution)/shard_map/ppermute | solution.py:229
  173.1 0.8 copy-start.4
  176.1 10.7 %collective-permute-start.5 = (bf16[40,16,128]{2,1,0:T(8,128)(2,1)}, bf16[40,16,128]{2,1,0:T(8,128)(2,1)S(1)}, u32[]{:S(2)}, u32[]{:S(2)}) collective-permute-start(bf16[40,16,128]{2,1,0:T(8,128)(2,1)} %get-tuple-element.18), channel_id=1, source_target_pairs={{0,128},{64,192},{128,256},{192,320},{256,384},{320,448},{384,0},{... | collective-permute-start | bytes 491528 | tf_op jit(solution)/shard_map/ppermute | solution.py:225
  179.9 9.9 %collective-permute-start.6 = (bf16[40,16,128]{2,1,0:T(8,128)(2,1)}, bf16[40,16,128]{2,1,0:T(8,128)(2,1)S(1)}, u32[]{:S(2)}, u32[]{:S(2)}) collective-permute-start(bf16[40,16,128]{2,1,0:T(8,128)(2,1)} %get-tuple-element.19), channel_id=1, source_target_pairs={{0,256},{64,320},{128,384},{192,448},{256,0},{320,64},{384,128},{4... | collective-permute-start | bytes 491528 | tf_op jit(solution)/shard_map/ppermute | solution.py:225
  183.8 7.9 %collective-permute-start.7 = (bf16[40,16,128]{2,1,0:T(8,128)(2,1)}, bf16[40,16,128]{2,1,0:T(8,128)(2,1)S(1)}, u32[]{:S(2)}, u32[]{:S(2)}) collective-permute-start(bf16[40,16,128]{2,1,0:T(8,128)(2,1)} %get-tuple-element.20), channel_id=1, source_target_pairs={{0,384},{64,448},{128,0},{192,64},{256,128},{320,192},{384,256},{4... | collective-permute-start | bytes 491528 | tf_op jit(solution)/shard_map/ppermute | solution.py:225
  186.8 4.9 %copy-start.11 = (bf16[40,16,128]{2,1,0:T(8,128)(2,1)}, bf16[40,16,128]{2,1,0:T(8,128)(2,1)S(1)}, u32[]{:S(2)}) copy-start(bf16[40,16,128]{2,1,0:T(8,128)(2,1)S(1)} %collective-permute-done.5.refs_0_) | copy-start | bytes 491524
  189.8 1.9 copy-start.13
  194.3 11.3 %collective-permute-start.15 = (bf16[40,16,128]{2,1,0:T(8,128)(2,1)}, bf16[40,16,128]{2,1,0:T(8,128)(2,1)S(1)}, u32[]{:S(2)}, u32[]{:S(2)}) collective-permute-start(bf16[40,16,128]{2,1,0:T(8,128)(2,1)} %shard_map.83.new_a_ref.refs_0_), channel_id=1, source_target_pairs={{0,384},{64,448},{128,0},{192,64},{256,128},{320,192},{384,256},{4... | collective-permute-start | bytes 491528 | tf_op jit(solution)/shard_map/ppermute | solution.py:225
  198.9 10.6 %collective-permute-start.16 = (bf16[40,16,128]{2,1,0:T(8,128)(2,1)}, bf16[40,16,128]{2,1,0:T(8,128)(2,1)S(1)}, u32[]{:S(2)}, u32[]{:S(2)}) collective-permute-start(bf16[40,16,128]{2,1,0:T(8,128)(2,1)} %shard_map.83.new_a_ref.refs_0_), channel_id=1, source_target_pairs={{0,256},{64,320},{128,384},{192,448},{256,0},{320,64},{384,128},{4... | collective-permute-start | bytes 491528 | tf_op jit(solution)/shard_map/ppermute | solution.py:225
  201.9 9.9 %collective-permute-start.17 = (bf16[40,16,128]{2,1,0:T(8,128)(2,1)}, bf16[40,16,128]{2,1,0:T(8,128)(2,1)S(1)}, u32[]{:S(2)}, u32[]{:S(2)}) collective-permute-start(bf16[40,16,128]{2,1,0:T(8,128)(2,1)} %shard_map.83.new_a_ref.refs_0_), channel_id=1, source_target_pairs={{0,128},{64,192},{128,256},{192,320},{256,384},{320,448},{384,0},{... | collective-permute-start | bytes 491528 | tf_op jit(solution)/shard_map/ppermute | solution.py:225
  205.6 6.2 %copy-start.15 = (bf16[40,16,128]{2,1,0:T(8,128)(2,1)}, bf16[40,16,128]{2,1,0:T(8,128)(2,1)S(1)}, u32[]{:S(2)}) copy-start(bf16[40,16,128]{2,1,0:T(8,128)(2,1)S(1)} %collective-permute-done.15.refs_1_) | copy-start | bytes 491524
  209.5 2.3 copy-start.19
  215.6 63.6 %all-to-all-start.5 = ((bf16[128,16,128]{2,1,0:T(8,128)(2,1)}), bf16[128,16,128]{2,1,0:T(8,128)(2,1)S(1)}, u32[]{:S(2)}, u32[]{:S(2)}) async-start(bf16[128,16,128]{2,1,0:T(8,128)(2,1)} %shard_map.90), calls=%async_computation.5 | async-start | bytes 1048576 | tf_op jit(solution)/shard_map/all_to_all | solution.py:221
  233.4 4.2 %collective-permute-start.8 = (bf16[160,16,128]{2,1,0:T(8,128)(2,1)}, bf16[160,16,128]{2,1,0:T(8,128)(2,1)S(1)}, u32[]{:S(2)}, u32[]{:S(2)}) collective-permute-start(bf16[160,16,128]{2,1,0:T(8,128)(2,1)} %shard_map.85.part_ref), channel_id=1, source_target_pairs={{0,64},{64,0},{128,192},{192,128},{256,320},{320,256},{384,448},{4... | collective-permute-start | bytes 1966088 | tf_op jit(solution)/shard_map/ppermute | solution.py:229
  237.6 0.8 copy-start.5
  240.7 13.1 %collective-permute-start.9 = (bf16[40,16,128]{2,1,0:T(8,128)(2,1)}, bf16[40,16,128]{2,1,0:T(8,128)(2,1)S(1)}, u32[]{:S(2)}, u32[]{:S(2)}) collective-permute-start(bf16[40,16,128]{2,1,0:T(8,128)(2,1)} %get-tuple-element.23), channel_id=1, source_target_pairs={{0,128},{64,192},{128,256},{192,320},{256,384},{320,448},{384,0},{... | collective-permute-start | bytes 491528 | tf_op jit(solution)/shard_map/ppermute | solution.py:225
  242.6 11.1 %collective-permute-start.10 = (bf16[40,16,128]{2,1,0:T(8,128)(2,1)}, bf16[40,16,128]{2,1,0:T(8,128)(2,1)S(1)}, u32[]{:S(2)}, u32[]{:S(2)}) collective-permute-start(bf16[40,16,128]{2,1,0:T(8,128)(2,1)} %get-tuple-element.24), channel_id=1, source_target_pairs={{0,256},{64,320},{128,384},{192,448},{256,0},{320,64},{384,128},{4... | collective-permute-start | bytes 491528 | tf_op jit(solution)/shard_map/ppermute | solution.py:225
  246.1 10.2 %collective-permute-start.11 = (bf16[40,16,128]{2,1,0:T(8,128)(2,1)}, bf16[40,16,128]{2,1,0:T(8,128)(2,1)S(1)}, u32[]{:S(2)}, u32[]{:S(2)}) collective-permute-start(bf16[40,16,128]{2,1,0:T(8,128)(2,1)} %get-tuple-element.25), channel_id=1, source_target_pairs={{0,384},{64,448},{128,0},{192,64},{256,128},{320,192},{384,256},{4... | collective-permute-start | bytes 491528 | tf_op jit(solution)/shard_map/ppermute | solution.py:225
  253.7 2.5 copy-start.10
  253.7 2.5 copy-start.12
  258.9 11.8 %collective-permute-start.12 = (bf16[40,16,128]{2,1,0:T(8,128)(2,1)}, bf16[40,16,128]{2,1,0:T(8,128)(2,1)S(1)}, u32[]{:S(2)}, u32[]{:S(2)}) collective-permute-start(bf16[40,16,128]{2,1,0:T(8,128)(2,1)} %shard_map.87.new_b_ref.refs_0_), channel_id=1, source_target_pairs={{0,384},{64,448},{128,0},{192,64},{256,128},{320,192},{384,256},{4... | collective-permute-start | bytes 491528 | tf_op jit(solution)/shard_map/ppermute | solution.py:225
  263.4 10.7 %collective-permute-start.13 = (bf16[40,16,128]{2,1,0:T(8,128)(2,1)}, bf16[40,16,128]{2,1,0:T(8,128)(2,1)S(1)}, u32[]{:S(2)}, u32[]{:S(2)}) collective-permute-start(bf16[40,16,128]{2,1,0:T(8,128)(2,1)} %shard_map.87.new_b_ref.refs_0_), channel_id=1, source_target_pairs={{0,256},{64,320},{128,384},{192,448},{256,0},{320,64},{384,128},{4... | collective-permute-start | bytes 491528 | tf_op jit(solution)/shard_map/ppermute | solution.py:225
  265.5 10.7 %collective-permute-start.14 = (bf16[40,16,128]{2,1,0:T(8,128)(2,1)}, bf16[40,16,128]{2,1,0:T(8,128)(2,1)S(1)}, u32[]{:S(2)}, u32[]{:S(2)}) collective-permute-start(bf16[40,16,128]{2,1,0:T(8,128)(2,1)} %shard_map.87.new_b_ref.refs_0_), channel_id=1, source_target_pairs={{0,128},{64,192},{128,256},{192,320},{256,384},{320,448},{384,0},{... | collective-permute-start | bytes 491528 | tf_op jit(solution)/shard_map/ppermute | solution.py:225
  270.7 5.5 %copy-start.14 = (bf16[40,16,128]{2,1,0:T(8,128)(2,1)}, bf16[40,16,128]{2,1,0:T(8,128)(2,1)S(1)}, u32[]{:S(2)}) copy-start(bf16[40,16,128]{2,1,0:T(8,128)(2,1)S(1)} %collective-permute-done.12.refs_1_) | copy-start | bytes 491524
  274.1 2.1 copy-start.18
  280.0 47.6 %all-to-all-start.4 = ((bf16[128,16,128]{2,1,0:T(8,128)(2,1)}), bf16[128,16,128]{2,1,0:T(8,128)(2,1)S(1)}, u32[]{:S(2)}, u32[]{:S(2)}) async-start(bf16[128,16,128]{2,1,0:T(8,128)(2,1)} %shard_map.89), calls=%async_computation.4 | async-start | bytes 1048576 | tf_op jit(solution)/shard_map/all_to_all | solution.py:221
  (12 other events, 8.9 us)

commit v5 on v3

--- a/solution.py
+++ b/solution.py
@@ -39,17 +39,17 @@
         return carry
 
     def place(t, carry):
-        block = tile_slice_ref[t] // per_device
-        owner = block % owners
-        group = block // owners
+        block = lax.div(tile_slice_ref[t], per_device)
+        owner = lax.rem(block, owners)
+        group = lax.div(block, owners)
         rank = count_ref[owner]
         count_ref[owner] = rank + 1
         slot_ref[t] = 2 * owner + rank
-        wanted_ref[owner, 0, rank] = group * per_device + tile_slice_ref[t] % per_device
+        wanted_ref[owner, 0, rank] = group * per_device + tile_slice_ref[t] - block * per_device
         return carry
 
     lax.fori_loop(0, owners, clear, 0, unroll=8)
-    lax.fori_loop(0, slot_ref.shape[0], place, 0, unroll=4)
+    lax.fori_loop(0, slot_ref.shape[0], place, 0, unroll=8)
 
 
 def pick_rows(ids_ref, table_ref, out_ref):
@@ -162,16 +162,33 @@
     lax.fori_loop(0, left_ref.shape[0] // wide, step, 0)
 
 
-def call(kernel, in_specs, outs, scratch=(), out_specs=None, flops=10**6, moved=4 * 10**6):
+def call(kernel, in_specs, outs, scratch=(), out_specs=None, keep=True):
     many = isinstance(outs, tuple)
-    return pl.pallas_call(
+    outs = outs if many else (outs,)
+    specs = out_specs or (VMEM,) * len(outs)
+    shapes = tuple(
+        pltpu.VMEM(out.shape, out.dtype) if keep and spec is VMEM else out
+        for out, spec in zip(outs, specs)
+    )
+    run = pl.pallas_call(
         kernel,
-        out_shape=outs,
+        out_shape=shapes,
         in_specs=in_specs,
-        out_specs=out_specs or ((VMEM,) * len(outs) if many else VMEM),
+        out_specs=tuple(specs),
         scratch_shapes=list(scratch),
-        cost_estimate=pl.CostEstimate(flops=flops, bytes_accessed=moved, transcendentals=0),
-    )
+        compiler_params=pltpu.CompilerParams(vmem_limit_bytes=12 * 2**20),
+        cost_estimate=pl.CostEstimate(flops=10**6, bytes_accessed=4 * 10**6, transcendentals=0),
+    )
+
+    def place(*args):
+        placed = [
+            pltpu.with_memory_space_constraint(arg, pltpu.VMEM) if spec is VMEM else arg
+            for arg, spec in zip(args, in_specs)
+        ]
+        results = run(*placed)
+        return results if many else results[0]
+
+    return place
 
 
 def exchange(x, axis):
@@ -254,7 +271,7 @@
         me, ids, new_near, new_far
     )
     new_got = exchange(outgoing, "own")
-    new_left_t = call(refresh_kernel, [SMEM, VMEM, VMEM], sds(left_t.shape, BF16))(
+    new_left_t = call(refresh_kernel, [SMEM, VMEM, VMEM], sds(left_t.shape, BF16), keep=False)(
         slot, left_t, new_got
     )
     return (new_core, jnp.swapaxes(new_left_t, 1, 2))

time: 306 us -> 288 us (0.941)
  blocking collectives: 212 us -> 146 us
  waiting for transfers between devices: 18.1 us -> 72.6 us
  Pallas kernels: 29.5 us -> 16.6 us
  starting transfers between devices: 42.6 us -> 48.6 us
    all_to_all x3 -> x2, blocking collectives: 182 us -> 119 us  [exchange(): return lax.all_to_all(x, axis, split_axis=0, concat_axis=0, tiled=True)]
    all_to_all x1 -> x2, waiting for transfers between devices: 13.7 us -> 68.5 us  [exchange(): return lax.all_to_all(x, axis, split_axis=0, concat_axis=0, tiled=True)]
    pallas_call x9, Pallas kernels: 29.5 us -> 16.6 us  [place(): results = run(*placed)]
    all_to_all x1 -> x2, starting transfers between devices: 18.7 us -> 24.7 us  [exchange(): return lax.all_to_all(x, axis, split_axis=0, concat_axis=0, tiled=True)]
  transfers between devices with their start and end apart: 10 -> 11, of which waited for: 3 -> 4; matrix products, arithmetic and copies ran while one was open for 0% -> 0% of each run, Pallas kernels for 1% -> 1%
where the time goes in v5:
time: 288 us; the launch traced here: 287 us
  blocking collectives  146 us (51%)
  waiting for transfers between devices  72.6 us (25%)
  starting transfers between devices  48.6 us (17%)
  Pallas kernels  16.6 us (6%)
    all_to_all x2, blocking collectives, exchange(): return lax.all_to_all(x, axis, split_axis=0, concat_axis=0, tiled=True)  119 us
    all_to_all x2, waiting for transfers between devices, exchange(): return lax.all_to_all(x, axis, split_axis=0, concat_axis=0, tiled=True)  68.5 us
    all_to_all x2, blocking collectives, exchange_x(): lax.all_to_all(x, 'grp', split_axis=0, concat_axis=0, tiled=True, axis_in...  26.9 us
    all_to_all x2, starting transfers between devices, exchange(): return lax.all_to_all(x, axis, split_axis=0, concat_axis=0, tiled=True)  24.7 us
    pallas_call x9, Pallas kernels, place(): results = run(*placed)  16.6 us
    ppermute x6, starting transfers between devices, swap(): return lax.ppermute(x, 'grp', [(g, g ^ 1) for g in range(groups)])  12.5 us
    ppermute x3, starting transfers between devices, shift(): lax.ppermute(x, 'grp', [(g, (g + 2 * step) % groups) for g in range(group...  11.4 us
  transfers between devices with their start and end apart: 11, of which 4 were waited for; matrix products, arithmetic and copies ran while one was open for 0% of the time, Pallas kernels for 1%

profile of v5, /device:TPU:8, one launch (start us, length us, event | category | flops | bytes accessed | tf_op | source)
XLA Modules:
  0.0 286.9 jit_solution(481607748624908037)
XLA Ops:
  0.6 1.0 copy-done.2
  1.6 0.2 shard_map.77.refs_0_.table_ref
  1.8 3.4 %collective-permute-start.2 = (bf16[20,32,128]{2,1,0:T(8,128)(2,1)S(1)}, bf16[20,32,128]{2,1,0:T(8,128)(2,1)S(1)}, u32[]{:S(2)}, u32[]{:S(2)}) collective-permute-start(bf16[20,32,128]{2,1,0:T(8,128)(2,1)S(1)} %shard_map.77.refs_0_.table_ref), channel_id=1, source_target_pairs={{0,128},{64,192},{128,256},{192,320},{256,384},{320,448},{384,0},{... | collective-permute-start | bytes 491528 | tf_op jit(solution)/shard_map/ppermute | solution.py:199
  5.2 4.6 %collective-permute-start.1 = (bf16[20,32,128]{2,1,0:T(8,128)(2,1)S(1)}, bf16[20,32,128]{2,1,0:T(8,128)(2,1)S(1)}, u32[]{:S(2)}, u32[]{:S(2)}) collective-permute-start(bf16[20,32,128]{2,1,0:T(8,128)(2,1)S(1)} %shard_map.77.refs_0_.table_ref), channel_id=1, source_target_pairs={{0,256},{64,320},{128,384},{192,448},{256,0},{320,64},{384,128},{4... | collective-permute-start | bytes 491528 | tf_op jit(solution)/shard_map/ppermute | solution.py:199
  9.9 3.3 %collective-permute-start = (bf16[20,32,128]{2,1,0:T(8,128)(2,1)S(1)}, bf16[20,32,128]{2,1,0:T(8,128)(2,1)S(1)}, u32[]{:S(2)}, u32[]{:S(2)}) collective-permute-start(bf16[20,32,128]{2,1,0:T(8,128)(2,1)S(1)} %shard_map.77.refs_0_.table_ref), channel_id=1, source_target_pairs={{0,384},{64,448},{128,0},{192,64},{256,128},{320,192},{384,256},{4... | collective-permute-start | bytes 491528 | tf_op jit(solution)/shard_map/ppermute | solution.py:199
  13.2 1.9 collective-permute-start.3
  15.2 2.4 collective-permute-start.6
  17.6 1.9 collective-permute-start.5
  19.5 2.4 collective-permute-start.4
  22.0 0.0 copy-start.5
  22.0 0.6 copy-done.5
  22.6 2.4 shard_map.78
  25.1 18.7 %all-to-all-start = ((s32[64,1,128]{2,1,0:T(1,128)}), s32[64,1,128]{2,1,0:T(1,128)S(1)}, u32[]{:S(2)}, u32[]{:S(2)}) async-start(s32[64,1,128]{2,1,0:T(1,128)} %get-tuple-element.8), calls=%async_computation | async-start | bytes 65536 | tf_op jit(solution)/shard_map/all_to_all | solution.py:195
  43.8 13.7 %all-to-all-done.ids_ref = s32[64,1,128]{2,1,0:T(1,128)S(1)} async-done(((s32[64,1,128]{2,1,0:T(1,128)}), s32[64,1,128]{2,1,0:T(1,128)S(1)}, u32[]{:S(2)}, u32[]{:S(2)}) %all-to-all-start) | async-done | bytes 32800 | tf_op jit(solution)/shard_map/all_to_all | solution.py:195
  57.6 1.3 shard_map.79
  59.0 59.0 %all_to_all.30.slice_ref = bf16[128,32,128]{2,1,0:T(8,128)(2,1)S(1)} all-to-all(bf16[128,32,128]{2,1,0:T(8,128)(2,1)S(1)} %shard_map.79), channel_id=1, replica_groups=mesh['grp'=8,'own'=64] {'own'}, dimensions={0} | all-to-all | bytes 2097152 | tf_op jit(solution)/shard_map/all_to_all | solution.py:195
  118.0 4.5 %shard_map.80 = bf16[128,32,128]{2,1,0:T(8,128)(2,1)S(1)} custom-call(s32[64]{0:T(128)S(1)} %get-tuple-element.9.slot_ref, s32[64]{0:T(128)S(1)} %copy-done.4, bf16[64,64,128]{2,1,0:T(8,128)(2,1)S(1)} %bitcast.4, bf16[64,64,128]{2,1,0:T(8,128)(2,1)S(1)} %bitcast.6, bf16[64,128]{1,0:T(8,128)(2,1)S(1)} %copy-done.3, bf16[128,32,128]{2,1,0:T(8,128)(2,1)S(1)} %all_to_all.30.slice_ref), custom_call_target="tpu_custom_call" | custom-call | flops 1000000 | bytes 4000000 | tf_op jit(solution)/shard_map/pallas_call | solution.py:188
  122.4 60.0 %all_to_all.31.grad_ref = bf16[128,32,128]{2,1,0:T(8,128)(2,1)S(1)} all-to-all(bf16[128,32,128]{2,1,0:T(8,128)(2,1)S(1)} %shard_map.80), channel_id=1, replica_groups=mesh['grp'=8,'own'=64] {'own'}, dimensions={0} | all-to-all | bytes 2097152 | tf_op jit(solution)/shard_map/all_to_all | solution.py:195
  182.4 2.0 shard_map.81
  184.4 1.9 collective-permute-start.7
  186.3 2.1 collective-permute-done.7.other_ref
  188.4 0.1 shard_map.82
  188.5 13.9 %all_to_all.32.part_ref = bf16[4,20,32,128]{3,2,1,0:T(8,128)(2,1)S(1)} all-to-all(bf16[4,20,32,128]{3,2,1,0:T(8,128)(2,1)S(1)} %shard_map.82), channel_id=1, replica_groups={{0,128,256,384},{64,192,320,448},{1,129,257,385},{65,193,321,449},{2,13..., dimensions={0} | all-to-all | bytes 1310720 | tf_op jit(solution)/shard_map/all_to_all | solution.py:231
  202.4 0.4 shard_map.83
  202.8 13.0 %all_to_all.33.near_ref = bf16[4,20,32,128]{3,2,1,0:T(8,128)(2,1)S(1)} all-to-all(bf16[4,20,32,128]{3,2,1,0:T(8,128)(2,1)S(1)} %get-tuple-element.13), channel_id=1, replica_groups={{0,128,256,384},{64,192,320,448},{1,129,257,385},{65,193,321,449},{2,13..., dimensions={0} | all-to-all | bytes 1310720 | tf_op jit(solution)/shard_map/all_to_all | solution.py:231
  215.9 1.9 collective-permute-start.8
  217.8 2.1 collective-permute-done.8.far_ref
  219.8 2.3 shard_map.84
  222.1 6.0 %all-to-all-start.5 = ((bf16[128,32,128]{2,1,0:T(8,128)(2,1)}), bf16[128,32,128]{2,1,0:T(8,128)(2,1)S(1)}, u32[]{:S(2)}, u32[]{:S(2)}) async-start(bf16[128,32,128]{2,1,0:T(8,128)(2,1)} %shard_map.84), calls=%async_computation.5 | async-start | bytes 2097152 | tf_op jit(solution)/shard_map/all_to_all | solution.py:195
  228.1 0.7 copy.8
  228.9 54.7 %all-to-all-done.5.slice_ref = bf16[128,32,128]{2,1,0:T(8,128)(2,1)S(1)} async-done(((bf16[128,32,128]{2,1,0:T(8,128)(2,1)}), bf16[128,32,128]{2,1,0:T(8,128)(2,1)S(1)}, u32[]{:S(2)}, u32[]{:S(2)}) %all-to-all-start.5) | async-done | bytes 1048608 | tf_op jit(solution)/shard_map/all_to_all | solution.py:195
  283.6 3.3 %shard_map.85 = bf16[64,64,128]{2,1,0:T(8,128)(2,1)} custom-call(s32[64]{0:T(128)S(1)} %get-tuple-element.9.slot_ref, bf16[64,64,128]{2,1,0:T(8,128)(2,1)S(1)} %bitcast.5, bf16[128,32,128]{2,1,0:T(8,128)(2,1)S(1)} %all-to-all-done.5.slice_ref), custom_call_target="tpu_custom_call" | custom-call | flops 1000000 | bytes 4000000 | tf_op jit(solution)/shard_map/pallas_call | solution.py:188
  (16 shorter events, 0.0 us)
Async XLA Ops:
  0.6 1.0 copy-start.2
  1.8 13.3 %collective-permute-start.2 = (bf16[20,32,128]{2,1,0:T(8,128)(2,1)S(1)}, bf16[20,32,128]{2,1,0:T(8,128)(2,1)S(1)}, u32[]{:S(2)}, u32[]{:S(2)}) collective-permute-start(bf16[20,32,128]{2,1,0:T(8,128)(2,1)S(1)} %shard_map.77.refs_0_.table_ref), channel_id=1, source_target_pairs={{0,128},{64,192},{128,256},{192,320},{256,384},{320,448},{384,0},{... | collective-permute-start | bytes 491528 | tf_op jit(solution)/shard_map/ppermute | solution.py:199
  5.2 12.4 %collective-permute-start.1 = (bf16[20,32,128]{2,1,0:T(8,128)(2,1)S(1)}, bf16[20,32,128]{2,1,0:T(8,128)(2,1)S(1)}, u32[]{:S(2)}, u32[]{:S(2)}) collective-permute-start(bf16[20,32,128]{2,1,0:T(8,128)(2,1)S(1)} %shard_map.77.refs_0_.table_ref), channel_id=1, source_target_pairs={{0,256},{64,320},{128,384},{192,448},{256,0},{320,64},{384,128},{4... | collective-permute-start | bytes 491528 | tf_op jit(solution)/shard_map/ppermute | solution.py:199
  9.9 9.6 %collective-permute-start = (bf16[20,32,128]{2,1,0:T(8,128)(2,1)S(1)}, bf16[20,32,128]{2,1,0:T(8,128)(2,1)S(1)}, u32[]{:S(2)}, u32[]{:S(2)}) collective-permute-start(bf16[20,32,128]{2,1,0:T(8,128)(2,1)S(1)} %shard_map.77.refs_0_.table_ref), channel_id=1, source_target_pairs={{0,384},{64,448},{128,0},{192,64},{256,128},{320,192},{384,256},{4... | collective-permute-start | bytes 491528 | tf_op jit(solution)/shard_map/ppermute | solution.py:199
  13.2 44.3 %collective-permute-start.3 = (bf16[20,32,128]{2,1,0:T(8,128)(2,1)S(1)}, bf16[20,32,128]{2,1,0:T(8,128)(2,1)S(1)}, u32[]{:S(2)}, u32[]{:S(2)}) collective-permute-start(bf16[20,32,128]{2,1,0:T(8,128)(2,1)S(1)} %shard_map.77.refs_0_.table_ref), channel_id=1, source_target_pairs={{0,64},{64,0},{128,192},{192,128},{256,320},{320,256},{384,448},{4... | collective-permute-start | bytes 491528 | tf_op jit(solution)/shard_map/ppermute | solution.py:203
  15.2 42.4 %collective-permute-start.6 = (bf16[20,32,128]{2,1,0:T(8,128)(2,1)S(1)}, bf16[20,32,128]{2,1,0:T(8,128)(2,1)S(1)}, u32[]{:S(2)}, u32[]{:S(2)}) collective-permute-start(bf16[20,32,128]{2,1,0:T(8,128)(2,1)S(1)} %collective-permute-done.2.refs_3_), channel_id=1, source_target_pairs={{0,64},{64,0},{128,192},{192,128},{256,320},{320,256},{384,448},{4... | collective-permute-start | bytes 491528 | tf_op jit(solution)/shard_map/ppermute | solution.py:203
  17.6 39.9 %collective-permute-start.5 = (bf16[20,32,128]{2,1,0:T(8,128)(2,1)S(1)}, bf16[20,32,128]{2,1,0:T(8,128)(2,1)S(1)}, u32[]{:S(2)}, u32[]{:S(2)}) collective-permute-start(bf16[20,32,128]{2,1,0:T(8,128)(2,1)S(1)} %collective-permute-done.1.refs_2_), channel_id=1, source_target_pairs={{0,64},{64,0},{128,192},{192,128},{256,320},{320,256},{384,448},{4... | collective-permute-start | bytes 491528 | tf_op jit(solution)/shard_map/ppermute | solution.py:203
  19.5 38.0 %collective-permute-start.4 = (bf16[20,32,128]{2,1,0:T(8,128)(2,1)S(1)}, bf16[20,32,128]{2,1,0:T(8,128)(2,1)S(1)}, u32[]{:S(2)}, u32[]{:S(2)}) collective-permute-start(bf16[20,32,128]{2,1,0:T(8,128)(2,1)S(1)} %collective-permute-done.refs_1_), channel_id=1, source_target_pairs={{0,64},{64,0},{128,192},{192,128},{256,320},{320,256},{384,448},{4... | collective-permute-start | bytes 491528 | tf_op jit(solution)/shard_map/ppermute | solution.py:203
  22.0 0.7 copy-start.5
  25.1 32.5 %all-to-all-start = ((s32[64,1,128]{2,1,0:T(1,128)}), s32[64,1,128]{2,1,0:T(1,128)S(1)}, u32[]{:S(2)}, u32[]{:S(2)}) async-start(s32[64,1,128]{2,1,0:T(1,128)} %get-tuple-element.8), calls=%async_computation | async-start | bytes 65536 | tf_op jit(solution)/shard_map/all_to_all | solution.py:195
  57.6 60.4 %copy-start.3 = (bf16[64,128]{1,0:T(8,128)(2,1)S(1)}, bf16[64,128]{1,0:T(8,128)(2,1)}, u32[]{:S(2)}) copy-start(bf16[64,128]{1,0:T(8,128)(2,1)} %value_ref.1) | copy-start | bytes 49156
  58.9 59.0 %copy-start = (bf16[64,128,64]{1,2,0:T(8,128)(2,1)S(1)}, bf16[64,128,64]{1,2,0:T(8,128)(2,1)}, u32[]{:S(2)}) copy-start(bf16[64,128,64]{1,2,0:T(8,128)(2,1)} %param.6) | copy-start | bytes 3145732
  58.9 59.0 %copy-start.1 = (bf16[64,128,64]{1,2,0:T(8,128)(2,1)S(1)}, bf16[64,128,64]{1,2,0:T(8,128)(2,1)}, u32[]{:S(2)}) copy-start(bf16[64,128,64]{1,2,0:T(8,128)(2,1)} %param.7) | copy-start | bytes 3145732
  58.9 59.0 %copy-start.4 = (s32[64]{0:T(128)S(1)}, s32[64]{0:T(128)}, u32[]{:S(2)}) copy-start(s32[64]{0:T(128)} %fill_ref.1) | copy-start | bytes 772
  184.4 4.0 %collective-permute-start.7 = (bf16[4,20,32,128]{3,2,1,0:T(8,128)(2,1)S(1)}, bf16[4,20,32,128]{3,2,1,0:T(8,128)(2,1)S(1)}, u32[]{:S(2)}, u32[]{:S(2)}) collective-permute-start(bf16[4,20,32,128]{3,2,1,0:T(8,128)(2,1)S(1)} %get-tuple-element.11), channel_id=1, source_target_pairs={{0,64},{64,0},{128,192},{192,128},{256,320},{320,256},{384,448},{4... | collective-permute-start | bytes 1966088 | tf_op jit(solution)/shard_map/ppermute | solution.py:203
  215.9 4.0 %collective-permute-start.8 = (bf16[4,20,32,128]{3,2,1,0:T(8,128)(2,1)S(1)}, bf16[4,20,32,128]{3,2,1,0:T(8,128)(2,1)S(1)}, u32[]{:S(2)}, u32[]{:S(2)}) collective-permute-start(bf16[4,20,32,128]{3,2,1,0:T(8,128)(2,1)S(1)} %all_to_all.33.near_ref), channel_id=1, source_target_pairs={{0,64},{64,0},{128,192},{192,128},{256,320},{320,256},{384,448},{4... | collective-permute-start | bytes 1966088 | tf_op jit(solution)/shard_map/ppermute | solution.py:203
  222.1 61.5 %all-to-all-start.5 = ((bf16[128,32,128]{2,1,0:T(8,128)(2,1)}), bf16[128,32,128]{2,1,0:T(8,128)(2,1)S(1)}, u32[]{:S(2)}, u32[]{:S(2)}) async-start(bf16[128,32,128]{2,1,0:T(8,128)(2,1)} %shard_map.84), calls=%async_computation.5 | async-start | bytes 2097152 | tf_op jit(solution)/shard_map/all_to_all | solution.py:195

commit v6 on v5

--- a/solution.py
+++ b/solution.py
@@ -64,22 +64,20 @@
     lax.fori_loop(0, out_ref.shape[0] // 8, step, 0, unroll=2)
 
 
-def rotated_kernel(me_ref, ids_ref, *refs):
-    pieces, out_ref, table_ref = refs[:-2], refs[-2], refs[-1]
-    groups, size = len(pieces), pieces[0].shape[0]
-    for i, piece in enumerate(pieces):
-        core, step = divmod(i, groups // 2)
-        place = lax.rem((me_ref[0] ^ core) + 2 * step, groups)
-        table_ref[pl.ds(place * size, size)] = piece[...]
-    pick_rows(ids_ref, table_ref, out_ref)
-
-
-def sided_kernel(me_ref, ids_ref, near_ref, far_ref, out_ref, table_ref):
-    size = near_ref.shape[1]
+def bundle_kernel(*refs):
+    pieces, out_ref = refs[:-1], refs[-1]
+    for k, piece in enumerate(pieces):
+        out_ref[k] = piece[...]
+
+
+def sided_kernel(turned, me_ref, ids_ref, near_ref, far_ref, out_ref, table_ref):
+    chips, size = near_ref.shape[:2]
     side = lax.rem(me_ref[0], 2)
-    for x in range(near_ref.shape[0]):
-        table_ref[pl.ds((2 * x + side) * size, size)] = near_ref[x]
-        table_ref[pl.ds((2 * x + 1 - side) * size, size)] = far_ref[x]
+    turn = lax.div(me_ref[0], 2) if turned else 0
+    for x in range(chips):
+        place = 2 * lax.rem(turn + x, chips)
+        table_ref[pl.ds((place + side) * size, size)] = near_ref[x]
+        table_ref[pl.ds((place + 1 - side) * size, size)] = far_ref[x]
     pick_rows(ids_ref, table_ref, out_ref)
 
 
@@ -162,13 +160,13 @@
     lax.fori_loop(0, left_ref.shape[0] // wide, step, 0)
 
 
-def call(kernel, in_specs, outs, scratch=(), out_specs=None, keep=True):
+def call(kernel, in_specs, outs, scratch=(), out_specs=None, loose=()):
     many = isinstance(outs, tuple)
     outs = outs if many else (outs,)
     specs = out_specs or (VMEM,) * len(outs)
     shapes = tuple(
-        pltpu.VMEM(out.shape, out.dtype) if keep and spec is VMEM else out
-        for out, spec in zip(outs, specs)
+        pltpu.VMEM(out.shape, out.dtype) if spec is VMEM and i not in loose else out
+        for i, (out, spec) in enumerate(zip(outs, specs))
     )
     run = pl.pallas_call(
         kernel,
@@ -204,8 +202,7 @@
 
 
 def spread(mine, groups):
-    near = [mine] + [shift(mine, groups, -k) for k in range(1, groups // 2)]
-    return near + [swap(piece, groups) for piece in near]
+    return [mine] + [shift(mine, groups, -k) for k in range(1, groups // 2)]
 
 
 def body(left, right, values, core, tile_slice, tile_fill):
@@ -244,9 +241,10 @@
     ids = exchange(wanted, "own")
     mine = call(pack_kernel, [VMEM], mine_sds)(core)
     pieces = spread(mine, groups)
+    near = call(bundle_kernel, [VMEM] * chips, sds(chip_shape, BF16))(*pieces)
     outgoing = call(
-        rotated_kernel, [SMEM] * 2 + [VMEM] * groups, slot_sds, [table_scr]
-    )(me, ids, *pieces)
+        functools.partial(sided_kernel, True), [SMEM] * 2 + [VMEM] * 2, slot_sds, [table_scr]
+    )(me, ids, near, swap(near, groups))
     got = exchange(outgoing, "own")
     grads = call(
         grad_kernel,
@@ -263,15 +261,16 @@
     )(ids, got_grads, me)
     joined = call(join_kernel, [VMEM] * 2, sds(chip_shape, BF16))(near, swap(far, groups))
     new_spread, new_core = call(
-        update_kernel, [VMEM] * 2, (sds(chip_shape, BF16), sds(core.shape, BF16))
+        update_kernel, [VMEM] * 2, (sds(chip_shape, BF16), sds(core.shape, BF16)), loose=(1,)
     )(mine, exchange_x(joined))
     new_near = exchange_x(new_spread)
     new_far = swap(new_near, groups)
-    outgoing = call(sided_kernel, [SMEM, SMEM, VMEM, VMEM], slot_sds, [table_scr])(
+    outgoing = call(
+        functools.partial(sided_kernel, False), [SMEM] * 2 + [VMEM] * 2, slot_sds, [table_scr])(
         me, ids, new_near, new_far
     )
     new_got = exchange(outgoing, "own")
-    new_left_t = call(refresh_kernel, [SMEM, VMEM, VMEM], sds(left_t.shape, BF16), keep=False)(
+    new_left_t = call(refresh_kernel, [SMEM, VMEM, VMEM], sds(left_t.shape, BF16), loose=(0,))(
         slot, left_t, new_got
     )
     return (new_core, jnp.swapaxes(new_left_t, 1, 2))

time: 288 us -> 285 us (0.990)
  blocking collectives: 146 us -> 208 us
  waiting for transfers between devices: 72.6 us -> 21.6 us
  starting transfers between devices: 48.6 us -> 35.9 us
    all_to_all x2 -> x3, blocking collectives: 119 us -> 181 us  [exchange(): return lax.all_to_all(x, axis, split_axis=0, concat_axis=0, tiled=True)]
    all_to_all x2 -> x1, waiting for transfers between devices: 68.5 us -> 13.6 us  [exchange(): return lax.all_to_all(x, axis, split_axis=0, concat_axis=0, tiled=True)]
    ppermute x6 -> x3, starting transfers between devices: 12.5 us -> 5.75 us  [swap(): return lax.ppermute(x, 'grp', [(g, g ^ 1) for g in range(groups)])]
    all_to_all x2 -> x1, starting transfers between devices: 24.7 us -> 18.7 us  [exchange(): return lax.all_to_all(x, axis, split_axis=0, concat_axis=0, tiled=True)]
    ppermute x3, waiting for transfers between devices: 0.01 us -> 3.91 us  [shift(): lax.ppermute(x, 'grp', [(g, (g + 2 * step) % groups) for g in range(group...]
    pallas_call x9 -> x10, Pallas kernels: 16.6 us -> 16.4 us  [place(): results = run(*placed)]
  transfers between devices with their start and end apart: 11 -> 7, of which waited for: 4 -> 5; matrix products, arithmetic and copies ran while one was open for 0% -> 0% of each run, Pallas kernels for 1% -> 1%
where the time goes in v6:
time: 285 us; the launch traced here: 284 us
  blocking collectives  208 us (73%)
  starting transfers between devices  35.9 us (13%)
  waiting for transfers between devices  21.6 us (8%)
  Pallas kernels  16.4 us (6%)
    all_to_all x3, blocking collectives, exchange(): return lax.all_to_all(x, axis, split_axis=0, concat_axis=0, tiled=True)  181 us
    all_to_all x2, blocking collectives, exchange_x(): lax.all_to_all(x, 'grp', split_axis=0, concat_axis=0, tiled=True, axis_in...  27.4 us
    all_to_all x1, starting transfers between devices, exchange(): return lax.all_to_all(x, axis, split_axis=0, concat_axis=0, tiled=True)  18.7 us
    pallas_call x10, Pallas kernels, place(): results = run(*placed)  16.4 us
    all_to_all x1, waiting for transfers between devices, exchange(): return lax.all_to_all(x, axis, split_axis=0, concat_axis=0, tiled=True)  13.6 us
    ppermute x3, starting transfers between devices, shift(): lax.ppermute(x, 'grp', [(g, (g + 2 * step) % groups) for g in range(group...  11.4 us
    ppermute x3, starting transfers between devices, swap(): return lax.ppermute(x, 'grp', [(g, g ^ 1) for g in range(groups)])  5.75 us
  transfers between devices with their start and end apart: 7, of which 5 were waited for; matrix products, arithmetic and copies ran while one was open for 0% of the time, Pallas kernels for 1%

profile of v6, /device:TPU:8, one launch (start us, length us, event | category | flops | bytes accessed | tf_op | source)
XLA Modules:
  0.0 284.0 jit_solution(932026990488438631)
XLA Ops:
  0.6 1.0 copy-done.2
  1.6 0.2 shard_map.77.refs_0_.table_ref
  1.8 3.4 %collective-permute-start.2 = (bf16[20,32,128]{2,1,0:T(8,128)(2,1)S(1)}, bf16[20,32,128]{2,1,0:T(8,128)(2,1)S(1)}, u32[]{:S(2)}, u32[]{:S(2)}) collective-permute-start(bf16[20,32,128]{2,1,0:T(8,128)(2,1)S(1)} %shard_map.77.refs_0_.table_ref), channel_id=1, source_target_pairs={{0,128},{64,192},{128,256},{192,320},{256,384},{320,448},{384,0},{... | collective-permute-start | bytes 491528 | tf_op jit(solution)/shard_map/ppermute | solution.py:197
  5.2 4.6 %collective-permute-start.1 = (bf16[20,32,128]{2,1,0:T(8,128)(2,1)S(1)}, bf16[20,32,128]{2,1,0:T(8,128)(2,1)S(1)}, u32[]{:S(2)}, u32[]{:S(2)}) collective-permute-start(bf16[20,32,128]{2,1,0:T(8,128)(2,1)S(1)} %shard_map.77.refs_0_.table_ref), channel_id=1, source_target_pairs={{0,256},{64,320},{128,384},{192,448},{256,0},{320,64},{384,128},{4... | collective-permute-start | bytes 491528 | tf_op jit(solution)/shard_map/ppermute | solution.py:197
  9.9 3.3 %collective-permute-start = (bf16[20,32,128]{2,1,0:T(8,128)(2,1)S(1)}, bf16[20,32,128]{2,1,0:T(8,128)(2,1)S(1)}, u32[]{:S(2)}, u32[]{:S(2)}) collective-permute-start(bf16[20,32,128]{2,1,0:T(8,128)(2,1)S(1)} %shard_map.77.refs_0_.table_ref), channel_id=1, source_target_pairs={{0,384},{64,448},{128,0},{192,64},{256,128},{320,192},{384,256},{4... | collective-permute-start | bytes 491528 | tf_op jit(solution)/shard_map/ppermute | solution.py:197
  13.2 0.0 collective-permute-done.2.refs_3_
  13.3 2.1 collective-permute-done.1.refs_2_
  15.4 1.8 collective-permute-done.refs_1_
  17.2 1.9 collective-permute-start.3
  19.2 2.4 shard_map.78
  21.6 18.7 %all-to-all-start = ((s32[64,1,128]{2,1,0:T(1,128)}), s32[64,1,128]{2,1,0:T(1,128)S(1)}, u32[]{:S(2)}, u32[]{:S(2)}) async-start(s32[64,1,128]{2,1,0:T(1,128)} %get-tuple-element.8), calls=%async_computation | async-start | bytes 65536 | tf_op jit(solution)/shard_map/all_to_all | solution.py:193
  40.3 13.6 %all-to-all-done.ids_ref = s32[64,1,128]{2,1,0:T(1,128)S(1)} async-done(((s32[64,1,128]{2,1,0:T(1,128)}), s32[64,1,128]{2,1,0:T(1,128)S(1)}, u32[]{:S(2)}, u32[]{:S(2)}) %all-to-all-start) | async-done | bytes 32800 | tf_op jit(solution)/shard_map/all_to_all | solution.py:193
  53.9 0.0 collective-permute-done.3.far_ref
  53.9 1.3 shard_map.80
  55.3 0.0 copy-start
  55.3 0.0 copy-start.1
  55.3 0.0 copy-start.4
  55.3 59.6 %all_to_all.30.slice_ref = bf16[128,32,128]{2,1,0:T(8,128)(2,1)S(1)} all-to-all(bf16[128,32,128]{2,1,0:T(8,128)(2,1)S(1)} %shard_map.80), channel_id=1, replica_groups=mesh['grp'=8,'own'=64] {'own'}, dimensions={0} | all-to-all | bytes 2097152 | tf_op jit(solution)/shard_map/all_to_all | solution.py:193
  115.0 4.5 %shard_map.81 = bf16[128,32,128]{2,1,0:T(8,128)(2,1)S(1)} custom-call(s32[64]{0:T(128)S(1)} %get-tuple-element.9.slot_ref, s32[64]{0:T(128)S(1)} %copy-done.4, bf16[64,64,128]{2,1,0:T(8,128)(2,1)S(1)} %bitcast.4, bf16[64,64,128]{2,1,0:T(8,128)(2,1)S(1)} %bitcast.6, bf16[64,128]{1,0:T(8,128)(2,1)S(1)} %copy-done.3, bf16[128,32,128]{2,1,0:T(8,128)(2,1)S(1)} %all_to_all.30.slice_ref), custom_call_target="tpu_custom_call" | custom-call | flops 1000000 | bytes 4000000 | tf_op jit(solution)/shard_map/pallas_call | solution.py:186
  119.4 60.0 %all_to_all.31.grad_ref = bf16[128,32,128]{2,1,0:T(8,128)(2,1)S(1)} all-to-all(bf16[128,32,128]{2,1,0:T(8,128)(2,1)S(1)} %shard_map.81), channel_id=1, replica_groups=mesh['grp'=8,'own'=64] {'own'}, dimensions={0} | all-to-all | bytes 2097152 | tf_op jit(solution)/shard_map/all_to_all | solution.py:193
  179.4 2.0 shard_map.82
  181.4 1.9 collective-permute-start.4
  183.3 2.1 collective-permute-done.4.other_ref
  185.4 0.1 shard_map.83
  185.5 15.0 %all_to_all.32.part_ref = bf16[4,20,32,128]{3,2,1,0:T(8,128)(2,1)S(1)} all-to-all(bf16[4,20,32,128]{3,2,1,0:T(8,128)(2,1)S(1)} %shard_map.83), channel_id=1, replica_groups={{0,128,256,384},{64,192,320,448},{1,129,257,385},{65,193,321,449},{2,13..., dimensions={0} | all-to-all | bytes 1310720 | tf_op jit(solution)/shard_map/all_to_all | solution.py:228
  200.5 1.1 shard_map.84
  201.7 12.4 %all_to_all.33.near_ref = bf16[4,20,32,128]{3,2,1,0:T(8,128)(2,1)S(1)} all-to-all(bf16[4,20,32,128]{3,2,1,0:T(8,128)(2,1)S(1)} %get-tuple-element.13), channel_id=1, replica_groups={{0,128,256,384},{64,192,320,448},{1,129,257,385},{65,193,321,449},{2,13..., dimensions={0} | all-to-all | bytes 1310720 | tf_op jit(solution)/shard_map/all_to_all | solution.py:228
  214.1 1.9 collective-permute-start.5
  216.0 2.1 collective-permute-done.5.far_ref
  218.1 1.3 shard_map.85
  219.4 61.2 %all_to_all.34.slice_ref = bf16[128,32,128]{2,1,0:T(8,128)(2,1)S(1)} all-to-all(bf16[128,32,128]{2,1,0:T(8,128)(2,1)S(1)} %shard_map.85), channel_id=1, replica_groups=mesh['grp'=8,'own'=64] {'own'}, dimensions={0} | all-to-all | bytes 2097152 | tf_op jit(solution)/shard_map/all_to_all | solution.py:193
  280.7 3.3 %shard_map.86 = bf16[64,64,128]{2,1,0:T(8,128)(2,1)} custom-call(s32[64]{0:T(128)S(1)} %get-tuple-element.9.slot_ref, bf16[64,64,128]{2,1,0:T(8,128)(2,1)S(1)} %bitcast.5, bf16[128,32,128]{2,1,0:T(8,128)(2,1)S(1)} %all_to_all.34.slice_ref), custom_call_target="tpu_custom_call" | custom-call | flops 1000000 | bytes 4000000 | tf_op jit(solution)/shard_map/pallas_call | solution.py:186
  (9 shorter events, 0.1 us)
Async XLA Ops:
  0.6 1.0 copy-start.2
  1.6 17.5 %copy-start.5 = (s32[64]{0:T(128)S(1)}, s32[64]{0:T(128)}, u32[]{:S(2)}) copy-start(s32[64]{0:T(128)} %tile_slice_ref.1) | copy-start | bytes 772
  1.8 11.4 %collective-permute-start.2 = (bf16[20,32,128]{2,1,0:T(8,128)(2,1)S(1)}, bf16[20,32,128]{2,1,0:T(8,128)(2,1)S(1)}, u32[]{:S(2)}, u32[]{:S(2)}) collective-permute-start(bf16[20,32,128]{2,1,0:T(8,128)(2,1)S(1)} %shard_map.77.refs_0_.table_ref), channel_id=1, source_target_pairs={{0,128},{64,192},{128,256},{192,320},{256,384},{320,448},{384,0},{... | collective-permute-start | bytes 491528 | tf_op jit(solution)/shard_map/ppermute | solution.py:197
  5.2 10.1 %collective-permute-start.1 = (bf16[20,32,128]{2,1,0:T(8,128)(2,1)S(1)}, bf16[20,32,128]{2,1,0:T(8,128)(2,1)S(1)}, u32[]{:S(2)}, u32[]{:S(2)}) collective-permute-start(bf16[20,32,128]{2,1,0:T(8,128)(2,1)S(1)} %shard_map.77.refs_0_.table_ref), channel_id=1, source_target_pairs={{0,256},{64,320},{128,384},{192,448},{256,0},{320,64},{384,128},{4... | collective-permute-start | bytes 491528 | tf_op jit(solution)/shard_map/ppermute | solution.py:197
  9.9 7.3 %collective-permute-start = (bf16[20,32,128]{2,1,0:T(8,128)(2,1)S(1)}, bf16[20,32,128]{2,1,0:T(8,128)(2,1)S(1)}, u32[]{:S(2)}, u32[]{:S(2)}) collective-permute-start(bf16[20,32,128]{2,1,0:T(8,128)(2,1)S(1)} %shard_map.77.refs_0_.table_ref), channel_id=1, source_target_pairs={{0,384},{64,448},{128,0},{192,64},{256,128},{320,192},{384,256},{4... | collective-permute-start | bytes 491528 | tf_op jit(solution)/shard_map/ppermute | solution.py:197
  17.2 36.7 %collective-permute-start.3 = (bf16[4,20,32,128]{3,2,1,0:T(8,128)(2,1)S(1)}, bf16[4,20,32,128]{3,2,1,0:T(8,128)(2,1)S(1)}, u32[]{:S(2)}, u32[]{:S(2)}) collective-permute-start(bf16[4,20,32,128]{3,2,1,0:T(8,128)(2,1)S(1)} %shard_map.79.near_ref), channel_id=1, source_target_pairs={{0,64},{64,0},{128,192},{192,128},{256,320},{320,256},{384,448},{4... | collective-permute-start | bytes 1966088 | tf_op jit(solution)/shard_map/ppermute | solution.py:201
  21.6 32.3 %all-to-all-start = ((s32[64,1,128]{2,1,0:T(1,128)}), s32[64,1,128]{2,1,0:T(1,128)S(1)}, u32[]{:S(2)}, u32[]{:S(2)}) async-start(s32[64,1,128]{2,1,0:T(1,128)} %get-tuple-element.8), calls=%async_computation | async-start | bytes 65536 | tf_op jit(solution)/shard_map/all_to_all | solution.py:193
  53.9 61.0 %copy-start.3 = (bf16[64,128]{1,0:T(8,128)(2,1)S(1)}, bf16[64,128]{1,0:T(8,128)(2,1)}, u32[]{:S(2)}) copy-start(bf16[64,128]{1,0:T(8,128)(2,1)} %value_ref.1) | copy-start | bytes 49156
  55.3 59.7 %copy-start = (bf16[64,128,64]{1,2,0:T(8,128)(2,1)S(1)}, bf16[64,128,64]{1,2,0:T(8,128)(2,1)}, u32[]{:S(2)}) copy-start(bf16[64,128,64]{1,2,0:T(8,128)(2,1)} %param.6) | copy-start | bytes 3145732
  55.3 59.6 %copy-start.1 = (bf16[64,128,64]{1,2,0:T(8,128)(2,1)S(1)}, bf16[64,128,64]{1,2,0:T(8,128)(2,1)}, u32[]{:S(2)}) copy-start(bf16[64,128,64]{1,2,0:T(8,128)(2,1)} %param.7) | copy-start | bytes 3145732
  55.3 59.6 %copy-start.4 = (s32[64]{0:T(128)S(1)}, s32[64]{0:T(128)}, u32[]{:S(2)}) copy-start(s32[64]{0:T(128)} %fill_ref.1) | copy-start | bytes 772
  181.4 4.0 %collective-permute-start.4 = (bf16[4,20,32,128]{3,2,1,0:T(8,128)(2,1)S(1)}, bf16[4,20,32,128]{3,2,1,0:T(8,128)(2,1)S(1)}, u32[]{:S(2)}, u32[]{:S(2)}) collective-permute-start(bf16[4,20,32,128]{3,2,1,0:T(8,128)(2,1)S(1)} %get-tuple-element.11), channel_id=1, source_target_pairs={{0,64},{64,0},{128,192},{192,128},{256,320},{320,256},{384,448},{4... | collective-permute-start | bytes 1966088 | tf_op jit(solution)/shard_map/ppermute | solution.py:201
  214.1 4.0 %collective-permute-start.5 = (bf16[4,20,32,128]{3,2,1,0:T(8,128)(2,1)S(1)}, bf16[4,20,32,128]{3,2,1,0:T(8,128)(2,1)S(1)}, u32[]{:S(2)}, u32[]{:S(2)}) collective-permute-start(bf16[4,20,32,128]{3,2,1,0:T(8,128)(2,1)S(1)} %all_to_all.33.near_ref), channel_id=1, source_target_pairs={{0,64},{64,0},{128,192},{192,128},{256,320},{320,256},{384,448},{4... | collective-permute-start | bytes 1966088 | tf_op jit(solution)/shard_map/ppermute | solution.py:201

commit v7 on v6

--- a/solution.py
+++ b/solution.py
@@ -10,6 +10,7 @@
 
 VMEM = pl.BlockSpec(memory_space=pltpu.VMEM)
 SMEM = pl.BlockSpec(memory_space=pltpu.SMEM)
+HBM = pl.BlockSpec(memory_space=pltpu.HBM)
 BF16 = jnp.bfloat16
 F32 = jnp.float32
 
@@ -24,13 +25,13 @@
     return jnp.concatenate([packed[:, :width], packed[:, width:]], axis=0)
 
 
-def pack_kernel(core_ref, out_ref):
-    for i in range(core_ref.shape[0]):
-        out_ref[i] = pack(core_ref[i].astype(F32).T).astype(BF16)
-
-
-def index_kernel(owners, groups, per_device, tile_slice_ref, slot_ref, wanted_ref, count_ref):
+def prepare_kernel(
+    owners, groups, tile_slice_ref, core_ref, slot_ref, wanted_ref, out_ref, count_ref, core_scr, sem
+):
+    per_device = core_ref.shape[0]
     dead = groups * per_device
+    fetch = pltpu.make_async_copy(core_ref, core_scr, sem)
+    fetch.start()
 
     def clear(c, carry):
         count_ref[c] = 0
@@ -45,11 +46,14 @@
         rank = count_ref[owner]
         count_ref[owner] = rank + 1
         slot_ref[t] = 2 * owner + rank
-        wanted_ref[owner, 0, rank] = group * per_device + tile_slice_ref[t] - block * per_device
+        wanted_ref[owner, 0, rank] = (group - block) * per_device + tile_slice_ref[t]
         return carry
 
     lax.fori_loop(0, owners, clear, 0, unroll=8)
     lax.fori_loop(0, slot_ref.shape[0], place, 0, unroll=8)
+    fetch.wait()
+    for i in range(per_device):
+        out_ref[i] = pack(core_scr[i].astype(F32).T).astype(BF16)
 
 
 def pick_rows(ids_ref, table_ref, out_ref):
@@ -84,7 +88,7 @@
 def grad_kernel(slot_ref, fill_ref, left_ref, right_ref, value_ref, slice_ref, out_ref, value_scr):
     value_scr[...] = value_ref[...].astype(F32)
     lanes = lax.broadcasted_iota(jnp.int32, (1, left_ref.shape[2]), 1)
-    wide = 8
+    wide = left_ref.shape[0]
 
     def step(k, carry):
         tiles = [wide * k + i for i in range(wide)]
@@ -145,7 +149,7 @@
 
 
 def refresh_kernel(slot_ref, left_ref, slice_ref, out_ref):
-    wide = 8
+    wide = left_ref.shape[0]
 
     def step(k, carry):
         tiles = [wide * k + i for i in range(wide)]
@@ -180,7 +184,7 @@
 
     def place(*args):
         placed = [
-            pltpu.with_memory_space_constraint(arg, pltpu.VMEM) if spec is VMEM else arg
+            arg if spec is SMEM else pltpu.with_memory_space_constraint(arg, spec.memory_space)
             for arg, spec in zip(args, in_specs)
         ]
         results = run(*placed)
@@ -199,10 +203,6 @@
 
 def swap(x, groups):
     return lax.ppermute(x, "grp", [(g, g ^ 1) for g in range(groups)])
-
-
-def spread(mine, groups):
-    return [mine] + [shift(mine, groups, -k) for k in range(1, groups // 2)]
 
 
 def body(left, right, values, core, tile_slice, tile_fill):
@@ -231,16 +231,21 @@
 
     me = lax.axis_index("grp").astype(jnp.int32).reshape(1)
 
-    slot, wanted = call(
-        functools.partial(index_kernel, owners, groups, per_device),
-        [SMEM],
-        (sds((tiles,), jnp.int32), sds((owners, 1, 128), jnp.int32)),
-        [pltpu.SMEM((owners,), jnp.int32)],
-        (SMEM, SMEM),
-    )(tile_slice)
+    slot, wanted, mine = call(
+        functools.partial(prepare_kernel, owners, groups),
+        [SMEM, HBM],
+        (sds((tiles,), jnp.int32), sds((owners, 1, 128), jnp.int32), mine_sds),
+        [
+            pltpu.SMEM((owners,), jnp.int32),
+            pltpu.VMEM(core.shape, BF16),
+            pltpu.SemaphoreType.DMA,
+        ],
+        (SMEM, SMEM, VMEM),
+    )(pltpu.with_memory_space_constraint(tile_slice, pltpu.HBM), core)
+    distant = {k: shift(mine, groups, -k) for k in range(2, chips, 2)}
     ids = exchange(wanted, "own")
-    mine = call(pack_kernel, [VMEM], mine_sds)(core)
-    pieces = spread(mine, groups)
+    adjacent = {k: shift(mine, groups, -k) for k in range(1, chips, 2)}
+    pieces = [mine] + [{**distant, **adjacent}[k] for k in range(1, chips)]
     near = call(bundle_kernel, [VMEM] * chips, sds(chip_shape, BF16))(*pieces)
     outgoing = call(
         functools.partial(sided_kernel, True), [SMEM] * 2 + [VMEM] * 2, slot_sds, [table_scr]
@@ -270,9 +275,7 @@
         me, ids, new_near, new_far
     )
     new_got = exchange(outgoing, "own")
-    new_left_t = call(refresh_kernel, [SMEM, VMEM, VMEM], sds(left_t.shape, BF16), loose=(0,))(
-        slot, left_t, new_got
-    )
+    new_left_t = call(refresh_kernel, [SMEM, VMEM, VMEM], sds(left_t.shape, BF16), loose=(0,))(slot, left_t, new_got)
     return (new_core, jnp.swapaxes(new_left_t, 1, 2))
 
 

time: 285 us -> 280 us (0.982)
  Pallas kernels: 16.4 us -> 12.5 us
    pallas_call x10 -> x9, Pallas kernels: 16.4 us -> 12.5 us  [place(): results = run(*placed)]
  transfers between devices with their start and end apart: 7 -> 7, of which waited for: 5 -> 5; matrix products, arithmetic and copies ran while one was open for 0% -> 0% of each run, Pallas kernels for 1% -> 0%
where the time goes in v7:
time: 280 us; the launch traced here: 279 us
  blocking collectives  208 us (74%)
  starting transfers between devices  35.9 us (13%)
  waiting for transfers between devices  21.6 us (8%)
  Pallas kernels  12.5 us (4%)
    all_to_all x3, blocking collectives, exchange(): return lax.all_to_all(x, axis, split_axis=0, concat_axis=0, tiled=True)  181 us
    all_to_all x2, blocking collectives, exchange_x(): lax.all_to_all(x, 'grp', split_axis=0, concat_axis=0, tiled=True, axis_in...  27.4 us
    all_to_all x1, starting transfers between devices, exchange(): return lax.all_to_all(x, axis, split_axis=0, concat_axis=0, tiled=True)  18.7 us
    all_to_all x1, waiting for transfers between devices, exchange(): return lax.all_to_all(x, axis, split_axis=0, concat_axis=0, tiled=True)  13.6 us
    pallas_call x9, Pallas kernels, place(): results = run(*placed)  12.5 us
    ppermute x3, starting transfers between devices, shift(): lax.ppermute(x, 'grp', [(g, (g + 2 * step) % groups) for g in range(group...  11.4 us
    ppermute x3, starting transfers between devices, swap(): return lax.ppermute(x, 'grp', [(g, g ^ 1) for g in range(groups)])  5.75 us
  transfers between devices with their start and end apart: 7, of which 5 were waited for; matrix products, arithmetic and copies ran while one was open for 0% of the time, Pallas kernels for 0%

profile of v7, /device:TPU:8, one launch (start us, length us, event | category | flops | bytes accessed | tf_op | source)
XLA Modules:
  0.0 279.1 jit_solution(17050692223393564208)
XLA Ops:
  0.6 2.7 shard_map.77
  3.3 3.4 %collective-permute-start.2 = (bf16[20,32,128]{2,1,0:T(8,128)(2,1)S(1)}, bf16[20,32,128]{2,1,0:T(8,128)(2,1)S(1)}, u32[]{:S(2)}, u32[]{:S(2)}) collective-permute-start(bf16[20,32,128]{2,1,0:T(8,128)(2,1)S(1)} %get-tuple-element.9.refs_0_.table_ref), channel_id=1, source_target_pairs={{0,128},{64,192},{128,256},{192,320},{256,384},{320,448},{384,0},{... | collective-permute-start | bytes 491528 | tf_op jit(solution)/shard_map/ppermute | solution.py:201
  6.8 4.6 %collective-permute-start.1 = (bf16[20,32,128]{2,1,0:T(8,128)(2,1)S(1)}, bf16[20,32,128]{2,1,0:T(8,128)(2,1)S(1)}, u32[]{:S(2)}, u32[]{:S(2)}) collective-permute-start(bf16[20,32,128]{2,1,0:T(8,128)(2,1)S(1)} %get-tuple-element.9.refs_0_.table_ref), channel_id=1, source_target_pairs={{0,256},{64,320},{128,384},{192,448},{256,0},{320,64},{384,128},{4... | collective-permute-start | bytes 491528 | tf_op jit(solution)/shard_map/ppermute | solution.py:201
  11.4 3.3 %collective-permute-start = (bf16[20,32,128]{2,1,0:T(8,128)(2,1)S(1)}, bf16[20,32,128]{2,1,0:T(8,128)(2,1)S(1)}, u32[]{:S(2)}, u32[]{:S(2)}) collective-permute-start(bf16[20,32,128]{2,1,0:T(8,128)(2,1)S(1)} %get-tuple-element.9.refs_0_.table_ref), channel_id=1, source_target_pairs={{0,384},{64,448},{128,0},{192,64},{256,128},{320,192},{384,256},{4... | collective-permute-start | bytes 491528 | tf_op jit(solution)/shard_map/ppermute | solution.py:201
  14.8 0.0 collective-permute-done.2.refs_3_
  14.8 2.1 collective-permute-done.1.refs_2_
  16.9 1.8 collective-permute-done.refs_1_
  18.7 1.9 collective-permute-start.3
  20.6 18.7 %all-to-all-start = ((s32[64,1,128]{2,1,0:T(1,128)}), s32[64,1,128]{2,1,0:T(1,128)S(1)}, u32[]{:S(2)}, u32[]{:S(2)}) async-start(s32[64,1,128]{2,1,0:T(1,128)} %get-tuple-element.10), calls=%async_computation | async-start | bytes 65536 | tf_op jit(solution)/shard_map/all_to_all | solution.py:197
  39.4 13.6 %all-to-all-done.ids_ref = s32[64,1,128]{2,1,0:T(1,128)S(1)} async-done(((s32[64,1,128]{2,1,0:T(1,128)}), s32[64,1,128]{2,1,0:T(1,128)S(1)}, u32[]{:S(2)}, u32[]{:S(2)}) %all-to-all-start) | async-done | bytes 32800 | tf_op jit(solution)/shard_map/all_to_all | solution.py:197
  53.0 0.0 collective-permute-done.3.far_ref
  53.0 1.3 shard_map.79
  54.3 0.0 copy-start
  54.4 0.0 copy-start.1
  54.4 0.0 copy-start.3
  54.4 59.6 %all_to_all.30.slice_ref = bf16[128,32,128]{2,1,0:T(8,128)(2,1)S(1)} all-to-all(bf16[128,32,128]{2,1,0:T(8,128)(2,1)S(1)} %shard_map.79), channel_id=1, replica_groups=mesh['grp'=8,'own'=64] {'own'}, dimensions={0} | all-to-all | bytes 2097152 | tf_op jit(solution)/shard_map/all_to_all | solution.py:197
  114.0 0.0 copy-done.2
  114.0 0.0 copy-done
  114.0 1.8 shard_map.80
  115.8 60.0 %all_to_all.31.grad_ref = bf16[128,32,128]{2,1,0:T(8,128)(2,1)S(1)} all-to-all(bf16[128,32,128]{2,1,0:T(8,128)(2,1)S(1)} %shard_map.80), channel_id=1, replica_groups=mesh['grp'=8,'own'=64] {'own'}, dimensions={0} | all-to-all | bytes 2097152 | tf_op jit(solution)/shard_map/all_to_all | solution.py:197
  175.8 2.0 shard_map.81
  177.8 1.9 collective-permute-start.4
  179.7 2.1 collective-permute-done.4.other_ref
  181.8 0.1 shard_map.82
  181.9 15.0 %all_to_all.32.part_ref = bf16[4,20,32,128]{3,2,1,0:T(8,128)(2,1)S(1)} all-to-all(bf16[4,20,32,128]{3,2,1,0:T(8,128)(2,1)S(1)} %shard_map.82), channel_id=1, replica_groups={{0,128,256,384},{64,192,320,448},{1,129,257,385},{65,193,321,449},{2,13..., dimensions={0} | all-to-all | bytes 1310720 | tf_op jit(solution)/shard_map/all_to_all | solution.py:228
  196.9 1.1 shard_map.83
  198.1 12.4 %all_to_all.33.near_ref = bf16[4,20,32,128]{3,2,1,0:T(8,128)(2,1)S(1)} all-to-all(bf16[4,20,32,128]{3,2,1,0:T(8,128)(2,1)S(1)} %get-tuple-element.15), channel_id=1, replica_groups={{0,128,256,384},{64,192,320,448},{1,129,257,385},{65,193,321,449},{2,13..., dimensions={0} | all-to-all | bytes 1310720 | tf_op jit(solution)/shard_map/all_to_all | solution.py:228
  210.5 1.9 collective-permute-start.5
  212.4 2.1 collective-permute-done.5.far_ref
  214.5 1.3 shard_map.84
  215.8 61.2 %all_to_all.34.slice_ref = bf16[128,32,128]{2,1,0:T(8,128)(2,1)S(1)} all-to-all(bf16[128,32,128]{2,1,0:T(8,128)(2,1)S(1)} %shard_map.84), channel_id=1, replica_groups=mesh['grp'=8,'own'=64] {'own'}, dimensions={0} | all-to-all | bytes 2097152 | tf_op jit(solution)/shard_map/all_to_all | solution.py:197
  277.1 2.0 shard_map.85
  (4 shorter events, 0.0 us)
Async XLA Ops:
  3.3 11.4 %collective-permute-start.2 = (bf16[20,32,128]{2,1,0:T(8,128)(2,1)S(1)}, bf16[20,32,128]{2,1,0:T(8,128)(2,1)S(1)}, u32[]{:S(2)}, u32[]{:S(2)}) collective-permute-start(bf16[20,32,128]{2,1,0:T(8,128)(2,1)S(1)} %get-tuple-element.9.refs_0_.table_ref), channel_id=1, source_target_pairs={{0,128},{64,192},{128,256},{192,320},{256,384},{320,448},{384,0},{... | collective-permute-start | bytes 491528 | tf_op jit(solution)/shard_map/ppermute | solution.py:201
  6.8 10.1 %collective-permute-start.1 = (bf16[20,32,128]{2,1,0:T(8,128)(2,1)S(1)}, bf16[20,32,128]{2,1,0:T(8,128)(2,1)S(1)}, u32[]{:S(2)}, u32[]{:S(2)}) collective-permute-start(bf16[20,32,128]{2,1,0:T(8,128)(2,1)S(1)} %get-tuple-element.9.refs_0_.table_ref), channel_id=1, source_target_pairs={{0,256},{64,320},{128,384},{192,448},{256,0},{320,64},{384,128},{4... | collective-permute-start | bytes 491528 | tf_op jit(solution)/shard_map/ppermute | solution.py:201
  11.4 7.3 %collective-permute-start = (bf16[20,32,128]{2,1,0:T(8,128)(2,1)S(1)}, bf16[20,32,128]{2,1,0:T(8,128)(2,1)S(1)}, u32[]{:S(2)}, u32[]{:S(2)}) collective-permute-start(bf16[20,32,128]{2,1,0:T(8,128)(2,1)S(1)} %get-tuple-element.9.refs_0_.table_ref), channel_id=1, source_target_pairs={{0,384},{64,448},{128,0},{192,64},{256,128},{320,192},{384,256},{4... | collective-permute-start | bytes 491528 | tf_op jit(solution)/shard_map/ppermute | solution.py:201
  18.7 34.3 %collective-permute-start.3 = (bf16[4,20,32,128]{3,2,1,0:T(8,128)(2,1)S(1)}, bf16[4,20,32,128]{3,2,1,0:T(8,128)(2,1)S(1)}, u32[]{:S(2)}, u32[]{:S(2)}) collective-permute-start(bf16[4,20,32,128]{3,2,1,0:T(8,128)(2,1)S(1)} %shard_map.78.near_ref), channel_id=1, source_target_pairs={{0,64},{64,0},{128,192},{192,128},{256,320},{320,256},{384,448},{4... | collective-permute-start | bytes 1966088 | tf_op jit(solution)/shard_map/ppermute | solution.py:205
  20.6 32.3 %all-to-all-start = ((s32[64,1,128]{2,1,0:T(1,128)}), s32[64,1,128]{2,1,0:T(1,128)S(1)}, u32[]{:S(2)}, u32[]{:S(2)}) async-start(s32[64,1,128]{2,1,0:T(1,128)} %get-tuple-element.10), calls=%async_computation | async-start | bytes 65536 | tf_op jit(solution)/shard_map/all_to_all | solution.py:197
  53.0 61.0 %copy-start.2 = (bf16[64,128]{1,0:T(8,128)(2,1)S(1)}, bf16[64,128]{1,0:T(8,128)(2,1)}, u32[]{:S(2)}) copy-start(bf16[64,128]{1,0:T(8,128)(2,1)} %value_ref.1) | copy-start | bytes 49156
  54.3 59.7 %copy-start = (bf16[64,128,64]{1,2,0:T(8,128)(2,1)S(1)}, bf16[64,128,64]{1,2,0:T(8,128)(2,1)}, u32[]{:S(2)}) copy-start(bf16[64,128,64]{1,2,0:T(8,128)(2,1)} %param.6) | copy-start | bytes 3145732
  54.4 59.6 %copy-start.1 = (bf16[64,128,64]{1,2,0:T(8,128)(2,1)S(1)}, bf16[64,128,64]{1,2,0:T(8,128)(2,1)}, u32[]{:S(2)}) copy-start(bf16[64,128,64]{1,2,0:T(8,128)(2,1)} %param.7) | copy-start | bytes 3145732
  54.4 59.6 %copy-start.3 = (s32[64]{0:T(128)S(1)}, s32[64]{0:T(128)}, u32[]{:S(2)}) copy-start(s32[64]{0:T(128)} %fill_ref.1) | copy-start | bytes 772
  177.8 4.0 %collective-permute-start.4 = (bf16[4,20,32,128]{3,2,1,0:T(8,128)(2,1)S(1)}, bf16[4,20,32,128]{3,2,1,0:T(8,128)(2,1)S(1)}, u32[]{:S(2)}, u32[]{:S(2)}) collective-permute-start(bf16[4,20,32,128]{3,2,1,0:T(8,128)(2,1)S(1)} %get-tuple-element.13), channel_id=1, source_target_pairs={{0,64},{64,0},{128,192},{192,128},{256,320},{320,256},{384,448},{4... | collective-permute-start | bytes 1966088 | tf_op jit(solution)/shard_map/ppermute | solution.py:205
  210.5 4.0 %collective-permute-start.5 = (bf16[4,20,32,128]{3,2,1,0:T(8,128)(2,1)S(1)}, bf16[4,20,32,128]{3,2,1,0:T(8,128)(2,1)S(1)}, u32[]{:S(2)}, u32[]{:S(2)}) collective-permute-start(bf16[4,20,32,128]{3,2,1,0:T(8,128)(2,1)S(1)} %all_to_all.33.near_ref), channel_id=1, source_target_pairs={{0,64},{64,0},{128,192},{192,128},{256,320},{320,256},{384,448},{4... | collective-permute-start | bytes 1966088 | tf_op jit(solution)/shard_map/ppermute | solution.py:205

commit v8 on v7

--- a/solution.py
+++ b/solution.py
@@ -13,6 +13,7 @@
 HBM = pl.BlockSpec(memory_space=pltpu.HBM)
 BF16 = jnp.bfloat16
 F32 = jnp.float32
+SHIFT = 16
 
 
 def pack(square):
@@ -26,31 +27,37 @@
 
 
 def prepare_kernel(
-    owners, groups, tile_slice_ref, core_ref, slot_ref, wanted_ref, out_ref, count_ref, core_scr, sem
+    owners, groups, tiles_ref, core_ref, slot_ref, wanted_ref, out_ref, core_scr, index_scr, sem, index_sem
 ):
-    per_device = core_ref.shape[0]
-    dead = groups * per_device
+    fetch_index = pltpu.make_async_copy(tiles_ref, index_scr, index_sem)
+    fetch_index.start()
     fetch = pltpu.make_async_copy(core_ref, core_scr, sem)
     fetch.start()
-
-    def clear(c, carry):
-        count_ref[c] = 0
-        wanted_ref[c, 0, 0] = dead
-        wanted_ref[c, 0, 1] = dead
-        return carry
-
-    def place(t, carry):
-        block = lax.div(tile_slice_ref[t], per_device)
-        owner = lax.rem(block, owners)
-        group = lax.div(block, owners)
-        rank = count_ref[owner]
-        count_ref[owner] = rank + 1
-        slot_ref[t] = 2 * owner + rank
-        wanted_ref[owner, 0, rank] = (group - block) * per_device + tile_slice_ref[t]
-        return carry
-
-    lax.fori_loop(0, owners, clear, 0, unroll=8)
-    lax.fori_loop(0, slot_ref.shape[0], place, 0, unroll=8)
+    per_device = core_ref.shape[0]
+    tiles = tiles_ref.shape[1]
+    magic = -(-(2**SHIFT) // per_device)
+    fetch_index.wait()
+    index = index_scr[...]
+    block = lax.shift_right_logical(index * magic, SHIFT)
+    group = lax.shift_right_logical(block * -(-(2**SHIFT) // owners), SHIFT)
+    owner = block - group * owners
+    local = (group - block) * per_device + index
+
+    mine = jnp.broadcast_to(owner.astype(F32), (tiles, tiles))
+    row = lax.broadcasted_iota(jnp.int32, (tiles, tiles), 0)
+    col = lax.broadcasted_iota(jnp.int32, (tiles, tiles), 1)
+    earlier = jnp.where((mine == mine.T) & (row < col), 1, 0)
+    slot = 2 * owner + jnp.sum(earlier, axis=0, keepdims=True)
+    slot_ref[...] = slot
+
+    dead = groups * per_device
+    lane = lax.broadcasted_iota(jnp.int32, wanted_ref.shape, 1)
+    seat = 2 * lax.broadcasted_iota(jnp.int32, (owners, tiles), 0)
+    asked = [
+        jnp.sum(jnp.where(slot == seat + r, local - dead, 0), axis=1, keepdims=True) + dead
+        for r in range(2)
+    ]
+    wanted_ref[...] = jnp.where(lane == 0, asked[0], asked[1])
     fetch.wait()
     for i in range(per_device):
         out_ref[i] = pack(core_scr[i].astype(F32).T).astype(BF16)
@@ -233,17 +240,18 @@
 
     slot, wanted, mine = call(
         functools.partial(prepare_kernel, owners, groups),
-        [SMEM, HBM],
-        (sds((tiles,), jnp.int32), sds((owners, 1, 128), jnp.int32), mine_sds),
+        [HBM, HBM],
+        (sds((1, tiles), jnp.int32), sds((owners, 128), jnp.int32), mine_sds),
         [
-            pltpu.SMEM((owners,), jnp.int32),
             pltpu.VMEM(core.shape, BF16),
+            pltpu.VMEM((1, tiles), jnp.int32),
+            pltpu.SemaphoreType.DMA,
             pltpu.SemaphoreType.DMA,
         ],
-        (SMEM, SMEM, VMEM),
-    )(pltpu.with_memory_space_constraint(tile_slice, pltpu.HBM), core)
+    )(tile_slice.reshape(1, tiles), core)
+    slot = slot.reshape(tiles)
     distant = {k: shift(mine, groups, -k) for k in range(2, chips, 2)}
-    ids = exchange(wanted, "own")
+    ids = exchange(wanted.reshape(owners, 1, 128), "own")
     adjacent = {k: shift(mine, groups, -k) for k in range(1, chips, 2)}
     pieces = [mine] + [{**distant, **adjacent}[k] for k in range(1, chips)]
     near = call(bundle_kernel, [VMEM] * chips, sds(chip_shape, BF16))(*pieces)

time: 280 us -> 279 us (level)
  no operation moved by 1% of the time
where the time goes in v8:
time: 279 us; the launch traced here: 278 us
  blocking collectives  208 us (75%)
  starting transfers between devices  35.9 us (13%)
  waiting for transfers between devices  21.6 us (8%)
  Pallas kernels  11.4 us (4%)
    all_to_all x3, blocking collectives, exchange(): return lax.all_to_all(x, axis, split_axis=0, concat_axis=0, tiled=True)  181 us
    all_to_all x2, blocking collectives, exchange_x(): lax.all_to_all(x, 'grp', split_axis=0, concat_axis=0, tiled=True, axis_in...  27.4 us
    all_to_all x1, starting transfers between devices, exchange(): return lax.all_to_all(x, axis, split_axis=0, concat_axis=0, tiled=True)  18.7 us
    all_to_all x1, waiting for transfers between devices, exchange(): return lax.all_to_all(x, axis, split_axis=0, concat_axis=0, tiled=True)  13.6 us
    pallas_call x9, Pallas kernels, place(): results = run(*placed)  11.4 us
    ppermute x3, starting transfers between devices, shift(): lax.ppermute(x, 'grp', [(g, (g + 2 * step) % groups) for g in range(group...  11.4 us
    ppermute x3, starting transfers between devices, swap(): return lax.ppermute(x, 'grp', [(g, g ^ 1) for g in range(groups)])  5.75 us
  transfers between devices with their start and end apart: 7, of which 5 were waited for; matrix products, arithmetic and copies ran while one was open for 0% of the time, Pallas kernels for 0%

profile of v8, /device:TPU:8, one launch (start us, length us, event | category | flops | bytes accessed | tf_op | source)
XLA Modules:
  0.0 278.0 jit_solution(10287069294401553073)
XLA Ops:
  0.6 1.6 shard_map.77
  2.3 3.4 %collective-permute-start.2 = (bf16[20,32,128]{2,1,0:T(8,128)(2,1)S(1)}, bf16[20,32,128]{2,1,0:T(8,128)(2,1)S(1)}, u32[]{:S(2)}, u32[]{:S(2)}) collective-permute-start(bf16[20,32,128]{2,1,0:T(8,128)(2,1)S(1)} %get-tuple-element.9.refs_0_.table_ref), channel_id=1, source_target_pairs={{0,128},{64,192},{128,256},{192,320},{256,384},{320,448},{384,0},{... | collective-permute-start | bytes 491528 | tf_op jit(solution)/shard_map/ppermute | solution.py:208
  5.7 4.6 %collective-permute-start.1 = (bf16[20,32,128]{2,1,0:T(8,128)(2,1)S(1)}, bf16[20,32,128]{2,1,0:T(8,128)(2,1)S(1)}, u32[]{:S(2)}, u32[]{:S(2)}) collective-permute-start(bf16[20,32,128]{2,1,0:T(8,128)(2,1)S(1)} %get-tuple-element.9.refs_0_.table_ref), channel_id=1, source_target_pairs={{0,256},{64,320},{128,384},{192,448},{256,0},{320,64},{384,128},{4... | collective-permute-start | bytes 491528 | tf_op jit(solution)/shard_map/ppermute | solution.py:208
  10.3 3.3 %collective-permute-start = (bf16[20,32,128]{2,1,0:T(8,128)(2,1)S(1)}, bf16[20,32,128]{2,1,0:T(8,128)(2,1)S(1)}, u32[]{:S(2)}, u32[]{:S(2)}) collective-permute-start(bf16[20,32,128]{2,1,0:T(8,128)(2,1)S(1)} %get-tuple-element.9.refs_0_.table_ref), channel_id=1, source_target_pairs={{0,384},{64,448},{128,0},{192,64},{256,128},{320,192},{384,256},{4... | collective-permute-start | bytes 491528 | tf_op jit(solution)/shard_map/ppermute | solution.py:208
  13.7 0.0 collective-permute-done.2.refs_3_
  13.7 2.1 collective-permute-done.1.refs_2_
  15.8 1.8 collective-permute-done.refs_1_
  17.6 1.9 collective-permute-start.3
  19.6 18.7 %all-to-all-start = ((s32[64,1,128]{2,1,0:T(1,128)}), s32[64,1,128]{2,1,0:T(1,128)S(1)}, u32[]{:S(2)}, u32[]{:S(2)}) async-start(s32[64,1,128]{2,1,0:T(1,128)} %bitcast.1), calls=%async_computation | async-start | bytes 65536 | tf_op jit(solution)/shard_map/all_to_all | solution.py:204
  38.3 13.6 %all-to-all-done.ids_ref = s32[64,1,128]{2,1,0:T(1,128)S(1)} async-done(((s32[64,1,128]{2,1,0:T(1,128)}), s32[64,1,128]{2,1,0:T(1,128)S(1)}, u32[]{:S(2)}, u32[]{:S(2)}) %all-to-all-start) | async-done | bytes 32800 | tf_op jit(solution)/shard_map/all_to_all | solution.py:204
  51.9 0.0 collective-permute-done.3.far_ref
  51.9 1.3 shard_map.79
  53.3 0.0 copy-start
  53.3 0.0 copy-start.1
  53.3 0.0 copy-start.3
  53.3 59.6 %all_to_all.30.slice_ref = bf16[128,32,128]{2,1,0:T(8,128)(2,1)S(1)} all-to-all(bf16[128,32,128]{2,1,0:T(8,128)(2,1)S(1)} %shard_map.79), channel_id=1, replica_groups=mesh['grp'=8,'own'=64] {'own'}, dimensions={0} | all-to-all | bytes 2097152 | tf_op jit(solution)/shard_map/all_to_all | solution.py:204
  112.9 0.0 copy-done.2
  112.9 0.0 copy-done.3
  112.9 1.8 shard_map.80
  114.8 60.0 %all_to_all.31.grad_ref = bf16[128,32,128]{2,1,0:T(8,128)(2,1)S(1)} all-to-all(bf16[128,32,128]{2,1,0:T(8,128)(2,1)S(1)} %shard_map.80), channel_id=1, replica_groups=mesh['grp'=8,'own'=64] {'own'}, dimensions={0} | all-to-all | bytes 2097152 | tf_op jit(solution)/shard_map/all_to_all | solution.py:204
  174.8 2.0 shard_map.81
  176.7 1.9 collective-permute-start.4
  178.7 2.1 collective-permute-done.4.other_ref
  180.7 0.1 shard_map.82
  180.9 15.0 %all_to_all.32.part_ref = bf16[4,20,32,128]{3,2,1,0:T(8,128)(2,1)S(1)} all-to-all(bf16[4,20,32,128]{3,2,1,0:T(8,128)(2,1)S(1)} %shard_map.82), channel_id=1, replica_groups={{0,128,256,384},{64,192,320,448},{1,129,257,385},{65,193,321,449},{2,13..., dimensions={0} | all-to-all | bytes 1310720 | tf_op jit(solution)/shard_map/all_to_all | solution.py:235
  195.9 1.1 shard_map.83
  197.0 12.4 %all_to_all.33.near_ref = bf16[4,20,32,128]{3,2,1,0:T(8,128)(2,1)S(1)} all-to-all(bf16[4,20,32,128]{3,2,1,0:T(8,128)(2,1)S(1)} %get-tuple-element.15), channel_id=1, replica_groups={{0,128,256,384},{64,192,320,448},{1,129,257,385},{65,193,321,449},{2,13..., dimensions={0} | all-to-all | bytes 1310720 | tf_op jit(solution)/shard_map/all_to_all | solution.py:235
  209.4 1.9 collective-permute-start.5
  211.3 2.1 collective-permute-done.5.far_ref
  213.4 1.3 shard_map.84
  214.8 61.2 %all_to_all.34.slice_ref = bf16[128,32,128]{2,1,0:T(8,128)(2,1)S(1)} all-to-all(bf16[128,32,128]{2,1,0:T(8,128)(2,1)S(1)} %shard_map.84), channel_id=1, replica_groups=mesh['grp'=8,'own'=64] {'own'}, dimensions={0} | all-to-all | bytes 2097152 | tf_op jit(solution)/shard_map/all_to_all | solution.py:204
  276.0 2.0 shard_map.85
  (4 shorter events, 0.0 us)
Async XLA Ops:
  2.3 11.4 %collective-permute-start.2 = (bf16[20,32,128]{2,1,0:T(8,128)(2,1)S(1)}, bf16[20,32,128]{2,1,0:T(8,128)(2,1)S(1)}, u32[]{:S(2)}, u32[]{:S(2)}) collective-permute-start(bf16[20,32,128]{2,1,0:T(8,128)(2,1)S(1)} %get-tuple-element.9.refs_0_.table_ref), channel_id=1, source_target_pairs={{0,128},{64,192},{128,256},{192,320},{256,384},{320,448},{384,0},{... | collective-permute-start | bytes 491528 | tf_op jit(solution)/shard_map/ppermute | solution.py:208
  5.7 10.1 %collective-permute-start.1 = (bf16[20,32,128]{2,1,0:T(8,128)(2,1)S(1)}, bf16[20,32,128]{2,1,0:T(8,128)(2,1)S(1)}, u32[]{:S(2)}, u32[]{:S(2)}) collective-permute-start(bf16[20,32,128]{2,1,0:T(8,128)(2,1)S(1)} %get-tuple-element.9.refs_0_.table_ref), channel_id=1, source_target_pairs={{0,256},{64,320},{128,384},{192,448},{256,0},{320,64},{384,128},{4... | collective-permute-start | bytes 491528 | tf_op jit(solution)/shard_map/ppermute | solution.py:208
  10.3 7.3 %collective-permute-start = (bf16[20,32,128]{2,1,0:T(8,128)(2,1)S(1)}, bf16[20,32,128]{2,1,0:T(8,128)(2,1)S(1)}, u32[]{:S(2)}, u32[]{:S(2)}) collective-permute-start(bf16[20,32,128]{2,1,0:T(8,128)(2,1)S(1)} %get-tuple-element.9.refs_0_.table_ref), channel_id=1, source_target_pairs={{0,384},{64,448},{128,0},{192,64},{256,128},{320,192},{384,256},{4... | collective-permute-start | bytes 491528 | tf_op jit(solution)/shard_map/ppermute | solution.py:208
  17.6 34.3 %collective-permute-start.3 = (bf16[4,20,32,128]{3,2,1,0:T(8,128)(2,1)S(1)}, bf16[4,20,32,128]{3,2,1,0:T(8,128)(2,1)S(1)}, u32[]{:S(2)}, u32[]{:S(2)}) collective-permute-start(bf16[4,20,32,128]{3,2,1,0:T(8,128)(2,1)S(1)} %shard_map.78.near_ref), channel_id=1, source_target_pairs={{0,64},{64,0},{128,192},{192,128},{256,320},{320,256},{384,448},{4... | collective-permute-start | bytes 1966088 | tf_op jit(solution)/shard_map/ppermute | solution.py:212
  19.6 32.3 %all-to-all-start = ((s32[64,1,128]{2,1,0:T(1,128)}), s32[64,1,128]{2,1,0:T(1,128)S(1)}, u32[]{:S(2)}, u32[]{:S(2)}) async-start(s32[64,1,128]{2,1,0:T(1,128)} %bitcast.1), calls=%async_computation | async-start | bytes 65536 | tf_op jit(solution)/shard_map/all_to_all | solution.py:204
  51.9 61.0 %copy-start.2 = (bf16[64,128]{1,0:T(8,128)(2,1)S(1)}, bf16[64,128]{1,0:T(8,128)(2,1)}, u32[]{:S(2)}) copy-start(bf16[64,128]{1,0:T(8,128)(2,1)} %value_ref.1) | copy-start | bytes 49156
  53.3 59.7 %copy-start = (bf16[64,128,64]{1,2,0:T(8,128)(2,1)S(1)}, bf16[64,128,64]{1,2,0:T(8,128)(2,1)}, u32[]{:S(2)}) copy-start(bf16[64,128,64]{1,2,0:T(8,128)(2,1)} %param.6) | copy-start | bytes 3145732
  53.3 59.6 %copy-start.1 = (bf16[64,128,64]{1,2,0:T(8,128)(2,1)S(1)}, bf16[64,128,64]{1,2,0:T(8,128)(2,1)}, u32[]{:S(2)}) copy-start(bf16[64,128,64]{1,2,0:T(8,128)(2,1)} %param.7) | copy-start | bytes 3145732
  53.3 59.6 %copy-start.3 = (s32[64]{0:T(128)S(1)}, s32[64]{0:T(128)}, u32[]{:S(2)}) copy-start(s32[64]{0:T(128)} %fill_ref.1) | copy-start | bytes 772
  176.7 4.0 %collective-permute-start.4 = (bf16[4,20,32,128]{3,2,1,0:T(8,128)(2,1)S(1)}, bf16[4,20,32,128]{3,2,1,0:T(8,128)(2,1)S(1)}, u32[]{:S(2)}, u32[]{:S(2)}) collective-permute-start(bf16[4,20,32,128]{3,2,1,0:T(8,128)(2,1)S(1)} %get-tuple-element.13), channel_id=1, source_target_pairs={{0,64},{64,0},{128,192},{192,128},{256,320},{320,256},{384,448},{4... | collective-permute-start | bytes 1966088 | tf_op jit(solution)/shard_map/ppermute | solution.py:212
  209.4 4.0 %collective-permute-start.5 = (bf16[4,20,32,128]{3,2,1,0:T(8,128)(2,1)S(1)}, bf16[4,20,32,128]{3,2,1,0:T(8,128)(2,1)S(1)}, u32[]{:S(2)}, u32[]{:S(2)}) collective-permute-start(bf16[4,20,32,128]{3,2,1,0:T(8,128)(2,1)S(1)} %all_to_all.33.near_ref), channel_id=1, source_target_pairs={{0,64},{64,0},{128,192},{192,128},{256,320},{320,256},{384,448},{4... | collective-permute-start | bytes 1966088 | tf_op jit(solution)/shard_map/ppermute | solution.py:212

commit v9 on v8

--- a/solution.py
+++ b/solution.py
@@ -41,7 +41,8 @@
     block = lax.shift_right_logical(index * magic, SHIFT)
     group = lax.shift_right_logical(block * -(-(2**SHIFT) // owners), SHIFT)
     owner = block - group * owners
-    local = (group - block) * per_device + index
+    side_major = (group & 1) * (groups // 2) + lax.shift_right_logical(group, 1)
+    local = (side_major - block) * per_device + index
 
     mine = jnp.broadcast_to(owner.astype(F32), (tiles, tiles))
     row = lax.broadcasted_iota(jnp.int32, (tiles, tiles), 0)
@@ -75,20 +76,18 @@
     lax.fori_loop(0, out_ref.shape[0] // 8, step, 0, unroll=2)
 
 
-def bundle_kernel(*refs):
+def bundle_kernel(me_ref, *refs):
     pieces, out_ref = refs[:-1], refs[-1]
     for k, piece in enumerate(pieces):
-        out_ref[k] = piece[...]
-
-
-def sided_kernel(turned, me_ref, ids_ref, near_ref, far_ref, out_ref, table_ref):
+        out_ref[lax.rem(lax.div(me_ref[0], 2) + k, len(pieces))] = piece[...]
+
+
+def sided_kernel(me_ref, ids_ref, near_ref, far_ref, out_ref, table_ref):
     chips, size = near_ref.shape[:2]
     side = lax.rem(me_ref[0], 2)
-    turn = lax.div(me_ref[0], 2) if turned else 0
     for x in range(chips):
-        place = 2 * lax.rem(turn + x, chips)
-        table_ref[pl.ds((place + side) * size, size)] = near_ref[x]
-        table_ref[pl.ds((place + 1 - side) * size, size)] = far_ref[x]
+        table_ref[pl.ds((side * chips + x) * size, size)] = near_ref[x]
+        table_ref[pl.ds(((1 - side) * chips + x) * size, size)] = far_ref[x]
     pick_rows(ids_ref, table_ref, out_ref)
 
 
@@ -126,33 +125,48 @@
     lax.fori_loop(0, left_ref.shape[0] // wide, step, 0)
 
 
-def sum_kernel(ids_ref, grad_ref, me_ref, near_ref, far_ref, acc_ref):
+def add_side(side, ids_ref, grad_ref, acc_ref):
+    size = acc_ref.shape[0] - 1
     acc_ref[...] = jnp.zeros_like(acc_ref)
 
     def step(c, carry):
         for r in range(2):
-            acc_ref[ids_ref[c, 0, r]] += grad_ref[2 * c + r].astype(F32)
+            row = ids_ref[c, 0, r] - side * size
+            row = jnp.where((row >= 0) & (row < size), row, size)
+            acc_ref[row] += grad_ref[2 * c + r].astype(F32)
         return carry
 
     lax.fori_loop(0, grad_ref.shape[0] // 2, step, 0, unroll=4)
-    per_device = near_ref.shape[1]
-    side = lax.rem(me_ref[0], 2)
-    for x in range(near_ref.shape[0]):
-        near_ref[x] = acc_ref[pl.ds((2 * x + side) * per_device, per_device)]
-        far_ref[x] = acc_ref[pl.ds((2 * x + 1 - side) * per_device, per_device)].astype(BF16)
+
+
+def far_kernel(me_ref, ids_ref, grad_ref, out_ref, acc_ref):
+    add_side(1 - lax.rem(me_ref[0], 2), ids_ref, grad_ref, acc_ref)
+    size = out_ref.shape[1]
+    for x in range(out_ref.shape[0]):
+        out_ref[x] = acc_ref[x * size : (x + 1) * size].astype(BF16)
+
+
+def near_kernel(me_ref, ids_ref, grad_ref, acc_ref):
+    add_side(lax.rem(me_ref[0], 2), ids_ref, grad_ref, acc_ref)
 
 
 def join_kernel(near_ref, other_ref, out_ref):
-    out_ref[...] = (near_ref[...] + other_ref[...].astype(F32)).astype(BF16)
-
-
-def update_kernel(table_ref, part_ref, packed_ref, out_ref):
+    size = out_ref.shape[1]
+    for x in range(out_ref.shape[0]):
+        near = near_ref[x * size : (x + 1) * size]
+        out_ref[x] = (near + other_ref[x].astype(F32)).astype(BF16)
+
+
+def update_kernel(table_ref, part_ref, packed_ref):
     total = jnp.sum(part_ref[...].astype(F32), axis=0)
     packed = (table_ref[...].astype(F32) - total).astype(BF16)
     for x in range(packed_ref.shape[0]):
         packed_ref[x] = packed
+
+
+def core_kernel(packed_ref, out_ref):
     for i in range(out_ref.shape[0]):
-        out_ref[i] = unpack(packed[i].astype(F32)).T.astype(BF16)
+        out_ref[i] = unpack(packed_ref[0, i].astype(F32)).T.astype(BF16)
 
 
 def refresh_kernel(slot_ref, left_ref, slice_ref, out_ref):
@@ -254,9 +268,9 @@
     ids = exchange(wanted.reshape(owners, 1, 128), "own")
     adjacent = {k: shift(mine, groups, -k) for k in range(1, chips, 2)}
     pieces = [mine] + [{**distant, **adjacent}[k] for k in range(1, chips)]
-    near = call(bundle_kernel, [VMEM] * chips, sds(chip_shape, BF16))(*pieces)
+    near = call(bundle_kernel, [SMEM] + [VMEM] * chips, sds(chip_shape, BF16))(me, *pieces)
     outgoing = call(
-        functools.partial(sided_kernel, True), [SMEM] * 2 + [VMEM] * 2, slot_sds, [table_scr]
+        sided_kernel, [SMEM] * 2 + [VMEM] * 2, slot_sds, [table_scr]
     )(me, ids, near, swap(near, groups))
     got = exchange(outgoing, "own")
     grads = call(
@@ -266,24 +280,29 @@
         [pltpu.VMEM((tiles, rows), F32)],
     )(slot, tile_fill, left_t, right_t, values, got)
     got_grads = exchange(grads, "own")
-    near, far = call(
-        sum_kernel,
-        [SMEM, VMEM, SMEM],
-        (sds(chip_shape, F32), sds(chip_shape, BF16)),
-        [pltpu.VMEM((local_count + 1,) + packed_shape, F32)],
-    )(ids, got_grads, me)
-    joined = call(join_kernel, [VMEM] * 2, sds(chip_shape, BF16))(near, swap(far, groups))
-    new_spread, new_core = call(
-        update_kernel, [VMEM] * 2, (sds(chip_shape, BF16), sds(core.shape, BF16)), loose=(1,)
-    )(mine, exchange_x(joined))
+    side_rows = chips * per_device + 1
+    far = call(
+        far_kernel,
+        [SMEM, SMEM, VMEM],
+        sds(chip_shape, BF16),
+        [pltpu.VMEM((side_rows,) + packed_shape, F32)],
+    )(me, ids, got_grads)
+    other = swap(far, groups)
+    near = call(
+        near_kernel, [SMEM, SMEM, VMEM], sds((side_rows,) + packed_shape, F32)
+    )(me, ids, got_grads)
+    joined = call(join_kernel, [VMEM] * 2, sds(chip_shape, BF16))(near, other)
+    new_spread = call(update_kernel, [VMEM] * 2, sds(chip_shape, BF16))(mine, exchange_x(joined))
     new_near = exchange_x(new_spread)
     new_far = swap(new_near, groups)
-    outgoing = call(
-        functools.partial(sided_kernel, False), [SMEM] * 2 + [VMEM] * 2, slot_sds, [table_scr])(
+    new_core = call(core_kernel, [VMEM], sds(core.shape, BF16), loose=(0,))(new_spread)
+    outgoing = call(sided_kernel, [SMEM] * 2 + [VMEM] * 2, slot_sds, [table_scr])(
         me, ids, new_near, new_far
     )
     new_got = exchange(outgoing, "own")
-    new_left_t = call(refresh_kernel, [SMEM, VMEM, VMEM], sds(left_t.shape, BF16), loose=(0,))(slot, left_t, new_got)
+    new_left_t = call(refresh_kernel, [SMEM, VMEM, VMEM], sds(left_t.shape, BF16), loose=(0,))(
+        slot, left_t, new_got
+    )
     return (new_core, jnp.swapaxes(new_left_t, 1, 2))
 
 

time: 279 us -> 279 us (level)
  waiting for transfers between devices: 21.6 us -> 60.5 us
  blocking collectives: 208 us -> 180 us
  starting transfers between devices: 35.9 us -> 22.9 us
    all_to_all x1, waiting for transfers between devices: 13.6 us -> 54.4 us  [exchange(): return lax.all_to_all(x, axis, split_axis=0, concat_axis=0, tiled=True)]
    all_to_all x3, blocking collectives: 181 us -> 152 us  [exchange(): return lax.all_to_all(x, axis, split_axis=0, concat_axis=0, tiled=True)]
    all_to_all x1, starting transfers between devices: 18.7 us -> 5.76 us  [exchange(): return lax.all_to_all(x, axis, split_axis=0, concat_axis=0, tiled=True)]
    pallas_call x9 -> x11, Pallas kernels: 11.4 us -> 13 us  [place(): results = run(*placed)]
  transfers between devices with their start and end apart: 7 -> 7, of which waited for: 5 -> 5; matrix products, arithmetic and copies ran while one was open for 0% -> 0% of each run, Pallas kernels for 0% -> 1%
where the time goes in v9:
time: 279 us; the launch traced here: 278 us
  blocking collectives  180 us (65%)
  waiting for transfers between devices  60.5 us (22%)
  starting transfers between devices  22.9 us (8%)
  Pallas kernels  13 us (5%)
    all_to_all x3, blocking collectives, exchange(): return lax.all_to_all(x, axis, split_axis=0, concat_axis=0, tiled=True)  152 us
    all_to_all x1, waiting for transfers between devices, exchange(): return lax.all_to_all(x, axis, split_axis=0, concat_axis=0, tiled=True)  54.4 us
    all_to_all x2, blocking collectives, exchange_x(): lax.all_to_all(x, 'grp', split_axis=0, concat_axis=0, tiled=True, axis_in...  28.3 us
    pallas_call x11, Pallas kernels, place(): results = run(*placed)  13 us
    ppermute x3, starting transfers between devices, shift(): lax.ppermute(x, 'grp', [(g, (g + 2 * step) % groups) for g in range(group...  11.4 us
    all_to_all x1, starting transfers between devices, exchange(): return lax.all_to_all(x, axis, split_axis=0, concat_axis=0, tiled=True)  5.76 us
    ppermute x3, starting transfers between devices, swap(): return lax.ppermute(x, 'grp', [(g, g ^ 1) for g in range(groups)])  5.75 us
  transfers between devices with their start and end apart: 7, of which 5 were waited for; matrix products, arithmetic and copies ran while one was open for 0% of the time, Pallas kernels for 1%

profile of v9, /device:TPU:8, one launch (start us, length us, event | category | flops | bytes accessed | tf_op | source)
XLA Modules:
  0.0 278.2 jit_solution(225359896533121045)
XLA Ops:
  0.6 1.2 shard_map.77
  1.9 3.4 %collective-permute-start.2 = (bf16[20,32,128]{2,1,0:T(8,128)(2,1)S(1)}, bf16[20,32,128]{2,1,0:T(8,128)(2,1)S(1)}, u32[]{:S(2)}, u32[]{:S(2)}) collective-permute-start(bf16[20,32,128]{2,1,0:T(8,128)(2,1)S(1)} %get-tuple-element.5.refs_0_.table_ref), channel_id=1, source_target_pairs={{0,128},{64,192},{128,256},{192,320},{256,384},{320,448},{384,0},{... | collective-permute-start | bytes 491528 | tf_op jit(solution)/shard_map/ppermute | solution.py:222
  5.3 4.6 %collective-permute-start.1 = (bf16[20,32,128]{2,1,0:T(8,128)(2,1)S(1)}, bf16[20,32,128]{2,1,0:T(8,128)(2,1)S(1)}, u32[]{:S(2)}, u32[]{:S(2)}) collective-permute-start(bf16[20,32,128]{2,1,0:T(8,128)(2,1)S(1)} %get-tuple-element.5.refs_0_.table_ref), channel_id=1, source_target_pairs={{0,256},{64,320},{128,384},{192,448},{256,0},{320,64},{384,128},{4... | collective-permute-start | bytes 491528 | tf_op jit(solution)/shard_map/ppermute | solution.py:222
  9.9 3.3 %collective-permute-start = (bf16[20,32,128]{2,1,0:T(8,128)(2,1)S(1)}, bf16[20,32,128]{2,1,0:T(8,128)(2,1)S(1)}, u32[]{:S(2)}, u32[]{:S(2)}) collective-permute-start(bf16[20,32,128]{2,1,0:T(8,128)(2,1)S(1)} %get-tuple-element.5.refs_0_.table_ref), channel_id=1, source_target_pairs={{0,384},{64,448},{128,0},{192,64},{256,128},{320,192},{384,256},{4... | collective-permute-start | bytes 491528 | tf_op jit(solution)/shard_map/ppermute | solution.py:222
  13.3 2.1 collective-permute-done.1.refs_2_
  15.4 1.8 collective-permute-done.refs_1_
  17.3 1.9 collective-permute-start.3
  19.2 32.2 %all_to_all.30.ids_ref = s32[64,1,128]{2,1,0:T(1,128)S(1)} all-to-all(s32[64,1,128]{2,1,0:T(1,128)S(1)} %bitcast.10), channel_id=1, replica_groups=mesh['grp'=8,'own'=64] {'own'}, dimensions={0} | all-to-all | bytes 65536 | tf_op jit(solution)/shard_map/all_to_all | solution.py:218
  51.4 1.3 shard_map.79
  52.7 0.0 copy-start
  52.7 0.0 copy-start.2
  52.8 0.0 copy-start.4
  52.8 59.6 %all_to_all.31.slice_ref = bf16[128,32,128]{2,1,0:T(8,128)(2,1)S(1)} all-to-all(bf16[128,32,128]{2,1,0:T(8,128)(2,1)S(1)} %shard_map.79), channel_id=1, replica_groups=mesh['grp'=8,'own'=64] {'own'}, dimensions={0} | all-to-all | bytes 2097152 | tf_op jit(solution)/shard_map/all_to_all | solution.py:218
  112.4 1.9 shard_map.80
  114.3 60.0 %all_to_all.32.grad_ref = bf16[128,32,128]{2,1,0:T(8,128)(2,1)S(1)} all-to-all(bf16[128,32,128]{2,1,0:T(8,128)(2,1)S(1)} %shard_map.80), channel_id=1, replica_groups=mesh['grp'=8,'own'=64] {'own'}, dimensions={0} | all-to-all | bytes 2097152 | tf_op jit(solution)/shard_map/all_to_all | solution.py:218
  174.3 2.0 shard_map.82
  176.2 1.9 collective-permute-start.4
  178.2 1.9 shard_map.81.near_ref
  180.1 0.2 collective-permute-done.4.other_ref
  180.2 0.1 shard_map.83
  180.3 15.3 %all_to_all.33.part_ref = bf16[4,20,32,128]{3,2,1,0:T(8,128)(2,1)S(1)} all-to-all(bf16[4,20,32,128]{3,2,1,0:T(8,128)(2,1)S(1)} %shard_map.83), channel_id=1, replica_groups={{0,128,256,384},{64,192,320,448},{1,129,257,385},{65,193,321,449},{2,13..., dimensions={0} | all-to-all | bytes 1310720 | tf_op jit(solution)/shard_map/all_to_all | solution.py:249
  195.6 0.1 shard_map.84.packed_ref
  195.7 13.0 %all_to_all.34.near_ref = bf16[4,20,32,128]{3,2,1,0:T(8,128)(2,1)S(1)} all-to-all(bf16[4,20,32,128]{3,2,1,0:T(8,128)(2,1)S(1)} %shard_map.84.packed_ref), channel_id=1, replica_groups={{0,128,256,384},{64,192,320,448},{1,129,257,385},{65,193,321,449},{2,13..., dimensions={0} | all-to-all | bytes 1310720 | tf_op jit(solution)/shard_map/all_to_all | solution.py:249
  208.7 1.9 collective-permute-start.5
  210.6 2.1 collective-permute-done.5.far_ref
  212.7 1.3 shard_map.86
  214.0 0.0 copy-start.1
  214.0 1.0 copy-done.1
  215.0 5.8 %all-to-all-start.5 = ((bf16[128,32,128]{2,1,0:T(8,128)(2,1)}), bf16[128,32,128]{2,1,0:T(8,128)(2,1)S(1)}, u32[]{:S(2)}, u32[]{:S(2)}) async-start(bf16[128,32,128]{2,1,0:T(8,128)(2,1)} %copy-done.1), calls=%async_computation.5 | async-start | bytes 2097152 | tf_op jit(solution)/shard_map/all_to_all | solution.py:218
  220.8 1.1 shard_map.85
  221.9 54.4 %all-to-all-done.5.slice_ref = bf16[128,32,128]{2,1,0:T(8,128)(2,1)S(1)} async-done(((bf16[128,32,128]{2,1,0:T(8,128)(2,1)}), bf16[128,32,128]{2,1,0:T(8,128)(2,1)S(1)}, u32[]{:S(2)}, u32[]{:S(2)}) %all-to-all-start.5) | async-done | bytes 1048608 | tf_op jit(solution)/shard_map/all_to_all | solution.py:218
  276.2 2.0 shard_map.87
  (8 shorter events, 0.1 us)
Async XLA Ops:
  1.9 11.4 %collective-permute-start.2 = (bf16[20,32,128]{2,1,0:T(8,128)(2,1)S(1)}, bf16[20,32,128]{2,1,0:T(8,128)(2,1)S(1)}, u32[]{:S(2)}, u32[]{:S(2)}) collective-permute-start(bf16[20,32,128]{2,1,0:T(8,128)(2,1)S(1)} %get-tuple-element.5.refs_0_.table_ref), channel_id=1, source_target_pairs={{0,128},{64,192},{128,256},{192,320},{256,384},{320,448},{384,0},{... | collective-permute-start | bytes 491528 | tf_op jit(solution)/shard_map/ppermute | solution.py:222
  5.3 10.1 %collective-permute-start.1 = (bf16[20,32,128]{2,1,0:T(8,128)(2,1)S(1)}, bf16[20,32,128]{2,1,0:T(8,128)(2,1)S(1)}, u32[]{:S(2)}, u32[]{:S(2)}) collective-permute-start(bf16[20,32,128]{2,1,0:T(8,128)(2,1)S(1)} %get-tuple-element.5.refs_0_.table_ref), channel_id=1, source_target_pairs={{0,256},{64,320},{128,384},{192,448},{256,0},{320,64},{384,128},{4... | collective-permute-start | bytes 491528 | tf_op jit(solution)/shard_map/ppermute | solution.py:222
  9.9 7.3 %collective-permute-start = (bf16[20,32,128]{2,1,0:T(8,128)(2,1)S(1)}, bf16[20,32,128]{2,1,0:T(8,128)(2,1)S(1)}, u32[]{:S(2)}, u32[]{:S(2)}) collective-permute-start(bf16[20,32,128]{2,1,0:T(8,128)(2,1)S(1)} %get-tuple-element.5.refs_0_.table_ref), channel_id=1, source_target_pairs={{0,384},{64,448},{128,0},{192,64},{256,128},{320,192},{384,256},{4... | collective-permute-start | bytes 491528 | tf_op jit(solution)/shard_map/ppermute | solution.py:222
  17.3 34.1 %collective-permute-start.3 = (bf16[4,20,32,128]{3,2,1,0:T(8,128)(2,1)S(1)}, bf16[4,20,32,128]{3,2,1,0:T(8,128)(2,1)S(1)}, u32[]{:S(2)}, u32[]{:S(2)}) collective-permute-start(bf16[4,20,32,128]{3,2,1,0:T(8,128)(2,1)S(1)} %shard_map.78.near_ref), channel_id=1, source_target_pairs={{0,64},{64,0},{128,192},{192,128},{256,320},{320,256},{384,448},{4... | collective-permute-start | bytes 1966088 | tf_op jit(solution)/shard_map/ppermute | solution.py:226
  51.4 61.0 %copy-start.3 = (bf16[64,128]{1,0:T(8,128)(2,1)S(1)}, bf16[64,128]{1,0:T(8,128)(2,1)}, u32[]{:S(2)}) copy-start(bf16[64,128]{1,0:T(8,128)(2,1)} %value_ref.1) | copy-start | bytes 49156
  52.7 59.7 %copy-start = (bf16[64,128,64]{1,2,0:T(8,128)(2,1)S(1)}, bf16[64,128,64]{1,2,0:T(8,128)(2,1)}, u32[]{:S(2)}) copy-start(bf16[64,128,64]{1,2,0:T(8,128)(2,1)} %param.6) | copy-start | bytes 3145732
  52.7 59.6 %copy-start.2 = (bf16[64,128,64]{1,2,0:T(8,128)(2,1)S(1)}, bf16[64,128,64]{1,2,0:T(8,128)(2,1)}, u32[]{:S(2)}) copy-start(bf16[64,128,64]{1,2,0:T(8,128)(2,1)} %param.7) | copy-start | bytes 3145732
  52.8 59.6 %copy-start.4 = (s32[64]{0:T(128)S(1)}, s32[64]{0:T(128)}, u32[]{:S(2)}) copy-start(s32[64]{0:T(128)} %fill_ref.1) | copy-start | bytes 772
  176.2 4.0 %collective-permute-start.4 = (bf16[4,20,32,128]{3,2,1,0:T(8,128)(2,1)S(1)}, bf16[4,20,32,128]{3,2,1,0:T(8,128)(2,1)S(1)}, u32[]{:S(2)}, u32[]{:S(2)}) collective-permute-start(bf16[4,20,32,128]{3,2,1,0:T(8,128)(2,1)S(1)} %shard_map.82), channel_id=1, source_target_pairs={{0,64},{64,0},{128,192},{192,128},{256,320},{320,256},{384,448},{4... | collective-permute-start | bytes 1966088 | tf_op jit(solution)/shard_map/ppermute | solution.py:226
  208.7 4.0 %collective-permute-start.5 = (bf16[4,20,32,128]{3,2,1,0:T(8,128)(2,1)S(1)}, bf16[4,20,32,128]{3,2,1,0:T(8,128)(2,1)S(1)}, u32[]{:S(2)}, u32[]{:S(2)}) collective-permute-start(bf16[4,20,32,128]{3,2,1,0:T(8,128)(2,1)S(1)} %all_to_all.34.near_ref), channel_id=1, source_target_pairs={{0,64},{64,0},{128,192},{192,128},{256,320},{320,256},{384,448},{4... | collective-permute-start | bytes 1966088 | tf_op jit(solution)/shard_map/ppermute | solution.py:226
  214.0 1.0 copy-start.1
  215.0 61.2 %all-to-all-start.5 = ((bf16[128,32,128]{2,1,0:T(8,128)(2,1)}), bf16[128,32,128]{2,1,0:T(8,128)(2,1)S(1)}, u32[]{:S(2)}, u32[]{:S(2)}) async-start(bf16[128,32,128]{2,1,0:T(8,128)(2,1)} %copy-done.1), calls=%async_computation.5 | async-start | bytes 2097152 | tf_op jit(solution)/shard_map/all_to_all | solution.py:218

commit v10 on v9

--- a/solution.py
+++ b/solution.py
@@ -64,13 +64,20 @@
         out_ref[i] = pack(core_scr[i].astype(F32).T).astype(BF16)
 
 
-def pick_rows(ids_ref, table_ref, out_ref):
-    table_ref[table_ref.shape[0] - 1] = jnp.zeros(table_ref.shape[1:], BF16)
+def pick_side(side, ids_ref, table_ref, out_ref, prior_ref=None):
+    count = table_ref.shape[0]
 
     def step(k, carry):
-        rows = [table_ref[ids_ref[4 * k + i // 2, 0, i % 2]] for i in range(8)]
-        for i, row in enumerate(rows):
-            out_ref[8 * k + i] = row
+        rows = []
+        for i in range(8):
+            row = ids_ref[4 * k + i // 2, 0, i % 2] - side * count
+            inside = (row >= 0) & (row < count)
+            value = table_ref[jnp.where(inside, row, 0)]
+            if prior_ref is not None:
+                value = jnp.where(inside, value, prior_ref[8 * k + i])
+            rows.append(value)
+        for i, value in enumerate(rows):
+            out_ref[8 * k + i] = value
         return carry
 
     lax.fori_loop(0, out_ref.shape[0] // 8, step, 0, unroll=2)
@@ -82,13 +89,12 @@
         out_ref[lax.rem(lax.div(me_ref[0], 2) + k, len(pieces))] = piece[...]
 
 
-def sided_kernel(me_ref, ids_ref, near_ref, far_ref, out_ref, table_ref):
-    chips, size = near_ref.shape[:2]
-    side = lax.rem(me_ref[0], 2)
-    for x in range(chips):
-        table_ref[pl.ds((side * chips + x) * size, size)] = near_ref[x]
-        table_ref[pl.ds(((1 - side) * chips + x) * size, size)] = far_ref[x]
-    pick_rows(ids_ref, table_ref, out_ref)
+def pick_near_kernel(me_ref, ids_ref, near_ref, out_ref):
+    pick_side(lax.rem(me_ref[0], 2), ids_ref, near_ref, out_ref)
+
+
+def pick_far_kernel(me_ref, ids_ref, far_ref, prior_ref, out_ref):
+    pick_side(1 - lax.rem(me_ref[0], 2), ids_ref, far_ref, out_ref, prior_ref)
 
 
 def grad_kernel(slot_ref, fill_ref, left_ref, right_ref, value_ref, slice_ref, out_ref, value_scr):
@@ -232,7 +238,6 @@
     chips = groups // 2
     tiles, rows, rank = left.shape
     per_device = core.shape[0]
-    local_count = groups * per_device
     slots = 2 * owners
     packed_shape = (rank // 2, 2 * rank)
     along_x = [[2 * x + side for x in range(chips)] for side in range(2)]
@@ -243,7 +248,9 @@
     slot_sds = sds((slots,) + packed_shape, BF16)
     mine_sds = sds((per_device,) + packed_shape, BF16)
     chip_shape = (chips, per_device) + packed_shape
-    table_scr = pltpu.VMEM((local_count + 1,) + packed_shape, BF16)
+    side_shape = (chips * per_device,) + packed_shape
+    pick_near = call(pick_near_kernel, [SMEM] * 2 + [VMEM], slot_sds)
+    pick_far = call(pick_far_kernel, [SMEM] * 2 + [VMEM] * 2, slot_sds)
 
     def exchange_x(x):
         return lax.all_to_all(
@@ -269,9 +276,9 @@
     adjacent = {k: shift(mine, groups, -k) for k in range(1, chips, 2)}
     pieces = [mine] + [{**distant, **adjacent}[k] for k in range(1, chips)]
     near = call(bundle_kernel, [SMEM] + [VMEM] * chips, sds(chip_shape, BF16))(me, *pieces)
-    outgoing = call(
-        sided_kernel, [SMEM] * 2 + [VMEM] * 2, slot_sds, [table_scr]
-    )(me, ids, near, swap(near, groups))
+    far = swap(near, groups)
+    prior = pick_near(me, ids, near.reshape(side_shape))
+    outgoing = pick_far(me, ids, far.reshape(side_shape), prior)
     got = exchange(outgoing, "own")
     grads = call(
         grad_kernel,
@@ -296,9 +303,8 @@
     new_near = exchange_x(new_spread)
     new_far = swap(new_near, groups)
     new_core = call(core_kernel, [VMEM], sds(core.shape, BF16), loose=(0,))(new_spread)
-    outgoing = call(sided_kernel, [SMEM] * 2 + [VMEM] * 2, slot_sds, [table_scr])(
-        me, ids, new_near, new_far
-    )
+    prior = pick_near(me, ids, new_near.reshape(side_shape))
+    outgoing = pick_far(me, ids, new_far.reshape(side_shape), prior)
     new_got = exchange(outgoing, "own")
     new_left_t = call(refresh_kernel, [SMEM, VMEM, VMEM], sds(left_t.shape, BF16), loose=(0,))(
         slot, left_t, new_got

time: 279 us -> 281 us (level)
  Pallas kernels: 13 us -> 16.1 us
    pallas_call x11 -> x13, Pallas kernels: 13 us -> 16.1 us  [place(): results = run(*placed)]
  transfers between devices with their start and end apart: 7 -> 7, of which waited for: 5 -> 5; matrix products, arithmetic and copies ran while one was open for 0% -> 0% of each run, Pallas kernels for 1% -> 2%
where the time goes in v10:
time: 281 us; the launch traced here: 280 us
  blocking collectives  180 us (64%)
  waiting for transfers between devices  59.1 us (21%)
  starting transfers between devices  22.9 us (8%)
  Pallas kernels  16.1 us (6%)
    all_to_all x3, blocking collectives, exchange(): return lax.all_to_all(x, axis, split_axis=0, concat_axis=0, tiled=True)  152 us
    all_to_all x1, waiting for transfers between devices, exchange(): return lax.all_to_all(x, axis, split_axis=0, concat_axis=0, tiled=True)  54.4 us
    all_to_all x2, blocking collectives, exchange_x(): lax.all_to_all(x, 'grp', split_axis=0, concat_axis=0, tiled=True, axis_in...  28.3 us
    pallas_call x13, Pallas kernels, place(): results = run(*placed)  16.1 us
    ppermute x3, starting transfers between devices, shift(): lax.ppermute(x, 'grp', [(g, (g + 2 * step) % groups) for g in range(group...  11.4 us
    all_to_all x1, starting transfers between devices, exchange(): return lax.all_to_all(x, axis, split_axis=0, concat_axis=0, tiled=True)  5.76 us
    ppermute x3, starting transfers between devices, swap(): return lax.ppermute(x, 'grp', [(g, g ^ 1) for g in range(groups)])  5.75 us
  transfers between devices with their start and end apart: 7, of which 5 were waited for; matrix products, arithmetic and copies ran while one was open for 0% of the time, Pallas kernels for 2%

profile of v10, /device:TPU:8, one launch (start us, length us, event | category | flops | bytes accessed | tf_op | source)
XLA Modules:
  0.0 280.0 jit_solution(14567308075727384568)
XLA Ops:
  0.6 1.2 shard_map.77
  1.9 3.4 %collective-permute-start.2 = (bf16[20,32,128]{2,1,0:T(8,128)(2,1)S(1)}, bf16[20,32,128]{2,1,0:T(8,128)(2,1)S(1)}, u32[]{:S(2)}, u32[]{:S(2)}) collective-permute-start(bf16[20,32,128]{2,1,0:T(8,128)(2,1)S(1)} %get-tuple-element.5.refs_0_.table_ref), channel_id=1, source_target_pairs={{0,128},{64,192},{128,256},{192,320},{256,384},{320,448},{384,0},{... | collective-permute-start | bytes 491528 | tf_op jit(solution)/shard_map/ppermute | solution.py:228
  5.3 4.6 %collective-permute-start.1 = (bf16[20,32,128]{2,1,0:T(8,128)(2,1)S(1)}, bf16[20,32,128]{2,1,0:T(8,128)(2,1)S(1)}, u32[]{:S(2)}, u32[]{:S(2)}) collective-permute-start(bf16[20,32,128]{2,1,0:T(8,128)(2,1)S(1)} %get-tuple-element.5.refs_0_.table_ref), channel_id=1, source_target_pairs={{0,256},{64,320},{128,384},{192,448},{256,0},{320,64},{384,128},{4... | collective-permute-start | bytes 491528 | tf_op jit(solution)/shard_map/ppermute | solution.py:228
  9.9 3.3 %collective-permute-start = (bf16[20,32,128]{2,1,0:T(8,128)(2,1)S(1)}, bf16[20,32,128]{2,1,0:T(8,128)(2,1)S(1)}, u32[]{:S(2)}, u32[]{:S(2)}) collective-permute-start(bf16[20,32,128]{2,1,0:T(8,128)(2,1)S(1)} %get-tuple-element.5.refs_0_.table_ref), channel_id=1, source_target_pairs={{0,384},{64,448},{128,0},{192,64},{256,128},{320,192},{384,256},{4... | collective-permute-start | bytes 491528 | tf_op jit(solution)/shard_map/ppermute | solution.py:228
  13.3 2.1 collective-permute-done.1.refs_2_
  15.4 1.8 collective-permute-done.refs_1_
  17.3 1.9 collective-permute-start.3
  19.2 32.2 %all_to_all.30.ids_ref = s32[64,1,128]{2,1,0:T(1,128)S(1)} all-to-all(s32[64,1,128]{2,1,0:T(1,128)S(1)} %bitcast.18), channel_id=1, replica_groups=mesh['grp'=8,'own'=64] {'own'}, dimensions={0} | all-to-all | bytes 65536 | tf_op jit(solution)/shard_map/all_to_all | solution.py:224
  51.4 1.4 shard_map.79.prior_ref
  52.8 0.0 copy-start.3
  52.8 1.5 shard_map.80
  54.4 0.0 copy-start
  54.4 59.6 %all_to_all.31.slice_ref = bf16[128,32,128]{2,1,0:T(8,128)(2,1)S(1)} all-to-all(bf16[128,32,128]{2,1,0:T(8,128)(2,1)S(1)} %shard_map.80), channel_id=1, replica_groups=mesh['grp'=8,'own'=64] {'own'}, dimensions={0} | all-to-all | bytes 2097152 | tf_op jit(solution)/shard_map/all_to_all | solution.py:224
  114.0 1.8 shard_map.81
  115.8 60.0 %all_to_all.32.grad_ref = bf16[128,32,128]{2,1,0:T(8,128)(2,1)S(1)} all-to-all(bf16[128,32,128]{2,1,0:T(8,128)(2,1)S(1)} %shard_map.81), channel_id=1, replica_groups=mesh['grp'=8,'own'=64] {'own'}, dimensions={0} | all-to-all | bytes 2097152 | tf_op jit(solution)/shard_map/all_to_all | solution.py:224
  175.8 2.0 shard_map.83
  177.8 1.9 collective-permute-start.4
  179.7 1.9 shard_map.82.near_ref
  181.6 0.2 collective-permute-done.4.other_ref
  181.8 0.1 shard_map.84
  181.9 15.3 %all_to_all.33.part_ref = bf16[4,20,32,128]{3,2,1,0:T(8,128)(2,1)S(1)} all-to-all(bf16[4,20,32,128]{3,2,1,0:T(8,128)(2,1)S(1)} %shard_map.84), channel_id=1, replica_groups={{0,128,256,384},{64,192,320,448},{1,129,257,385},{65,193,321,449},{2,13..., dimensions={0} | all-to-all | bytes 1310720 | tf_op jit(solution)/shard_map/all_to_all | solution.py:256
  197.2 0.1 shard_map.85.packed_ref
  197.3 13.0 %all_to_all.34 = bf16[4,20,32,128]{3,2,1,0:T(8,128)(2,1)S(1)} all-to-all(bf16[4,20,32,128]{3,2,1,0:T(8,128)(2,1)S(1)} %shard_map.85.packed_ref), channel_id=1, replica_groups={{0,128,256,384},{64,192,320,448},{1,129,257,385},{65,193,321,449},{2,13..., dimensions={0} | all-to-all | bytes 1310720 | tf_op jit(solution)/shard_map/all_to_all | solution.py:256
  210.3 1.9 collective-permute-start.5
  212.2 1.4 shard_map.87.prior_ref
  213.6 0.6 collective-permute-done.5
  214.2 1.5 shard_map.88
  215.8 1.0 copy-done.1
  216.8 5.8 %all-to-all-start.5 = ((bf16[128,32,128]{2,1,0:T(8,128)(2,1)}), bf16[128,32,128]{2,1,0:T(8,128)(2,1)S(1)}, u32[]{:S(2)}, u32[]{:S(2)}) async-start(bf16[128,32,128]{2,1,0:T(8,128)(2,1)} %copy-done.1), calls=%async_computation.5 | async-start | bytes 2097152 | tf_op jit(solution)/shard_map/all_to_all | solution.py:224
  222.5 1.1 shard_map.86
  223.6 54.4 %all-to-all-done.5.slice_ref = bf16[128,32,128]{2,1,0:T(8,128)(2,1)S(1)} async-done(((bf16[128,32,128]{2,1,0:T(8,128)(2,1)}), bf16[128,32,128]{2,1,0:T(8,128)(2,1)S(1)}, u32[]{:S(2)}, u32[]{:S(2)}) %all-to-all-start.5) | async-done | bytes 1048608 | tf_op jit(solution)/shard_map/all_to_all | solution.py:224
  278.0 2.0 shard_map.89
  (10 shorter events, 0.1 us)
Async XLA Ops:
  1.9 11.4 %collective-permute-start.2 = (bf16[20,32,128]{2,1,0:T(8,128)(2,1)S(1)}, bf16[20,32,128]{2,1,0:T(8,128)(2,1)S(1)}, u32[]{:S(2)}, u32[]{:S(2)}) collective-permute-start(bf16[20,32,128]{2,1,0:T(8,128)(2,1)S(1)} %get-tuple-element.5.refs_0_.table_ref), channel_id=1, source_target_pairs={{0,128},{64,192},{128,256},{192,320},{256,384},{320,448},{384,0},{... | collective-permute-start | bytes 491528 | tf_op jit(solution)/shard_map/ppermute | solution.py:228
  5.3 10.1 %collective-permute-start.1 = (bf16[20,32,128]{2,1,0:T(8,128)(2,1)S(1)}, bf16[20,32,128]{2,1,0:T(8,128)(2,1)S(1)}, u32[]{:S(2)}, u32[]{:S(2)}) collective-permute-start(bf16[20,32,128]{2,1,0:T(8,128)(2,1)S(1)} %get-tuple-element.5.refs_0_.table_ref), channel_id=1, source_target_pairs={{0,256},{64,320},{128,384},{192,448},{256,0},{320,64},{384,128},{4... | collective-permute-start | bytes 491528 | tf_op jit(solution)/shard_map/ppermute | solution.py:228
  9.9 7.3 %collective-permute-start = (bf16[20,32,128]{2,1,0:T(8,128)(2,1)S(1)}, bf16[20,32,128]{2,1,0:T(8,128)(2,1)S(1)}, u32[]{:S(2)}, u32[]{:S(2)}) collective-permute-start(bf16[20,32,128]{2,1,0:T(8,128)(2,1)S(1)} %get-tuple-element.5.refs_0_.table_ref), channel_id=1, source_target_pairs={{0,384},{64,448},{128,0},{192,64},{256,128},{320,192},{384,256},{4... | collective-permute-start | bytes 491528 | tf_op jit(solution)/shard_map/ppermute | solution.py:228
  17.3 35.6 %collective-permute-start.3 = (bf16[4,20,32,128]{3,2,1,0:T(8,128)(2,1)S(1)}, bf16[4,20,32,128]{3,2,1,0:T(8,128)(2,1)S(1)}, u32[]{:S(2)}, u32[]{:S(2)}) collective-permute-start(bf16[4,20,32,128]{3,2,1,0:T(8,128)(2,1)S(1)} %shard_map.78), channel_id=1, source_target_pairs={{0,64},{64,0},{128,192},{192,128},{256,320},{320,256},{384,448},{4... | collective-permute-start | bytes 1966088 | tf_op jit(solution)/shard_map/ppermute | solution.py:232
  52.8 61.2 %copy-start.3 = (bf16[64,128]{1,0:T(8,128)(2,1)S(1)}, bf16[64,128]{1,0:T(8,128)(2,1)}, u32[]{:S(2)}) copy-start(bf16[64,128]{1,0:T(8,128)(2,1)} %value_ref.1) | copy-start | bytes 49156
  54.4 59.7 %copy-start = (bf16[64,128,64]{1,2,0:T(8,128)(2,1)S(1)}, bf16[64,128,64]{1,2,0:T(8,128)(2,1)}, u32[]{:S(2)}) copy-start(bf16[64,128,64]{1,2,0:T(8,128)(2,1)} %param.6) | copy-start | bytes 3145732
  54.4 59.6 %copy-start.2 = (bf16[64,128,64]{1,2,0:T(8,128)(2,1)S(1)}, bf16[64,128,64]{1,2,0:T(8,128)(2,1)}, u32[]{:S(2)}) copy-start(bf16[64,128,64]{1,2,0:T(8,128)(2,1)} %param.7) | copy-start | bytes 3145732
  54.4 59.6 %copy-start.4 = (s32[64]{0:T(128)S(1)}, s32[64]{0:T(128)}, u32[]{:S(2)}) copy-start(s32[64]{0:T(128)} %fill_ref.1) | copy-start | bytes 772
  177.8 4.0 %collective-permute-start.4 = (bf16[4,20,32,128]{3,2,1,0:T(8,128)(2,1)S(1)}, bf16[4,20,32,128]{3,2,1,0:T(8,128)(2,1)S(1)}, u32[]{:S(2)}, u32[]{:S(2)}) collective-permute-start(bf16[4,20,32,128]{3,2,1,0:T(8,128)(2,1)S(1)} %shard_map.83), channel_id=1, source_target_pairs={{0,64},{64,0},{128,192},{192,128},{256,320},{320,256},{384,448},{4... | collective-permute-start | bytes 1966088 | tf_op jit(solution)/shard_map/ppermute | solution.py:232
  210.3 4.0 %collective-permute-start.5 = (bf16[4,20,32,128]{3,2,1,0:T(8,128)(2,1)S(1)}, bf16[4,20,32,128]{3,2,1,0:T(8,128)(2,1)S(1)}, u32[]{:S(2)}, u32[]{:S(2)}) collective-permute-start(bf16[4,20,32,128]{3,2,1,0:T(8,128)(2,1)S(1)} %all_to_all.34), channel_id=1, source_target_pairs={{0,64},{64,0},{128,192},{192,128},{256,320},{320,256},{384,448},{4... | collective-permute-start | bytes 1966088 | tf_op jit(solution)/shard_map/ppermute | solution.py:232
  215.8 1.0 copy-start.1
  216.8 61.2 %all-to-all-start.5 = ((bf16[128,32,128]{2,1,0:T(8,128)(2,1)}), bf16[128,32,128]{2,1,0:T(8,128)(2,1)S(1)}, u32[]{:S(2)}, u32[]{:S(2)}) async-start(bf16[128,32,128]{2,1,0:T(8,128)(2,1)} %copy-done.1), calls=%async_computation.5 | async-start | bytes 2097152 | tf_op jit(solution)/shard_map/all_to_all | solution.py:224

commit v11 on v9

--- a/solution.py
+++ b/solution.py
@@ -68,12 +68,18 @@
     table_ref[table_ref.shape[0] - 1] = jnp.zeros(table_ref.shape[1:], BF16)
 
     def step(k, carry):
-        rows = [table_ref[ids_ref[4 * k + i // 2, 0, i % 2]] for i in range(8)]
+        rows = [table_ref[ids_ref[8 * k + i]] for i in range(8)]
         for i, row in enumerate(rows):
             out_ref[8 * k + i] = row
         return carry
 
     lax.fori_loop(0, out_ref.shape[0] // 8, step, 0, unroll=2)
+
+
+def compact_kernel(ids_ref, out_ref):
+    for c in range(ids_ref.shape[0]):
+        for r in range(2):
+            out_ref[2 * c + r] = ids_ref[c, 0, r]
 
 
 def bundle_kernel(me_ref, *refs):
@@ -131,7 +137,7 @@
 
     def step(c, carry):
         for r in range(2):
-            row = ids_ref[c, 0, r] - side * size
+            row = ids_ref[2 * c + r] - side * size
             row = jnp.where((row >= 0) & (row < size), row, size)
             acc_ref[row] += grad_ref[2 * c + r].astype(F32)
         return carry
@@ -269,9 +275,11 @@
     adjacent = {k: shift(mine, groups, -k) for k in range(1, chips, 2)}
     pieces = [mine] + [{**distant, **adjacent}[k] for k in range(1, chips)]
     near = call(bundle_kernel, [SMEM] + [VMEM] * chips, sds(chip_shape, BF16))(me, *pieces)
-    outgoing = call(
-        sided_kernel, [SMEM] * 2 + [VMEM] * 2, slot_sds, [table_scr]
-    )(me, ids, near, swap(near, groups))
+    far = swap(near, groups)
+    ids = call(compact_kernel, [SMEM], sds((slots,), jnp.int32), out_specs=(SMEM,))(ids)
+    outgoing = call(sided_kernel, [SMEM] * 2 + [VMEM] * 2, slot_sds, [table_scr])(
+        me, ids, near, far
+    )
     got = exchange(outgoing, "own")
     grads = call(
         grad_kernel,

time: 279 us -> 278 us (level)
    pallas_call x11 -> x12, Pallas kernels: 13 us -> 12.6 us  [place(): results = run(*placed)]
  transfers between devices with their start and end apart: 7 -> 7, of which waited for: 5 -> 5; matrix products, arithmetic and copies ran while one was open for 0% -> 0% of each run, Pallas kernels for 1% -> 2%
where the time goes in v11:
time: 278 us
  blocking collectives  179 us (64%)
  waiting for transfers between devices  61 us (22%)
  starting transfers between devices  23.1 us (8%)
  Pallas kernels  12.6 us (5%)
    all_to_all x3, blocking collectives, exchange(): return lax.all_to_all(x, axis, split_axis=0, concat_axis=0, tiled=True)  152 us
    all_to_all x1, waiting for transfers between devices, exchange(): return lax.all_to_all(x, axis, split_axis=0, concat_axis=0, tiled=True)  54.4 us
    all_to_all x2, blocking collectives, exchange_x(): lax.all_to_all(x, 'grp', split_axis=0, concat_axis=0, tiled=True, axis_in...  27.5 us
    pallas_call x12, Pallas kernels, place(): results = run(*placed)  12.6 us
    ppermute x3, starting transfers between devices, shift(): lax.ppermute(x, 'grp', [(g, (g + 2 * step) % groups) for g in range(group...  11.4 us
    all_to_all x1, starting transfers between devices, exchange(): return lax.all_to_all(x, axis, split_axis=0, concat_axis=0, tiled=True)  5.93 us
    ppermute x3, starting transfers between devices, swap(): return lax.ppermute(x, 'grp', [(g, g ^ 1) for g in range(groups)])  5.75 us
  transfers between devices with their start and end apart: 7, of which 5 were waited for; matrix products, arithmetic and copies ran while one was open for 0% of the time, Pallas kernels for 2%

profile of v11, /device:TPU:8, one launch (start us, length us, event | category | flops | bytes accessed | tf_op | source)
XLA Modules:
  0.0 277.7 jit_solution(16357185856052779118)
XLA Ops:
  0.6 1.2 shard_map.77
  1.9 3.4 %collective-permute-start.2 = (bf16[20,32,128]{2,1,0:T(8,128)(2,1)S(1)}, bf16[20,32,128]{2,1,0:T(8,128)(2,1)S(1)}, u32[]{:S(2)}, u32[]{:S(2)}) collective-permute-start(bf16[20,32,128]{2,1,0:T(8,128)(2,1)S(1)} %get-tuple-element.5.refs_0_.table_ref), channel_id=1, source_target_pairs={{0,128},{64,192},{128,256},{192,320},{256,384},{320,448},{384,0},{... | collective-permute-start | bytes 491528 | tf_op jit(solution)/shard_map/ppermute | solution.py:228
  5.3 4.6 %collective-permute-start.1 = (bf16[20,32,128]{2,1,0:T(8,128)(2,1)S(1)}, bf16[20,32,128]{2,1,0:T(8,128)(2,1)S(1)}, u32[]{:S(2)}, u32[]{:S(2)}) collective-permute-start(bf16[20,32,128]{2,1,0:T(8,128)(2,1)S(1)} %get-tuple-element.5.refs_0_.table_ref), channel_id=1, source_target_pairs={{0,256},{64,320},{128,384},{192,448},{256,0},{320,64},{384,128},{4... | collective-permute-start | bytes 491528 | tf_op jit(solution)/shard_map/ppermute | solution.py:228
  9.9 3.3 %collective-permute-start = (bf16[20,32,128]{2,1,0:T(8,128)(2,1)S(1)}, bf16[20,32,128]{2,1,0:T(8,128)(2,1)S(1)}, u32[]{:S(2)}, u32[]{:S(2)}) collective-permute-start(bf16[20,32,128]{2,1,0:T(8,128)(2,1)S(1)} %get-tuple-element.5.refs_0_.table_ref), channel_id=1, source_target_pairs={{0,384},{64,448},{128,0},{192,64},{256,128},{320,192},{384,256},{4... | collective-permute-start | bytes 491528 | tf_op jit(solution)/shard_map/ppermute | solution.py:228
  13.3 2.1 collective-permute-done.1.refs_2_
  15.4 1.8 collective-permute-done.refs_1_
  17.3 1.9 collective-permute-start.3
  19.2 32.2 %all_to_all.30.ids_ref = s32[64,1,128]{2,1,0:T(1,128)S(1)} all-to-all(s32[64,1,128]{2,1,0:T(1,128)S(1)} %bitcast.10), channel_id=1, replica_groups=mesh['grp'=8,'own'=64] {'own'}, dimensions={0} | all-to-all | bytes 65536 | tf_op jit(solution)/shard_map/all_to_all | solution.py:224
  51.4 1.7 shard_map.78.ids_ref
  53.1 0.0 copy-start.3
  53.2 0.8 shard_map.80
  54.0 0.0 copy-start.4
  54.0 59.6 %all_to_all.31.slice_ref = bf16[128,32,128]{2,1,0:T(8,128)(2,1)S(1)} all-to-all(bf16[128,32,128]{2,1,0:T(8,128)(2,1)S(1)} %shard_map.80), channel_id=1, replica_groups=mesh['grp'=8,'own'=64] {'own'}, dimensions={0} | all-to-all | bytes 2097152 | tf_op jit(solution)/shard_map/all_to_all | solution.py:224
  113.6 1.8 shard_map.81
  115.5 60.0 %all_to_all.32.grad_ref = bf16[128,32,128]{2,1,0:T(8,128)(2,1)S(1)} all-to-all(bf16[128,32,128]{2,1,0:T(8,128)(2,1)S(1)} %shard_map.81), channel_id=1, replica_groups=mesh['grp'=8,'own'=64] {'own'}, dimensions={0} | all-to-all | bytes 2097152 | tf_op jit(solution)/shard_map/all_to_all | solution.py:224
  175.5 1.4 shard_map.83
  176.9 1.9 collective-permute-start.4
  178.8 1.4 shard_map.82.near_ref
  180.2 0.7 collective-permute-done.4.other_ref
  180.9 0.1 shard_map.84
  181.0 15.0 %all_to_all.33.part_ref = bf16[4,20,32,128]{3,2,1,0:T(8,128)(2,1)S(1)} all-to-all(bf16[4,20,32,128]{3,2,1,0:T(8,128)(2,1)S(1)} %shard_map.84), channel_id=1, replica_groups={{0,128,256,384},{64,192,320,448},{1,129,257,385},{65,193,321,449},{2,13..., dimensions={0} | all-to-all | bytes 1310720 | tf_op jit(solution)/shard_map/all_to_all | solution.py:255
  196.0 0.1 shard_map.85.packed_ref
  196.1 12.4 %all_to_all.34.near_ref = bf16[4,20,32,128]{3,2,1,0:T(8,128)(2,1)S(1)} all-to-all(bf16[4,20,32,128]{3,2,1,0:T(8,128)(2,1)S(1)} %shard_map.85.packed_ref), channel_id=1, replica_groups={{0,128,256,384},{64,192,320,448},{1,129,257,385},{65,193,321,449},{2,13..., dimensions={0} | all-to-all | bytes 1310720 | tf_op jit(solution)/shard_map/all_to_all | solution.py:255
  208.6 1.9 collective-permute-start.5
  210.5 2.1 collective-permute-done.5.far_ref
  212.6 0.8 shard_map.87
  213.4 0.0 copy-start.1
  213.4 1.0 copy-done.1
  214.3 5.9 %all-to-all-start.5 = ((bf16[128,32,128]{2,1,0:T(8,128)(2,1)}), bf16[128,32,128]{2,1,0:T(8,128)(2,1)S(1)}, u32[]{:S(2)}, u32[]{:S(2)}) async-start(bf16[128,32,128]{2,1,0:T(8,128)(2,1)} %copy-done.1), calls=%async_computation.5 | async-start | bytes 2097152 | tf_op jit(solution)/shard_map/all_to_all | solution.py:224
  220.3 1.1 shard_map.86
  221.4 54.4 %all-to-all-done.5.slice_ref = bf16[128,32,128]{2,1,0:T(8,128)(2,1)S(1)} async-done(((bf16[128,32,128]{2,1,0:T(8,128)(2,1)}), bf16[128,32,128]{2,1,0:T(8,128)(2,1)S(1)}, u32[]{:S(2)}, u32[]{:S(2)}) %all-to-all-start.5) | async-done | bytes 1048608 | tf_op jit(solution)/shard_map/all_to_all | solution.py:224
  275.8 2.0 shard_map.88
  (9 shorter events, 0.1 us)
Async XLA Ops:
  1.9 11.4 %collective-permute-start.2 = (bf16[20,32,128]{2,1,0:T(8,128)(2,1)S(1)}, bf16[20,32,128]{2,1,0:T(8,128)(2,1)S(1)}, u32[]{:S(2)}, u32[]{:S(2)}) collective-permute-start(bf16[20,32,128]{2,1,0:T(8,128)(2,1)S(1)} %get-tuple-element.5.refs_0_.table_ref), channel_id=1, source_target_pairs={{0,128},{64,192},{128,256},{192,320},{256,384},{320,448},{384,0},{... | collective-permute-start | bytes 491528 | tf_op jit(solution)/shard_map/ppermute | solution.py:228
  5.3 10.1 %collective-permute-start.1 = (bf16[20,32,128]{2,1,0:T(8,128)(2,1)S(1)}, bf16[20,32,128]{2,1,0:T(8,128)(2,1)S(1)}, u32[]{:S(2)}, u32[]{:S(2)}) collective-permute-start(bf16[20,32,128]{2,1,0:T(8,128)(2,1)S(1)} %get-tuple-element.5.refs_0_.table_ref), channel_id=1, source_target_pairs={{0,256},{64,320},{128,384},{192,448},{256,0},{320,64},{384,128},{4... | collective-permute-start | bytes 491528 | tf_op jit(solution)/shard_map/ppermute | solution.py:228
  9.9 7.3 %collective-permute-start = (bf16[20,32,128]{2,1,0:T(8,128)(2,1)S(1)}, bf16[20,32,128]{2,1,0:T(8,128)(2,1)S(1)}, u32[]{:S(2)}, u32[]{:S(2)}) collective-permute-start(bf16[20,32,128]{2,1,0:T(8,128)(2,1)S(1)} %get-tuple-element.5.refs_0_.table_ref), channel_id=1, source_target_pairs={{0,384},{64,448},{128,0},{192,64},{256,128},{320,192},{384,256},{4... | collective-permute-start | bytes 491528 | tf_op jit(solution)/shard_map/ppermute | solution.py:228
  17.3 35.9 %collective-permute-start.3 = (bf16[4,20,32,128]{3,2,1,0:T(8,128)(2,1)S(1)}, bf16[4,20,32,128]{3,2,1,0:T(8,128)(2,1)S(1)}, u32[]{:S(2)}, u32[]{:S(2)}) collective-permute-start(bf16[4,20,32,128]{3,2,1,0:T(8,128)(2,1)S(1)} %shard_map.79.near_ref), channel_id=1, source_target_pairs={{0,64},{64,0},{128,192},{192,128},{256,320},{320,256},{384,448},{4... | collective-permute-start | bytes 1966088 | tf_op jit(solution)/shard_map/ppermute | solution.py:232
  53.1 60.5 %copy-start.3 = (bf16[64,128]{1,0:T(8,128)(2,1)S(1)}, bf16[64,128]{1,0:T(8,128)(2,1)}, u32[]{:S(2)}) copy-start(bf16[64,128]{1,0:T(8,128)(2,1)} %value_ref.1) | copy-start | bytes 49156
  54.0 59.7 %copy-start = (bf16[64,128,64]{1,2,0:T(8,128)(2,1)S(1)}, bf16[64,128,64]{1,2,0:T(8,128)(2,1)}, u32[]{:S(2)}) copy-start(bf16[64,128,64]{1,2,0:T(8,128)(2,1)} %param.6) | copy-start | bytes 3145732
  54.0 59.6 %copy-start.2 = (bf16[64,128,64]{1,2,0:T(8,128)(2,1)S(1)}, bf16[64,128,64]{1,2,0:T(8,128)(2,1)}, u32[]{:S(2)}) copy-start(bf16[64,128,64]{1,2,0:T(8,128)(2,1)} %param.7) | copy-start | bytes 3145732
  54.0 59.6 %copy-start.4 = (s32[64]{0:T(128)S(1)}, s32[64]{0:T(128)}, u32[]{:S(2)}) copy-start(s32[64]{0:T(128)} %fill_ref.1) | copy-start | bytes 772
  176.9 4.0 %collective-permute-start.4 = (bf16[4,20,32,128]{3,2,1,0:T(8,128)(2,1)S(1)}, bf16[4,20,32,128]{3,2,1,0:T(8,128)(2,1)S(1)}, u32[]{:S(2)}, u32[]{:S(2)}) collective-permute-start(bf16[4,20,32,128]{3,2,1,0:T(8,128)(2,1)S(1)} %shard_map.83), channel_id=1, source_target_pairs={{0,64},{64,0},{128,192},{192,128},{256,320},{320,256},{384,448},{4... | collective-permute-start | bytes 1966088 | tf_op jit(solution)/shard_map/ppermute | solution.py:232
  208.6 4.0 %collective-permute-start.5 = (bf16[4,20,32,128]{3,2,1,0:T(8,128)(2,1)S(1)}, bf16[4,20,32,128]{3,2,1,0:T(8,128)(2,1)S(1)}, u32[]{:S(2)}, u32[]{:S(2)}) collective-permute-start(bf16[4,20,32,128]{3,2,1,0:T(8,128)(2,1)S(1)} %all_to_all.34.near_ref), channel_id=1, source_target_pairs={{0,64},{64,0},{128,192},{192,128},{256,320},{320,256},{384,448},{4... | collective-permute-start | bytes 1966088 | tf_op jit(solution)/shard_map/ppermute | solution.py:232
  213.4 1.0 copy-start.1
  214.3 61.4 %all-to-all-start.5 = ((bf16[128,32,128]{2,1,0:T(8,128)(2,1)}), bf16[128,32,128]{2,1,0:T(8,128)(2,1)S(1)}, u32[]{:S(2)}, u32[]{:S(2)}) async-start(bf16[128,32,128]{2,1,0:T(8,128)(2,1)} %copy-done.1), calls=%async_computation.5 | async-start | bytes 2097152 | tf_op jit(solution)/shard_map/all_to_all | solution.py:224
